TPU v7x, 128 devices: a whole 4x4x4 slice. The times are simulated.
128 devices in a mesh: shot: 2 (over z_lo), space: 64 (over z_hi, y, x, core).
Axes of the slice: x: 4, y: 4, z: 4 (z_hi: 2, z_lo: 2; z = z_hi * 2 + z_lo), core: 2. Of those that a mesh axis runs over, the one named last changes fastest.
Arguments:
- lame_lambda: float32 [512, 64, 128], P('space'), may hold values from 0.5 to 2
- lame_shear: float32 [512, 64, 128], P('space'), may hold values from 0.2 to 1
- buoyancy: float32 [512, 64, 128], P('space'), may hold values from 0.5 to 1.5
- fwd_state: float32 [9, 4, 512, 64, 128], P(None, 'shot', 'space'), may hold values from -3 to 3
- adj_state: float32 [9, 4, 512, 64, 128], P(None, 'shot', 'space'), may hold values from -3 to 3
- src_index: int32 [4], P('shot'), may hold values from 0 to 4194303
- src_amp: float32 [4, 3], P('shot'), may hold values from -12 to 12
- recv_index: int32 [4, 1024], P('shot'), may hold values from 0 to 4194303
- residual: float32 [4, 3, 1024], P('shot'), may hold values from -12 to 12
Outputs:
- grad_lambda: float32 [512, 64, 128], P('space', 'shot')
- grad_shear: float32 [512, 64, 128], P('space', 'shot')
Inputs may be any that keep to these rules, and one draw needn't show every extreme that they name: `src_index`: a cell number (x 64 + y) * 128 + z. `recv_index`: cell numbers (x 64 + y) * 128 + z, repeats possible.
All inputs are finite; a program needn't handle non-finite values.
Results may differ from a plain program's by a relative error of at most 0.00002.
Values sent between devices are 32-bit elements; how exact they have to be, the bound alone decides.
No kernel may reach another device: no remote copies, remote signals or barrier semaphores. Data moves between devices by JAX's collectives and lax.ppermute only.
A program may use at most 320 MiB of HBM per device.

v0:
```python
import jax
import jax.numpy as jnp
from jax import lax
from jax.sharding import PartitionSpec as P

courant = 0.2


def extended(cells, sides, width):
    for axis, dim in sides:
        count = lax.axis_size(axis)
        ends = count - 1
        head = lax.slice_in_dim(cells, 0, width, axis=dim)
        tail = lax.slice_in_dim(cells, cells.shape[dim] - width, cells.shape[dim], axis=dim)
        cells = jnp.concatenate(
            [
                lax.ppermute(tail, axis, [(i, (i + 1) % count) for i in range(ends)]),
                cells,
                lax.ppermute(head, axis, [((i + 1) % count, i) for i in range(ends)]),
            ],
            axis=dim,
        )
    return cells


def ahead_diff(source, along):
    length = source.shape[along]
    shifted = jnp.concatenate(
        [
            lax.slice_in_dim(source, 1, length, axis=along),
            jnp.zeros_like(lax.slice_in_dim(source, 0, 1, axis=along)),
        ],
        axis=along,
    )
    return shifted - source


def behind_diff(source, along):
    length = source.shape[along]
    shifted = jnp.concatenate(
        [
            jnp.zeros_like(lax.slice_in_dim(source, 0, 1, axis=along)),
            lax.slice_in_dim(source, 0, length - 1, axis=along),
        ],
        axis=along,
    )
    return source - shifted


def deposit(source, places, amounts):
    flat_field = source.reshape(-1).at[places].add(amounts)
    return flat_field.reshape(source.shape)


def local_push(cell_ids, amounts, anchor, row_count, plane_size):
    members = jnp.arange(cell_ids.shape[0], dtype=jnp.int32)[:, None]
    slab_row = cell_ids // plane_size - anchor
    inside = (slab_row >= 0) & (slab_row < row_count)
    flat_index = (members * row_count + slab_row) * plane_size + cell_ids % plane_size
    places = jnp.where(inside, flat_index, 0).reshape(-1)
    values = jnp.where(inside, amounts, 0.0).reshape(-1)
    return (places, values)


def stress_terms(stress):
    padded = extended(stress, (("space", 2),), 1)
    ahead_x = padded[:, :, 2:] - padded[:, :, 1:-1]
    behind_x = padded[:, :, 1:-1] - padded[:, :, :-2]
    return (ahead_x[0], behind_x[4], behind_x[5])


def velocity_terms(velocity):
    padded = extended(velocity, (("space", 2),), 1)
    vel_ahead = padded[:, :, 2:] - padded[:, :, 1:-1]
    vel_behind = padded[:, :, 1:-1] - padded[:, :, :-2]
    return (vel_behind[0], vel_ahead[1], vel_ahead[2])


def advance(fields, material, factor, vel_push, str_push):
    lame_lambda, lame_shear, buoyancy = (material[0], material[1], material[2])
    velocity_x, velocity_y, velocity_z = (fields[0], fields[1], fields[2])
    stress_xx, stress_yy, stress_zz = (fields[3], fields[4], fields[5])
    stress_yz, stress_xz, stress_xy = (fields[6], fields[7], fields[8])
    ahead_xx, behind_xz, behind_xy = stress_terms(fields[3:])
    scaled = factor * buoyancy
    velocity_x = velocity_x + scaled * (
        ahead_xx + behind_diff(stress_xy, 2) + behind_diff(stress_xz, 3)
    )
    velocity_y = velocity_y + scaled * (
        behind_xy + ahead_diff(stress_yy, 2) + behind_diff(stress_yz, 3)
    )
    velocity_z = velocity_z + scaled * (
        behind_xz + behind_diff(stress_yz, 2) + ahead_diff(stress_zz, 3)
    )
    if vel_push is not None:
        velocity_z = deposit(velocity_z, vel_push[0], vel_push[1])
    behind_vx, ahead_vy, ahead_vz = velocity_terms(jnp.stack([velocity_x, velocity_y, velocity_z]))
    strain_yy = behind_diff(velocity_y, 2)
    strain_zz = behind_diff(velocity_z, 3)
    strain_yz = ahead_diff(velocity_y, 3) + ahead_diff(velocity_z, 2)
    strain_xz = ahead_diff(velocity_x, 3) + ahead_vz
    strain_xy = ahead_diff(velocity_x, 2) + ahead_vy
    trace_sum = behind_vx + strain_yy + strain_zz
    bulk_term = lame_lambda * trace_sum
    stress_xx = stress_xx + factor * (bulk_term + 2.0 * lame_shear * behind_vx)
    stress_yy = stress_yy + factor * (bulk_term + 2.0 * lame_shear * strain_yy)
    stress_zz = stress_zz + factor * (bulk_term + 2.0 * lame_shear * strain_zz)
    stress_yz = stress_yz + factor * (lame_shear * strain_yz)
    stress_xz = stress_xz + factor * (lame_shear * strain_xz)
    stress_xy = stress_xy + factor * (lame_shear * strain_xy)
    if str_push is not None:
        stress_xx = deposit(stress_xx, str_push[0], str_push[1])
        stress_yy = deposit(stress_yy, str_push[0], str_push[1])
        stress_zz = deposit(stress_zz, str_push[0], str_push[1])
    fields = jnp.stack(
        [
            velocity_x,
            velocity_y,
            velocity_z,
            stress_xx,
            stress_yy,
            stress_zz,
            stress_yz,
            stress_xz,
            stress_xy,
        ]
    )
    strains = jnp.stack([behind_vx, strain_yy, strain_zz, strain_yz, strain_xz, strain_xy])
    return (fields, strains)


def shards(
    lame_lambda,
    lame_shear,
    buoyancy,
    fwd_state,
    adj_state,
    src_index,
    src_amp,
    recv_index,
    residual,
):
    shots_dev = fwd_state.shape[1]
    slab_rows = fwd_state.shape[2]
    plane_size = fwd_state.shape[3] * fwd_state.shape[4]
    steps_count = src_amp.shape[1]
    material = jnp.stack([lame_lambda, lame_shear, buoyancy])
    rim_width = 0
    row_count = slab_rows + 2 * rim_width
    anchor = lax.axis_index("space") * slab_rows - rim_width
    ahead_factor = jnp.full((shots_dev, 1, 1, 1), courant, jnp.float32)
    back_factor = -ahead_factor
    fwd_strains = [None] * steps_count
    adj_strains = [None] * steps_count
    fields = fwd_state
    for moment in range(steps_count):
        fields, strain = advance(
            fields,
            material,
            ahead_factor,
            None,
            local_push(
                src_index[:, None], src_amp[:, moment][:, None], anchor, row_count, plane_size
            ),
        )
        fwd_strains[moment] = strain
    fields = adj_state
    for moment in range(steps_count - 1, -1, -1):
        fields, strain = advance(
            fields,
            material,
            back_factor,
            local_push(recv_index, residual[:, moment, :], anchor, row_count, plane_size),
            None,
        )
        adj_strains[moment] = strain
    grad_lambda = jnp.zeros((slab_rows,) + fwd_state.shape[3:], jnp.float32)
    grad_shear = jnp.zeros((slab_rows,) + fwd_state.shape[3:], jnp.float32)
    for moment in range(steps_count - 1, -1, -1):
        forward = fwd_strains[moment]
        adjoint = adj_strains[moment]
        trace_fwd = forward[0] + forward[1] + forward[2]
        trace_adj = adjoint[0] + adjoint[1] + adjoint[2]
        grad_lambda = grad_lambda + jnp.sum(trace_fwd * trace_adj, axis=0)
        shear_term = (
            2.0 * (forward[0] * adjoint[0] + forward[1] * adjoint[1] + forward[2] * adjoint[2])
            + forward[3] * adjoint[3]
            + forward[4] * adjoint[4]
            + forward[5] * adjoint[5]
        )
        grad_shear = grad_shear + jnp.sum(shear_term, axis=0)
    owned = lax.psum_scatter(
        jnp.stack([grad_lambda, grad_shear]), "shot", scatter_dimension=2, tiled=True
    )
    return (owned[0], owned[1])


def solution(mesh):
    in_specs = (
        P("space", None, None),
        P("space", None, None),
        P("space", None, None),
        P(None, "shot", "space", None, None),
        P(None, "shot", "space", None, None),
        P("shot"),
        P("shot", None),
        P("shot", None),
        P("shot", None, None),
    )
    out_specs = (P("space", "shot", None), P("space", "shot", None))
    return jax.shard_map(shards, mesh=mesh, in_specs=in_specs, out_specs=out_specs, check_vma=False)
```

profile of v0, /device:TPU:64, one launch (start us, length us, event | category | flops | bytes accessed | tf_op | source)
XLA Modules:
  0.0 338.2 jit_solution(9125402988414577089)
XLA Ops:
  7.2 2.1 fusion.139
  11.2 9.6 %collective-permute-start.11 = (f32[6,2,1,64,128]{4,3,2,1,0:T(8,128)}, f32[6,2,1,64,128]{4,3,2,1,0:T(8,128)}, u32[]{:S(2)}, u32[]{:S(2)}) collective-permute-start(f32[6,2,1,64,128]{4,3,2,1,0:T(8,128)} %get-tuple-element.76), channel_id=1, source_target_pairs={{1,0},{2,1},{3,2},{4,3},{5,4},{6,5},{7,6},{8,7},{9,8},{10,9},{11,1... | collective-permute-start | bytes 1179656 | tf_op jit(solution)/shard_map/ppermute | solution.py:19
  20.9 2.1 fusion.138
  24.9 9.4 %collective-permute-start = (f32[6,2,1,64,128]{4,3,2,1,0:T(8,128)}, f32[6,2,1,64,128]{4,3,2,1,0:T(8,128)}, u32[]{:S(2)}, u32[]{:S(2)}) collective-permute-start(f32[6,2,1,64,128]{4,3,2,1,0:T(8,128)} %get-tuple-element.69), channel_id=1, source_target_pairs={{1,0},{2,1},{3,2},{4,3},{5,4},{6,5},{7,6},{8,7},{9,8},{10,9},{11,1... | collective-permute-start | bytes 1179656 | tf_op jit(solution)/shard_map/ppermute | solution.py:19
  34.3 2.8 slice_bitcast_fusion.28
  39.7 2.1 slice.660
  41.9 2.3 slice.578
  57.9 14.7 %scatter_fusion.6 = f32[131072]{0:T(1024)S(1)} fusion(f32[131072]{0:T(1024)S(1)} %bitcast.565, s32[2048]{0:T(1024)S(1)} %bitcast.716, f32[2048]{0:T(1024)S(1)} %get-tuple-element.123), kind=kCustom, calls=%fused_computation.6 | custom fusion | flops 2048 | bytes 32768 | tf_op jit(solution)/shard_map/scatter-add | solution.py:51
  73.4 2.1 collective-permute-start.13
  77.2 2.4 fusion.112
  84.2 9.4 %collective-permute-start.3 = (f32[3,2,1,64,128]{4,3,2,1,0:T(8,128)}, f32[3,2,1,64,128]{4,3,2,1,0:T(8,128)}, u32[]{:S(2)}, u32[]{:S(2)}) collective-permute-start(f32[3,2,1,64,128]{4,3,2,1,0:T(8,128)} %get-tuple-element.102), channel_id=1, source_target_pairs={{1,0},{2,1},{3,2},{4,3},{5,4},{6,5},{7,6},{8,7},{9,8},{10,9},{11,1... | collective-permute-start | bytes 589832 | tf_op jit(solution)/shard_map/ppermute | solution.py:19
  94.4 2.4 collective-permute-start.14
  96.9 2.3 bitcast_dynamic-update-slice_fusion.11
  99.2 2.3 bitcast_dynamic-update-slice_fusion.10
  101.5 2.1 bitcast_dynamic-update-slice_fusion.9
  103.6 2.7 multiply_add_fusion.19
  106.3 3.0 multiply_add_fusion.20
  109.3 2.5 scatter_fusion
  113.7 2.4 scatter_fusion.1
  116.1 2.4 scatter_fusion.2
  122.3 3.0 bitcast_dynamic-update-slice_fusion.17
  126.6 3.0 bitcast_dynamic-update-slice_fusion.16
  129.6 2.6 bitcast_dynamic-update-slice_fusion.15
  136.9 2.1 collective-permute-start.16
  138.9 9.4 %collective-permute-start.15 = (f32[6,2,1,64,128]{4,3,2,1,0:T(8,128)S(1)}, f32[6,2,1,64,128]{4,3,2,1,0:T(8,128)S(1)}, u32[]{:S(2)}, u32[]{:S(2)}) collective-permute-start(f32[6,2,1,64,128]{4,3,2,1,0:T(8,128)S(1)} %get-tuple-element.90), channel_id=1, source_target_pairs={{1,0},{2,1},{3,2},{4,3},{5,4},{6,5},{7,6},{8,7},{9,8},{10,9},{11,1... | collective-permute-start | bytes 1179656 | tf_op jit(solution)/shard_map/ppermute | solution.py:19
  148.6 2.1 fusion.143
  152.6 2.4 collective-permute-start.5
  159.7 14.7 %scatter_fusion.7 = f32[131072]{0:T(1024)S(1)} fusion(f32[131072]{0:T(1024)S(1)} %bitcast.578, s32[2048]{0:T(1024)S(1)} %bitcast.717, f32[2048]{0:T(1024)S(1)} %get-tuple-element.122), kind=kCustom, calls=%fused_computation.7 | custom fusion | flops 2048 | bytes 32768 | tf_op jit(solution)/shard_map/scatter-add | solution.py:51
  175.3 2.2 collective-permute-start.17
  191.3 9.4 %collective-permute-start.18 = (f32[3,2,1,64,128]{4,3,2,1,0:T(8,128)}, f32[3,2,1,64,128]{4,3,2,1,0:T(8,128)}, u32[]{:S(2)}, u32[]{:S(2)}) collective-permute-start(f32[3,2,1,64,128]{4,3,2,1,0:T(8,128)} %get-tuple-element.98), channel_id=1, source_target_pairs={{1,0},{2,1},{3,2},{4,3},{5,4},{6,5},{7,6},{8,7},{9,8},{10,9},{11,1... | collective-permute-start | bytes 589832 | tf_op jit(solution)/shard_map/ppermute | solution.py:19
  200.7 2.4 collective-permute-start.7
  205.4 2.6 bitcast_dynamic-update-slice_fusion.5
  212.4 2.4 scatter_fusion.3
  216.7 2.4 scatter_fusion.4
  219.1 2.5 scatter_fusion.5
  221.6 2.0 constant_dynamic-update-slice_fusion.4
  228.9 2.2 add_reduce_fusion
  233.5 3.3 collective-permute-start.8
  236.9 1.9 collective-permute-start.9
  241.6 2.0 fusion.141
  243.6 9.4 %collective-permute-start.19 = (f32[6,2,1,64,128]{4,3,2,1,0:T(8,128)}, f32[6,2,1,64,128]{4,3,2,1,0:T(8,128)}, u32[]{:S(2)}, u32[]{:S(2)}) collective-permute-start(f32[6,2,1,64,128]{4,3,2,1,0:T(8,128)} %get-tuple-element.88), channel_id=1, source_target_pairs={{1,0},{2,1},{3,2},{4,3},{5,4},{6,5},{7,6},{8,7},{9,8},{10,9},{11,1... | collective-permute-start | bytes 1179656 | tf_op jit(solution)/shard_map/ppermute | solution.py:19
  252.9 1.9 collective-permute-start.20
  260.8 9.5 %collective-permute-start.22 = (f32[3,2,1,64,128]{4,3,2,1,0:T(8,128)}, f32[3,2,1,64,128]{4,3,2,1,0:T(8,128)}, u32[]{:S(2)}, u32[]{:S(2)}) collective-permute-start(f32[3,2,1,64,128]{4,3,2,1,0:T(8,128)} %get-tuple-element.95), channel_id=1, source_target_pairs={{1,0},{2,1},{3,2},{4,3},{5,4},{6,5},{7,6},{8,7},{9,8},{10,9},{11,1... | collective-permute-start | bytes 589832 | tf_op jit(solution)/shard_map/ppermute | solution.py:19
  270.3 3.4 %fusion = f32[6,2,8,64,128]{4,3,2,1,0:T(8,128)S(1)} fusion(f32[6,2,8,64,128]{4,3,2,1,0:T(8,128)} %get-tuple-element.34, f32[6,2,1,64,128]{4,3,2,1,0:T(8,128)S(1)} %collective-permute-done.20), kind=kLoop, calls=%fused_computation.10 | loop fusion | flops 1572864 | bytes 6684672 | tf_op jit(solution)/shard_map/sub | solution.py:68
  275.2 14.7 %scatter_fusion.8 = f32[131072]{0:T(1024)S(1)} fusion(f32[131072]{0:T(1024)S(1)} %bitcast.590, s32[2048]{0:T(1024)S(1)} %bitcast.718, f32[2048]{0:T(1024)S(1)} %bitcast.719), kind=kCustom, calls=%fused_computation.8 | custom fusion | flops 2048 | bytes 32768 | tf_op jit(solution)/shard_map/scatter-add | solution.py:51
  293.9 1.9 collective-permute-start.21
  295.8 9.6 %collective-permute-start.23 = (f32[3,2,1,64,128]{4,3,2,1,0:T(8,128)S(1)}, f32[3,2,1,64,128]{4,3,2,1,0:T(8,128)S(1)}, u32[]{:S(2)}, u32[]{:S(2)}) collective-permute-start(f32[3,2,1,64,128]{4,3,2,1,0:T(8,128)S(1)} %get-tuple-element.97), channel_id=1, source_target_pairs={{1,0},{2,1},{3,2},{4,3},{5,4},{6,5},{7,6},{8,7},{9,8},{10,9},{11,1... | collective-permute-start | bytes 589832 | tf_op jit(solution)/shard_map/ppermute | solution.py:19
  315.4 14.2 %reduce-scatter.2.cloned.1.call-done = f32[2,8,32,128]{3,2,1,0:T(8,128)} async-done(((f32[2,8,64,128]{3,2,1,0:T(8,128)}), f32[2,8,32,128]{3,2,1,0:T(8,128)}) %reduce-scatter.2.cloned.1.call-update) | async-done | bytes 262160 | tf_op jit(solution)/shard_map/reduce_scatter | solution.py:192
  (394 shorter events, 102.3 us)
Async XLA Ops:
  7.2 322.5 %reduce-scatter.2.cloned.1.call-start = ((), (), s32[]{:S(2)}) async-start(), calls=%async_computation.1 | async-start | bytes 786432 | tf_op jit(solution)/shard_map/reduce_scatter | solution.py:192
  9.3 38.0 %collective-permute-start.12 = (f32[6,2,1,64,128]{4,3,2,1,0:T(8,128)}, f32[6,2,1,64,128]{4,3,2,1,0:T(8,128)}, u32[]{:S(2)}, u32[]{:S(2)}) collective-permute-start(f32[6,2,1,64,128]{4,3,2,1,0:T(8,128)} %get-tuple-element.77), channel_id=1, source_target_pairs={{0,1},{1,2},{2,3},{3,4},{4,5},{5,6},{6,7},{7,8},{8,9},{9,10},{10,1... | collective-permute-start | bytes 1179656 | tf_op jit(solution)/shard_map/ppermute | solution.py:17
  11.2 25.8 %copy-start.21 = (f32[9,2,8,64,128]{4,3,2,1,0:T(8,128)S(1)}, f32[9,2,8,64,128]{4,3,2,1,0:T(8,128)}, u32[]{:S(2)}) copy-start(f32[9,2,8,64,128]{4,3,2,1,0:T(8,128)} %param.12) | copy-start | bytes 14155780
  11.2 37.7 %collective-permute-start.11 = (f32[6,2,1,64,128]{4,3,2,1,0:T(8,128)}, f32[6,2,1,64,128]{4,3,2,1,0:T(8,128)}, u32[]{:S(2)}, u32[]{:S(2)}) collective-permute-start(f32[6,2,1,64,128]{4,3,2,1,0:T(8,128)} %get-tuple-element.76), channel_id=1, source_target_pairs={{1,0},{2,1},{3,2},{4,3},{5,4},{6,5},{7,6},{8,7},{9,8},{10,9},{11,1... | collective-permute-start | bytes 1179656 | tf_op jit(solution)/shard_map/ppermute | solution.py:19
  23.0 52.5 %collective-permute-start.1 = (f32[6,2,1,64,128]{4,3,2,1,0:T(8,128)}, f32[6,2,1,64,128]{4,3,2,1,0:T(8,128)}, u32[]{:S(2)}, u32[]{:S(2)}) collective-permute-start(f32[6,2,1,64,128]{4,3,2,1,0:T(8,128)} %get-tuple-element.70), channel_id=1, source_target_pairs={{0,1},{1,2},{2,3},{3,4},{4,5},{5,6},{6,7},{7,8},{8,9},{9,10},{10,1... | collective-permute-start | bytes 1179656 | tf_op jit(solution)/shard_map/ppermute | solution.py:17
  24.9 26.1 %collective-permute-start = (f32[6,2,1,64,128]{4,3,2,1,0:T(8,128)}, f32[6,2,1,64,128]{4,3,2,1,0:T(8,128)}, u32[]{:S(2)}, u32[]{:S(2)}) collective-permute-start(f32[6,2,1,64,128]{4,3,2,1,0:T(8,128)} %get-tuple-element.69), channel_id=1, source_target_pairs={{1,0},{2,1},{3,2},{4,3},{5,4},{6,5},{7,6},{8,7},{9,8},{10,9},{11,1... | collective-permute-start | bytes 1179656 | tf_op jit(solution)/shard_map/ppermute | solution.py:19
  38.5 12.5 %copy-start.51 = (f32[8,64,128]{2,1,0:T(8,128)}, f32[8,64,128]{2,1,0:T(8,128)S(1)}, u32[]{:S(2)}) copy-start(f32[8,64,128]{2,1,0:T(8,128)S(1)} %get-tuple-element.116) | copy-start | bytes 786436
  50.2 108.4 %copy-start.5 = (f32[2,8,64,128]{3,2,1,0:T(8,128)}, f32[2,8,64,128]{3,2,1,0:T(8,128)S(1)}, u32[]{:S(2)}) copy-start(f32[2,8,64,128]{3,2,1,0:T(8,128)S(1)} %fusion.71) | copy-start | bytes 1572868
  53.1 76.4 %copy-start.7 = (f32[2,8,64,128]{3,2,1,0:T(8,128)}, f32[2,8,64,128]{3,2,1,0:T(8,128)S(1)}, u32[]{:S(2)}) copy-start(f32[2,8,64,128]{3,2,1,0:T(8,128)S(1)} %fusion.117) | copy-start | bytes 1572868
  73.4 23.4 %collective-permute-start.13 = (f32[3,2,1,64,128]{4,3,2,1,0:T(8,128)S(1)}, f32[3,2,1,64,128]{4,3,2,1,0:T(8,128)S(1)}, u32[]{:S(2)}, u32[]{:S(2)}) collective-permute-start(f32[3,2,1,64,128]{4,3,2,1,0:T(8,128)S(1)} %get-tuple-element.105), channel_id=1, source_target_pairs={{0,1},{1,2},{2,3},{3,4},{4,5},{5,6},{6,7},{7,8},{8,9},{9,10},{10,1... | collective-permute-start | bytes 589832 | tf_op jit(solution)/shard_map/ppermute | solution.py:17
  79.6 45.6 %copy-start.2 = (f32[2,8,64,128]{3,2,1,0:T(8,128)}, f32[2,8,64,128]{3,2,1,0:T(8,128)S(1)}, u32[]{:S(2)}) copy-start(f32[2,8,64,128]{3,2,1,0:T(8,128)S(1)} %get-tuple-element.59) | copy-start | bytes 1572868
  80.6 16.2 %copy-start.25 = (f32[8,64,128]{2,1,0:T(8,128)S(1)}, f32[8,64,128]{2,1,0:T(8,128)}, u32[]{:S(2)}) copy-start(f32[8,64,128]{2,1,0:T(8,128)} %broadcast_multiply_fusion.1) | copy-start | bytes 786436
  80.6 16.2 %copy-start.29 = (f32[8,64,128]{2,1,0:T(8,128)S(1)}, f32[8,64,128]{2,1,0:T(8,128)}, u32[]{:S(2)}) copy-start(f32[8,64,128]{2,1,0:T(8,128)} %param.9) | copy-start | bytes 786436
  82.3 21.3 %collective-permute-start.2 = (f32[3,2,1,64,128]{4,3,2,1,0:T(8,128)S(1)}, f32[3,2,1,64,128]{4,3,2,1,0:T(8,128)S(1)}, u32[]{:S(2)}, u32[]{:S(2)}) collective-permute-start(f32[3,2,1,64,128]{4,3,2,1,0:T(8,128)S(1)} %get-tuple-element.103), channel_id=1, source_target_pairs={{0,1},{1,2},{2,3},{3,4},{4,5},{5,6},{6,7},{7,8},{8,9},{9,10},{10,1... | collective-permute-start | bytes 589832 | tf_op jit(solution)/shard_map/ppermute | solution.py:17
  84.2 41.0 %collective-permute-start.3 = (f32[3,2,1,64,128]{4,3,2,1,0:T(8,128)}, f32[3,2,1,64,128]{4,3,2,1,0:T(8,128)}, u32[]{:S(2)}, u32[]{:S(2)}) collective-permute-start(f32[3,2,1,64,128]{4,3,2,1,0:T(8,128)} %get-tuple-element.102), channel_id=1, source_target_pairs={{1,0},{2,1},{3,2},{4,3},{5,4},{6,5},{7,6},{8,7},{9,8},{10,9},{11,1... | collective-permute-start | bytes 589832 | tf_op jit(solution)/shard_map/ppermute | solution.py:19
  94.4 37.8 %collective-permute-start.14 = (f32[3,2,1,64,128]{4,3,2,1,0:T(8,128)}, f32[3,2,1,64,128]{4,3,2,1,0:T(8,128)}, u32[]{:S(2)}, u32[]{:S(2)}) collective-permute-start(f32[3,2,1,64,128]{4,3,2,1,0:T(8,128)} %get-tuple-element.104), channel_id=1, source_target_pairs={{1,0},{2,1},{3,2},{4,3},{5,4},{6,5},{7,6},{8,7},{9,8},{10,9},{11,1... | collective-permute-start | bytes 589832 | tf_op jit(solution)/shard_map/ppermute | solution.py:19
  132.2 25.4 %copy-start.46 = (f32[2,8,64,128]{3,2,1,0:T(8,128)}, f32[2,8,64,128]{3,2,1,0:T(8,128)S(1)}, u32[]{:S(2)}) copy-start(f32[2,8,64,128]{3,2,1,0:T(8,128)S(1)} %get-tuple-element.114) | copy-start | bytes 1572868
  135.2 23.3 %copy-start.61 = (f32[2,8,64,128]{3,2,1,0:T(8,128)}, f32[2,8,64,128]{3,2,1,0:T(8,128)S(1)}, u32[]{:S(2)}) copy-start(f32[2,8,64,128]{3,2,1,0:T(8,128)S(1)} %get-tuple-element.47) | copy-start | bytes 1572868
  135.2 13.1 %copy-start.67 = (f32[2,8,64,128]{3,2,1,0:T(8,128)S(1)}, f32[2,8,64,128]{3,2,1,0:T(8,128)}, u32[]{:S(2)}) copy-start(f32[2,8,64,128]{3,2,1,0:T(8,128)} %get-tuple-element.52) | copy-start | bytes 1572868
  135.2 13.3 %copy-start.69 = (f32[2,8,64,128]{3,2,1,0:T(8,128)S(1)}, f32[2,8,64,128]{3,2,1,0:T(8,128)}, u32[]{:S(2)}) copy-start(f32[2,8,64,128]{3,2,1,0:T(8,128)} %get-tuple-element.54) | copy-start | bytes 1572868
  136.8 21.8 %copy-start.59 = (f32[2,8,64,128]{3,2,1,0:T(8,128)}, f32[2,8,64,128]{3,2,1,0:T(8,128)S(1)}, u32[]{:S(2)}) copy-start(f32[2,8,64,128]{3,2,1,0:T(8,128)S(1)} %get-tuple-element.45) | copy-start | bytes 1572868
  136.8 18.2 %copy-start.35 = (f32[131072]{0:T(1024)S(1)}, f32[131072]{0:T(1024)}, u32[]{:S(2)}) copy-start(f32[131072]{0:T(1024)} %scatter_fusion.1) | copy-start | bytes 1572868
  136.8 19.1 %copy-start.37 = (f32[131072]{0:T(1024)S(1)}, f32[131072]{0:T(1024)}, u32[]{:S(2)}) copy-start(f32[131072]{0:T(1024)} %scatter_fusion.2) | copy-start | bytes 1572868
  136.9 20.0 %collective-permute-start.16 = (f32[6,2,1,64,128]{4,3,2,1,0:T(8,128)S(1)}, f32[6,2,1,64,128]{4,3,2,1,0:T(8,128)S(1)}, u32[]{:S(2)}, u32[]{:S(2)}) collective-permute-start(f32[6,2,1,64,128]{4,3,2,1,0:T(8,128)S(1)} %get-tuple-element.91), channel_id=1, source_target_pairs={{0,1},{1,2},{2,3},{3,4},{4,5},{5,6},{6,7},{7,8},{8,9},{9,10},{10,1... | collective-permute-start | bytes 1179656 | tf_op jit(solution)/shard_map/ppermute | solution.py:17
  138.9 19.6 %collective-permute-start.15 = (f32[6,2,1,64,128]{4,3,2,1,0:T(8,128)S(1)}, f32[6,2,1,64,128]{4,3,2,1,0:T(8,128)S(1)}, u32[]{:S(2)}, u32[]{:S(2)}) collective-permute-start(f32[6,2,1,64,128]{4,3,2,1,0:T(8,128)S(1)} %get-tuple-element.90), channel_id=1, source_target_pairs={{1,0},{2,1},{3,2},{4,3},{5,4},{6,5},{7,6},{8,7},{9,8},{10,9},{11,1... | collective-permute-start | bytes 1179656 | tf_op jit(solution)/shard_map/ppermute | solution.py:19
  150.6 29.4 %collective-permute-start.4 = (f32[6,2,1,64,128]{4,3,2,1,0:T(8,128)}, f32[6,2,1,64,128]{4,3,2,1,0:T(8,128)}, u32[]{:S(2)}, u32[]{:S(2)}) collective-permute-start(f32[6,2,1,64,128]{4,3,2,1,0:T(8,128)} %get-tuple-element.92), channel_id=1, source_target_pairs={{1,0},{2,1},{3,2},{4,3},{5,4},{6,5},{7,6},{8,7},{9,8},{10,9},{11,1... | collective-permute-start | bytes 1179656 | tf_op jit(solution)/shard_map/ppermute | solution.py:19
  152.6 24.9 %collective-permute-start.5 = (f32[6,2,1,64,128]{4,3,2,1,0:T(8,128)}, f32[6,2,1,64,128]{4,3,2,1,0:T(8,128)}, u32[]{:S(2)}, u32[]{:S(2)}) collective-permute-start(f32[6,2,1,64,128]{4,3,2,1,0:T(8,128)} %get-tuple-element.93), channel_id=1, source_target_pairs={{0,1},{1,2},{2,3},{3,4},{4,5},{5,6},{6,7},{7,8},{8,9},{9,10},{10,1... | collective-permute-start | bytes 1179656 | tf_op jit(solution)/shard_map/ppermute | solution.py:17
  159.7 14.7 %copy-start.10 = (f32[2,8,64,128]{3,2,1,0:T(8,128)S(1)}, f32[2,8,64,128]{3,2,1,0:T(8,128)}, u32[]{:S(2)}) copy-start(f32[2,8,64,128]{3,2,1,0:T(8,128)} %fusion.55) | copy-start | bytes 1572868
  175.3 28.7 %collective-permute-start.17 = (f32[3,2,1,64,128]{4,3,2,1,0:T(8,128)S(1)}, f32[3,2,1,64,128]{4,3,2,1,0:T(8,128)S(1)}, u32[]{:S(2)}, u32[]{:S(2)}) collective-permute-start(f32[3,2,1,64,128]{4,3,2,1,0:T(8,128)S(1)} %get-tuple-element.99), channel_id=1, source_target_pairs={{0,1},{1,2},{2,3},{3,4},{4,5},{5,6},{6,7},{7,8},{8,9},{9,10},{10,1... | collective-permute-start | bytes 589832 | tf_op jit(solution)/shard_map/ppermute | solution.py:17
  180.0 30.6 %copy-start = (f32[2,8,64,128]{3,2,1,0:T(8,128)}, f32[2,8,64,128]{3,2,1,0:T(8,128)S(1)}, u32[]{:S(2)}) copy-start(f32[2,8,64,128]{3,2,1,0:T(8,128)S(1)} %get-tuple-element.85) | copy-start | bytes 1572868
  181.8 22.1 %copy-start.14 = (f32[2,8,64,128]{3,2,1,0:T(8,128)}, f32[2,8,64,128]{3,2,1,0:T(8,128)S(1)}, u32[]{:S(2)}) copy-start(f32[2,8,64,128]{3,2,1,0:T(8,128)S(1)} %fusion.101) | copy-start | bytes 1572868
  182.7 21.2 %collective-permute-start.6 = (f32[3,2,1,64,128]{4,3,2,1,0:T(8,128)S(1)}, f32[3,2,1,64,128]{4,3,2,1,0:T(8,128)S(1)}, u32[]{:S(2)}, u32[]{:S(2)}) collective-permute-start(f32[3,2,1,64,128]{4,3,2,1,0:T(8,128)S(1)} %get-tuple-element.101), channel_id=1, source_target_pairs={{0,1},{1,2},{2,3},{3,4},{4,5},{5,6},{6,7},{7,8},{8,9},{9,10},{10,1... | collective-permute-start | bytes 589832 | tf_op jit(solution)/shard_map/ppermute | solution.py:17
  191.3 34.2 %collective-permute-start.18 = (f32[3,2,1,64,128]{4,3,2,1,0:T(8,128)}, f32[3,2,1,64,128]{4,3,2,1,0:T(8,128)}, u32[]{:S(2)}, u32[]{:S(2)}) collective-permute-start(f32[3,2,1,64,128]{4,3,2,1,0:T(8,128)} %get-tuple-element.98), channel_id=1, source_target_pairs={{1,0},{2,1},{3,2},{4,3},{5,4},{6,5},{7,6},{8,7},{9,8},{10,9},{11,1... | collective-permute-start | bytes 589832 | tf_op jit(solution)/shard_map/ppermute | solution.py:19
  200.7 26.5 %collective-permute-start.7 = (f32[3,2,1,64,128]{4,3,2,1,0:T(8,128)}, f32[3,2,1,64,128]{4,3,2,1,0:T(8,128)}, u32[]{:S(2)}, u32[]{:S(2)}) collective-permute-start(f32[3,2,1,64,128]{4,3,2,1,0:T(8,128)} %get-tuple-element.100), channel_id=1, source_target_pairs={{1,0},{2,1},{3,2},{4,3},{5,4},{6,5},{7,6},{8,7},{9,8},{10,9},{11,1... | collective-permute-start | bytes 589832 | tf_op jit(solution)/shard_map/ppermute | solution.py:19
  233.5 23.3 %collective-permute-start.8 = (f32[6,2,1,64,128]{4,3,2,1,0:T(8,128)S(1)}, f32[6,2,1,64,128]{4,3,2,1,0:T(8,128)S(1)}, u32[]{:S(2)}, u32[]{:S(2)}) collective-permute-start(f32[6,2,1,64,128]{4,3,2,1,0:T(8,128)S(1)} %get-tuple-element.86), channel_id=1, source_target_pairs={{1,0},{2,1},{3,2},{4,3},{5,4},{6,5},{7,6},{8,7},{9,8},{10,9},{11,1... | collective-permute-start | bytes 1179656 | tf_op jit(solution)/shard_map/ppermute | solution.py:19
  236.9 18.3 %collective-permute-start.9 = (f32[6,2,1,64,128]{4,3,2,1,0:T(8,128)S(1)}, f32[6,2,1,64,128]{4,3,2,1,0:T(8,128)S(1)}, u32[]{:S(2)}, u32[]{:S(2)}) collective-permute-start(f32[6,2,1,64,128]{4,3,2,1,0:T(8,128)S(1)} %get-tuple-element.87), channel_id=1, source_target_pairs={{0,1},{1,2},{2,3},{3,4},{4,5},{5,6},{6,7},{7,8},{8,9},{9,10},{10,1... | collective-permute-start | bytes 1179656 | tf_op jit(solution)/shard_map/ppermute | solution.py:17
  240.1 14.8 %copy-start.75 = (f32[2,8,64,128]{3,2,1,0:T(8,128)S(1)}, f32[2,8,64,128]{3,2,1,0:T(8,128)}, u32[]{:S(2)}) copy-start(f32[2,8,64,128]{3,2,1,0:T(8,128)} %get-tuple-element.41) | copy-start | bytes 1572868
  241.3 13.7 %copy-start.74 = (f32[2,8,64,128]{3,2,1,0:T(8,128)S(1)}, f32[2,8,64,128]{3,2,1,0:T(8,128)}, u32[]{:S(2)}) copy-start(f32[2,8,64,128]{3,2,1,0:T(8,128)} %get-tuple-element.43) | copy-start | bytes 1572868
  243.6 46.4 %collective-permute-start.19 = (f32[6,2,1,64,128]{4,3,2,1,0:T(8,128)}, f32[6,2,1,64,128]{4,3,2,1,0:T(8,128)}, u32[]{:S(2)}, u32[]{:S(2)}) collective-permute-start(f32[6,2,1,64,128]{4,3,2,1,0:T(8,128)} %get-tuple-element.88), channel_id=1, source_target_pairs={{1,0},{2,1},{3,2},{4,3},{5,4},{6,5},{7,6},{8,7},{9,8},{10,9},{11,1... | collective-permute-start | bytes 1179656 | tf_op jit(solution)/shard_map/ppermute | solution.py:19
  252.9 17.4 %collective-permute-start.20 = (f32[6,2,1,64,128]{4,3,2,1,0:T(8,128)S(1)}, f32[6,2,1,64,128]{4,3,2,1,0:T(8,128)S(1)}, u32[]{:S(2)}, u32[]{:S(2)}) collective-permute-start(f32[6,2,1,64,128]{4,3,2,1,0:T(8,128)S(1)} %get-tuple-element.89), channel_id=1, source_target_pairs={{0,1},{1,2},{2,3},{3,4},{4,5},{5,6},{6,7},{7,8},{8,9},{9,10},{10,1... | collective-permute-start | bytes 1179656 | tf_op jit(solution)/shard_map/ppermute | solution.py:17
  258.8 47.9 %collective-permute-start.10 = (f32[3,2,1,64,128]{4,3,2,1,0:T(8,128)}, f32[3,2,1,64,128]{4,3,2,1,0:T(8,128)}, u32[]{:S(2)}, u32[]{:S(2)}) collective-permute-start(f32[3,2,1,64,128]{4,3,2,1,0:T(8,128)} %get-tuple-element.94), channel_id=1, source_target_pairs={{0,1},{1,2},{2,3},{3,4},{4,5},{5,6},{6,7},{7,8},{8,9},{9,10},{10,1... | collective-permute-start | bytes 589832 | tf_op jit(solution)/shard_map/ppermute | solution.py:17
  260.8 12.9 %copy-start.50 = (f32[8,64,128]{2,1,0:T(8,128)S(1)}, f32[8,64,128]{2,1,0:T(8,128)}, u32[]{:S(2)}) copy-start(f32[8,64,128]{2,1,0:T(8,128)} %copy-done.48) | copy-start | bytes 786436
  260.8 44.7 %collective-permute-start.22 = (f32[3,2,1,64,128]{4,3,2,1,0:T(8,128)}, f32[3,2,1,64,128]{4,3,2,1,0:T(8,128)}, u32[]{:S(2)}, u32[]{:S(2)}) collective-permute-start(f32[3,2,1,64,128]{4,3,2,1,0:T(8,128)} %get-tuple-element.95), channel_id=1, source_target_pairs={{1,0},{2,1},{3,2},{4,3},{5,4},{6,5},{7,6},{8,7},{9,8},{10,9},{11,1... | collective-permute-start | bytes 589832 | tf_op jit(solution)/shard_map/ppermute | solution.py:19
  275.2 14.7 %copy-start.13 = (f32[2,8,64,128]{3,2,1,0:T(8,128)S(1)}, f32[2,8,64,128]{3,2,1,0:T(8,128)}, u32[]{:S(2)}) copy-start(f32[2,8,64,128]{3,2,1,0:T(8,128)} %fusion.55) | copy-start | bytes 1572868
  275.2 14.7 %copy-start.72 = (f32[2,8,64,128]{3,2,1,0:T(8,128)S(1)}, f32[2,8,64,128]{3,2,1,0:T(8,128)}, u32[]{:S(2)}) copy-start(f32[2,8,64,128]{3,2,1,0:T(8,128)} %get-tuple-element.37) | copy-start | bytes 1572868
  293.6 13.1 %copy-start.43 = (f32[2,8,64,128]{3,2,1,0:T(8,128)S(1)}, f32[2,8,64,128]{3,2,1,0:T(8,128)}, u32[]{:S(2)}) copy-start(f32[2,8,64,128]{3,2,1,0:T(8,128)} %copy-done.41) | copy-start | bytes 1572868
  293.9 16.6 %collective-permute-start.21 = (f32[3,2,1,64,128]{4,3,2,1,0:T(8,128)S(1)}, f32[3,2,1,64,128]{4,3,2,1,0:T(8,128)S(1)}, u32[]{:S(2)}, u32[]{:S(2)}) collective-permute-start(f32[3,2,1,64,128]{4,3,2,1,0:T(8,128)S(1)} %get-tuple-element.96), channel_id=1, source_target_pairs={{0,1},{1,2},{2,3},{3,4},{4,5},{5,6},{6,7},{7,8},{8,9},{9,10},{10,1... | collective-permute-start | bytes 589832 | tf_op jit(solution)/shard_map/ppermute | solution.py:17
  295.8 15.7 %collective-permute-start.23 = (f32[3,2,1,64,128]{4,3,2,1,0:T(8,128)S(1)}, f32[3,2,1,64,128]{4,3,2,1,0:T(8,128)S(1)}, u32[]{:S(2)}, u32[]{:S(2)}) collective-permute-start(f32[3,2,1,64,128]{4,3,2,1,0:T(8,128)S(1)} %get-tuple-element.97), channel_id=1, source_target_pairs={{1,0},{2,1},{3,2},{4,3},{5,4},{6,5},{7,6},{8,7},{9,8},{10,9},{11,1... | collective-permute-start | bytes 589832 | tf_op jit(solution)/shard_map/ppermute | solution.py:19
  (101 other events, 301.7 us)
Sparse Core Ops, SparseCore 0:
  315.6 14.0 reduce-scatter.1
where the time goes:
time: 342 us; the launch traced here: 338 us
  other arithmetic  135 us (39%)
  starting transfers between devices  110 us (32%)
  local copies, waits for them, and re-layouts  62.7 us (18%)
  between operations  16.1 us (5%)
  waiting for transfers between devices  14.3 us (4%)
    ppermute x12, starting transfers between devices, extended(): lax.ppermute(head, axis, [((i + 1) % count, i) for i in range(ends)])  85.6 us
    scatter-add x9, other arithmetic, deposit(): flat_field = source.reshape(-1).at[places].add(amounts)  58.5 us
    ppermute x12, starting transfers between devices, extended(): lax.ppermute(tail, axis, [(i, (i + 1) % count) for i in range(ends)])  24 us
    unnamed x16, other arithmetic  21.2 us
    slice x36, local copies, waits for them, and re-layouts, ahead_diff(): lax.slice_in_dim(source, 1, length, axis=along)  20.7 us
    unnamed x258, local copies, waits for them, and re-layouts  19.7 us
    reduce_scatter x1, waiting for transfers between devices, shards(): lax.psum_scatter(jnp.stack([grad_lambda, grad_shear]), 'shot', scatter_di...  14.2 us
    slice x10, local copies, waits for them, and re-layouts, extended(): head = lax.slice_in_dim(cells, 0, width, axis=dim)  11.2 us
  transfers between devices with their start and end apart: 25, of which 1 were waited for; matrix products, arithmetic and copies ran while one was open for 51% of the time, Pallas kernels for 0%

commit v1 on v0

v1 whole, which is shorter than its diff:
```python
import functools

import jax
import jax.numpy as jnp
from jax import lax
from jax.experimental import pallas as pl
from jax.experimental.pallas import tpu as pltpu
from jax.sharding import PartitionSpec as P

courant = 0.2
VX, VY, VZ, SXX, SYY, SZZ, SYZ, SXZ, SXY = range(9)

SLOTS = 14
OWN = 3
PAD = 8

RIGHTWARD = (
    (VX, 5, 3, 0), (VY, 6, 2, 1), (VZ, 6, 2, 1), (SXX, 6, 2, 1), (SYY, 7, 1, 2), (SZZ, 7, 1, 2),
    (SYZ, 7, 1, 2), (SXZ, 6, 2, 1), (SXY, 6, 2, 1),
)
LEFTWARD = (
    (VX, 0, 2, 11), (VY, 0, 3, 11), (VZ, 0, 3, 11), (SXX, 0, 2, 11), (SYY, 0, 2, 11), (SZZ, 0, 2, 11),
    (SYZ, 0, 2, 11), (SXZ, 0, 2, 11), (SXY, 0, 2, 11),
)
MATS_RIGHTWARD = (6, 1)
MATS_LEFTWARD = (0, 11)
SENT = 20
CHUNK = 32


def lanes(rows):
    return lax.broadcasted_iota(jnp.int32, (rows, 128), 1)


def below_z(x):
    return jnp.where(lanes(x.shape[0]) == 0, 0.0, pltpu.roll(x, 1, 1))


def above_z(x):
    return jnp.where(lanes(x.shape[0]) == 127, 0.0, pltpu.roll(x, 127, 1))


def velocity_plane(w, kb, q, inject=None):
    for start in range(0, 64, CHUNK):
        at = pl.ds(PAD + start, CHUNK)
        down = pl.ds(PAD + start - 1, CHUNK)
        up = pl.ds(PAD + start + 1, CHUNK)
        flat = pl.ds(start, CHUNK)
        xy_b, xz_b = w[SXY, q - 1, at, :], w[SXZ, q - 1, at, :]
        w[VX, q - 1, at, :] += kb(q - 1, flat) * (
            (w[SXX, q, at, :] - w[SXX, q - 1, at, :])
            + (xy_b - w[SXY, q - 1, down, :])
            + (xz_b - below_z(xz_b))
        )
        yz, zz = w[SYZ, q, at, :], w[SZZ, q, at, :]
        scaled = kb(q, flat)
        w[VY, q, at, :] += scaled * (
            (w[SXY, q, at, :] - xy_b) + (w[SYY, q, up, :] - w[SYY, q, at, :]) + (yz - below_z(yz))
        )
        new_z = w[VZ, q, at, :] + scaled * (
            (w[SXZ, q, at, :] - xz_b) + (yz - w[SYZ, q, down, :]) + (above_z(zz) - zz)
        )
        if inject is not None:
            new_z = new_z + inject[q, flat, :]
        w[VZ, q, at, :] = new_z


def strain_chunk(w, q, start):
    at = pl.ds(PAD + start, CHUNK)
    down = pl.ds(PAD + start - 1, CHUNK)
    up = pl.ds(PAD + start + 1, CHUNK)
    vx, vy, vz = w[VX, q, at, :], w[VY, q, at, :], w[VZ, q, at, :]
    exx = vx - w[VX, q - 1, at, :]
    eyy = vy - w[VY, q, down, :]
    ezz = vz - below_z(vz)
    eyz = (above_z(vy) - vy) + (w[VZ, q, up, :] - vz)
    exz = (above_z(vx) - vx) + (w[VZ, q + 1, at, :] - vz)
    exy = (w[VX, q, up, :] - vx) + (w[VY, q + 1, at, :] - vy)
    return exx, eyy, ezz, eyz, exz, exy


def stress_chunk(w, mats, q, start, strain):
    at = pl.ds(PAD + start, CHUNK)
    flat = pl.ds(start, CHUNK)
    exx, eyy, ezz, eyz, exz, exy = strain
    twice = mats[2, q, flat, :]
    bulk = mats[1, q, flat, :] * (exx + eyy + ezz)
    once = 0.5 * twice
    w[SXX, q, at, :] += bulk + twice * exx
    w[SYY, q, at, :] += bulk + twice * eyy
    w[SZZ, q, at, :] += bulk + twice * ezz
    w[SYZ, q, at, :] += once * eyz
    w[SXZ, q, at, :] += once * exz
    w[SXY, q, at, :] += once * exy


def planes(low, high, body):
    def step(q, carry):
        body(q)
        return carry

    lax.fori_loop(low, high, step, 0)


def clear_edges(w, slots):
    zero = jnp.zeros((PAD, 128), jnp.float32)
    for field, top in ((VX, 1), (VY, 0), (VZ, 1), (SXY, 0), (SYY, 1), (SYZ, 0)):
        for slot in range(slots):
            w[field, slot, pl.ds(PAD + 64 if top else 0, PAD), :] = zero


def pack_kernel(with_mats, meta, state, lam, mu, buoy, *rest):
    if with_mats:
        cross, chip, w, b, sems, out_sems, mat_sems = rest
        crosses = (cross, cross)
    else:
        cross_0, cross_1, chip, w, b, sems, out_sems, mat_sems = rest
        crosses = (cross_0, cross_1)
    odd = lax.rem(meta[0], 2) == 1
    loads = []
    for side, first in ((0, 0), (1, 5)):
        loads.append(
            pltpu.make_async_copy(
                buoy.at[pl.ds(first, 3)], b.at[pl.ds(3 * side, 3)], sems.at[4 + side]
            )
        )
        for shot in range(2):
            loads.append(
                pltpu.make_async_copy(
                    state.at[:, shot, pl.ds(first, 3)],
                    w.at[shot, :, pl.ds(3 * side, 3), pl.ds(PAD, 64)],
                    sems.at[2 * shot + side],
                )
            )
    for load in loads:
        load.start()
    mats = []
    if with_mats:
        for rightward in (True, False):
            first = MATS_RIGHTWARD[0] if rightward else MATS_LEFTWARD[0]
            for i, array in enumerate((buoy, lam, mu)):
                mats.append((rightward, array.at[pl.ds(first, 2)], 2 * SENT + 2 * i))

    def send(rightward, to_cross):
        for i, (go_right, source, at) in enumerate(mats):
            if go_right == rightward:
                target = cross if to_cross else chip
                pltpu.make_async_copy(source, target.at[pl.ds(at, 2)], mat_sems.at[i]).start()

    @pl.when(odd)
    def _():
        send(True, True)
        send(False, False)

    @pl.when(jnp.logical_not(odd))
    def _():
        send(True, False)
        send(False, True)

    for shot in range(2):
        clear_edges(w.at[shot], 6)
    for load in loads:
        load.wait()
    factor = courant if with_mats else -courant
    kb = lambda q, flat: factor * b[q, flat, :]
    for shot in range(2):
        velocity = functools.partial(velocity_plane, w.at[shot], kb)
        planes(1, 3, velocity)
        planes(4, 6, velocity)

    def copies(shot, rightward, to_cross):
        base = 0
        result = []
        for i, (field, first, count, _) in enumerate(RIGHTWARD if rightward else LEFTWARD):
            slot = first if first < 3 else first - 2
            if to_cross:
                target = crosses[shot].at[pl.ds((SENT * shot if with_mats else 0) + base, count)]
            else:
                target = chip.at[pl.ds(SENT * shot + base, count)]
            result.append(
                pltpu.make_async_copy(
                    w.at[shot, field, pl.ds(slot, count), pl.ds(PAD, 64)],
                    target,
                    out_sems.at[shot, 0 if rightward else 1, i],
                )
            )
            base += count
        return result

    def run(action):
        @pl.when(odd)
        def _():
            for shot in range(2):
                for copy in copies(shot, True, True) + copies(shot, False, False):
                    action(copy)

        @pl.when(jnp.logical_not(odd))
        def _():
            for shot in range(2):
                for copy in copies(shot, True, False) + copies(shot, False, True):
                    action(copy)

    run(lambda copy: copy.start())
    run(lambda copy: copy.wait())
    for i, (_, source, at) in enumerate(mats):
        pltpu.make_async_copy(source, cross.at[pl.ds(at, 2)], mat_sems.at[i]).wait()


def pack(meta, state, lam, mu, buoy, with_mats):
    anywhere = pl.BlockSpec(memory_space=pl.ANY)
    big = jax.ShapeDtypeStruct((2 * SENT + (6 if with_mats else 0), 64, 128), jnp.float32)
    half = jax.ShapeDtypeStruct((SENT, 64, 128), jnp.float32)
    out = (big, big) if with_mats else (half, half, big)
    return pl.pallas_call(
        functools.partial(pack_kernel, with_mats),
        out_shape=out,
        in_specs=[pl.BlockSpec(memory_space=pltpu.SMEM)] + [anywhere] * 4,
        out_specs=tuple(anywhere for _ in out),
        scratch_shapes=[
            pltpu.VMEM((2, 9, 6, 64 + 2 * PAD, 128), jnp.float32),
            pltpu.VMEM((6, 64, 128), jnp.float32),
            pltpu.SemaphoreType.DMA((6,)),
            pltpu.SemaphoreType.DMA((2, 2, 9)),
            pltpu.SemaphoreType.DMA((6,)),
        ],
        compiler_params=pltpu.CompilerParams(vmem_limit_bytes=12 << 20),
        name="pack_forward" if with_mats else "pack_adjoint",
    )(meta, state, lam, mu, buoy)


def load_mats(meta, lam, mu, buoy, cross, chip, mats, sems, action):
    odd = lax.rem(meta[0], 2) == 1
    for i, array in enumerate((buoy, lam, mu)):
        action(pltpu.make_async_copy(array, mats.at[i, pl.ds(OWN, 8)], sems.at[i, 0]))

    def halo(left, right):
        for i in range(3):
            at = pl.ds(2 * SENT + 2 * i, 2)
            action(pltpu.make_async_copy(left.at[at], mats.at[i, pl.ds(1, 2)], sems.at[i, 1]))
            action(pltpu.make_async_copy(right.at[at], mats.at[i, pl.ds(11, 2)], sems.at[i, 2]))

    @pl.when(odd)
    def _():
        halo(chip, cross)

    @pl.when(jnp.logical_not(odd))
    def _():
        halo(cross, chip)


def load_state(meta, state, shot, cross, cross_base, chip, w, sems, action):
    odd = lax.rem(meta[0], 2) == 1
    action(
        pltpu.make_async_copy(
            state.at[:, shot], w.at[:, pl.ds(OWN, 8), pl.ds(PAD, 64)], sems.at[0, 0]
        )
    )

    def halo(left, left_base, right, right_base):
        for side, ref, base, table in (
            (1, left, left_base, RIGHTWARD),
            (2, right, right_base, LEFTWARD),
        ):
            for i, (field, _, count, slot) in enumerate(table):
                action(
                    pltpu.make_async_copy(
                        ref.at[pl.ds(base, count)],
                        w.at[field, pl.ds(slot, count), pl.ds(PAD, 64)],
                        sems.at[side, i],
                    )
                )
                base += count

    @pl.when(odd)
    def _():
        halo(chip, SENT * shot, cross, cross_base)

    @pl.when(jnp.logical_not(odd))
    def _():
        halo(cross, cross_base, chip, SENT * shot)


def scale_mats(mats, factor):
    def one(q):
        mats[0, q] = factor * mats[0, q]
        mats[1, q] = factor * mats[1, q]
        mats[2, q] = (2.0 * factor) * mats[2, q]

    planes(1, 13, one)


def start(copy):
    copy.start()


def wait(copy):
    copy.wait()


def forward_kernel(
    meta, src_index, src_amp, state, lam, mu, buoy, cross, chip, strains, w, mats, mat_sems, sems
):
    load_mats(meta, lam, mu, buoy, cross, chip, mats, mat_sems, start)
    for shot in range(2):
        load_state(meta, state, shot, cross, SENT * shot, chip, w.at[shot], sems.at[shot], start)
    for shot in range(2):
        clear_edges(w.at[shot], SLOTS)
    load_mats(meta, lam, mu, buoy, cross, chip, mats, mat_sems, wait)
    scale_mats(mats, courant)
    kb = lambda q, flat: mats[0, q, flat, :]
    for shot in range(2):
        u = w.at[shot]
        load_state(meta, state, shot, cross, SENT * shot, chip, u, sems.at[shot], wait)

        def strain_only(moment, q):
            for begin in range(0, 64, CHUNK):
                for i, value in enumerate(strain_chunk(u, q, begin)):
                    strains[shot, moment, i, q - OWN, pl.ds(begin, CHUNK), :] = value

        def own(moment, q):
            for begin in range(0, 64, CHUNK):
                strain = strain_chunk(u, q, begin)
                for i, value in enumerate(strain):
                    strains[shot, moment, i, q - OWN, pl.ds(begin, CHUNK), :] = value
                stress_chunk(u, mats, q, begin, strain)

        def outer(q):
            for begin in range(0, 64, CHUNK):
                stress_chunk(u, mats, q, begin, strain_chunk(u, q, begin))

        cell = src_index[shot]
        slot = lax.shift_right_logical(cell, 13) - 8 * meta[0] + OWN
        row = jnp.bitwise_and(lax.shift_right_logical(cell, 7), 63) + PAD
        lane = jnp.bitwise_and(cell, 127)

        def source(moment, low, high):
            @pl.when(jnp.logical_and(slot >= low, slot < high))
            def _():
                amount = jnp.where(lanes(1) == lane, src_amp[shot, moment], 0.0)
                for field in (SXX, SYY, SZZ):
                    u[field, slot, pl.ds(row, 1), :] += amount

        velocity = functools.partial(velocity_plane, u, kb)
        planes(OWN, OWN + 9, velocity)
        planes(1, 3, outer)
        planes(OWN, OWN + 8, functools.partial(own, 0))
        planes(11, 13, outer)
        source(0, 1, 13)
        planes(OWN - 1, OWN + 10, velocity)
        planes(2, 3, outer)
        planes(OWN, OWN + 8, functools.partial(own, 1))
        planes(11, 12, outer)
        source(1, 2, 12)
        planes(OWN, OWN + 9, velocity)
        planes(OWN, OWN + 8, functools.partial(strain_only, 2))


def forward(meta, src_index, src_amp, state, lam, mu, buoy, cross, chip):
    anywhere = pl.BlockSpec(memory_space=pl.ANY)
    scalars = pl.BlockSpec(memory_space=pltpu.SMEM)
    return pl.pallas_call(
        forward_kernel,
        out_shape=jax.ShapeDtypeStruct((2, 3, 6, 8, 64, 128), jnp.float32),
        in_specs=[scalars] * 3 + [anywhere] * 6,
        out_specs=pl.BlockSpec(memory_space=pltpu.VMEM),
        scratch_shapes=[
            pltpu.VMEM((2, 9, SLOTS, 64 + 2 * PAD, 128), jnp.float32),
            pltpu.VMEM((3, SLOTS, 64, 128), jnp.float32),
            pltpu.SemaphoreType.DMA((3, 3)),
            pltpu.SemaphoreType.DMA((2, 3, 9)),
        ],
        compiler_params=pltpu.CompilerParams(vmem_limit_bytes=24 << 20),
        name="forward_steps",
    )(meta, src_index, src_amp, state, lam, mu, buoy, cross, chip)


def inject_kernel(meta, cells, amounts, out, rows_hot, values):
    base = (8 * meta[0] - OWN) * 64
    for shot in range(2):
        cell = cells[pl.ds(shot, 1), :]
        count = cell.shape[1]
        row = lax.shift_right_logical(cell, 7) - base
        lane = jnp.bitwise_and(cell, 127)

        def hot(k, carry):
            at = k * 128 + lax.broadcasted_iota(jnp.int32, (128, count), 0)
            rows_hot[pl.ds(k * 128, 128), :] = jnp.where(at == row, 1.0, 0.0).astype(jnp.bfloat16)
            return carry

        lax.fori_loop(0, SLOTS * 64 // 128, hot, 0)
        lane_hot = lax.broadcasted_iota(jnp.int32, (128, count), 0) == lane
        for moment in range(3):
            left = amounts[shot, pl.ds(moment, 1), :]
            for part in range(3):
                piece = left.astype(jnp.bfloat16).astype(jnp.float32)
                left = left - piece
                values[part, pl.ds(128 * moment, 128), :] = jnp.where(lane_hot, piece, 0.0).astype(
                    jnp.bfloat16
                )
        dims = (((1,), (1,)), ((), ()))
        size = SLOTS * 64 // 2
        for k in range(2):
            hot_rows = rows_hot[pl.ds(k * size, size), :]
            total = None
            for part in range(3):
                product = lax.dot_general(
                    hot_rows, values[part], dims, preferred_element_type=jnp.float32
                )
                total = product if total is None else total + product
            for moment in range(3):
                out[shot, moment, pl.ds(k * size, size), :] = total[:, 128 * moment : 128 * moment + 128]


def inject(meta, cells, amounts):
    count = cells.shape[1]
    vmem = pl.BlockSpec(memory_space=pltpu.VMEM)
    return pl.pallas_call(
        inject_kernel,
        out_shape=jax.ShapeDtypeStruct((2, 3, SLOTS * 64, 128), jnp.float32),
        in_specs=[pl.BlockSpec(memory_space=pltpu.SMEM), vmem, vmem],
        out_specs=vmem,
        scratch_shapes=[
            pltpu.VMEM((SLOTS * 64, count), jnp.bfloat16),
            pltpu.VMEM((3, 384, count), jnp.bfloat16),
        ],
        compiler_params=pltpu.CompilerParams(vmem_limit_bytes=24 << 20),
        name="receivers",
    )(meta, cells, amounts)


def adjoint_kernel(
    shot, meta, state, lam, mu, buoy, f_cross, f_chip, cross, chip, strains, dense, *rest
):
    if shot == 0:
        grads, w, mats, mat_sems, sems = rest
    else:
        before, keep, give, grads, w, mats, mat_sems, sems = rest
    load_mats(meta, lam, mu, buoy, f_cross, f_chip, mats, mat_sems, start)
    load_state(meta, state, shot, cross, 0, chip, w, sems, start)
    clear_edges(w, SLOTS)
    load_mats(meta, lam, mu, buoy, f_cross, f_chip, mats, mat_sems, wait)
    scale_mats(mats, -courant)
    load_state(meta, state, shot, cross, 0, chip, w, sems, wait)
    kb = lambda q, flat: mats[0, q, flat, :]

    def own(moment, stress, q):
        p = q - OWN
        for begin in range(0, 64, CHUNK):
            flat = pl.ds(begin, CHUNK)
            exx, eyy, ezz, eyz, exz, exy = strain_chunk(w, q, begin)
            fxx, fyy, fzz, fyz, fxz, fxy = [strains[shot, moment, i, p, flat, :] for i in range(6)]
            bulk = (fxx + fyy + fzz) * (exx + eyy + ezz)
            shear = 2.0 * (fxx * exx + fyy * eyy + fzz * ezz) + (
                fyz * eyz + fxz * exz + fxy * exy
            )
            if moment < 2:
                bulk, shear = bulk + grads[0, p, flat, :], shear + grads[1, p, flat, :]
            elif shot == 1:
                bulk, shear = bulk + before[0, p, flat, :], shear + before[1, p, flat, :]
            grads[0, p, flat, :] = bulk
            grads[1, p, flat, :] = shear
            if stress:
                stress_chunk(w, mats, q, begin, (exx, eyy, ezz, eyz, exz, exy))

    def outer(q):
        for begin in range(0, 64, CHUNK):
            stress_chunk(w, mats, q, begin, strain_chunk(w, q, begin))

    def velocity(moment, q):
        velocity_plane(w, kb, q, dense.at[shot, moment])

    for slot in (1, 2, 12, 13):
        w[VZ, slot, pl.ds(PAD, 64), :] += dense[shot, 2, slot]
    planes(OWN, OWN + 9, functools.partial(velocity, 2))
    planes(1, 3, outer)
    planes(OWN, OWN + 8, functools.partial(own, 2, True))
    planes(11, 13, outer)
    planes(OWN - 1, OWN + 10, functools.partial(velocity, 1))
    planes(2, 3, outer)
    planes(OWN, OWN + 8, functools.partial(own, 1, True))
    planes(11, 12, outer)
    planes(OWN, OWN + 9, functools.partial(velocity, 0))
    planes(OWN, OWN + 8, functools.partial(own, 0, False))
    if shot == 1:
        mine = pl.multiple_of(meta[1] * 32, 32)
        keep[...] = grads[:, :, pl.ds(mine, 32), :]
        give[...] = grads[:, :, pl.ds(pl.multiple_of(32 - mine, 32), 32), :]


def adjoint(shot, meta, state, lam, mu, buoy, f_cross, f_chip, cross, chip, strains, dense, before):
    anywhere = pl.BlockSpec(memory_space=pl.ANY)
    vmem = pl.BlockSpec(memory_space=pltpu.VMEM)
    whole = jax.ShapeDtypeStruct((2, 8, 64, 128), jnp.float32)
    half = jax.ShapeDtypeStruct((2, 8, 32, 128), jnp.float32)
    scratch = [
        pltpu.VMEM((9, SLOTS, 64 + 2 * PAD, 128), jnp.float32),
        pltpu.VMEM((3, SLOTS, 64, 128), jnp.float32),
        pltpu.SemaphoreType.DMA((3, 3)),
        pltpu.SemaphoreType.DMA((3, 9)),
    ]
    operands = [meta, state, lam, mu, buoy, f_cross, f_chip, cross, chip, strains, dense]
    in_specs = [pl.BlockSpec(memory_space=pltpu.SMEM)] + [anywhere] * 8 + [vmem] * 2
    if shot == 0:
        out_shape, out_specs = whole, vmem
    else:
        operands.append(before)
        in_specs.append(vmem)
        out_shape, out_specs = (half, half), (vmem, vmem)
        scratch = [pltpu.VMEM(whole.shape, jnp.float32)] + scratch
    return pl.pallas_call(
        functools.partial(adjoint_kernel, shot),
        out_shape=out_shape,
        in_specs=in_specs,
        out_specs=out_specs,
        scratch_shapes=scratch,
        compiler_params=pltpu.CompilerParams(vmem_limit_bytes=28 << 20),
        name="adjoint_steps",
    )(*operands)


def shards(
    lame_lambda, lame_shear, buoyancy, fwd_state, adj_state, src_index, src_amp, recv_index, residual
):
    count = lax.axis_size("space")
    onchip = [(i, i + 1) for i in range(0, count, 2)] + [(i + 1, i) for i in range(0, count, 2)]
    between = [(i, i + 1) for i in range(1, count - 1, 2)]
    between = between + [(j, i) for i, j in between]
    swap_chips = lambda x: lax.ppermute(x, "space", between)
    swap_cores = lambda x: lax.ppermute(x, "space", onchip)
    meta = jnp.stack([lax.axis_index("space"), lax.axis_index("shot")]).astype(jnp.int32)
    mats = (lame_lambda, lame_shear, buoyancy)
    f_cross, f_chip = pack(meta, fwd_state, *mats, True)
    f_cross = swap_chips(f_cross)
    a_cross_0, a_cross_1, a_chip = pack(meta, adj_state, *mats, False)
    a_cross_0 = swap_chips(a_cross_0)
    a_cross_1 = swap_chips(a_cross_1)
    f_chip = swap_cores(f_chip)
    a_chip = swap_cores(a_chip)
    dense = inject(meta, recv_index, residual).reshape(2, 3, SLOTS, 64, 128)
    strains = forward(meta, src_index, src_amp, fwd_state, *mats, f_cross, f_chip)
    grads = adjoint(
        0, meta, adj_state, *mats, f_cross, f_chip, a_cross_0, a_chip, strains, dense, None
    )
    keep, give = adjoint(
        1, meta, adj_state, *mats, f_cross, f_chip, a_cross_1, a_chip, strains, dense, grads
    )
    total = keep + lax.ppermute(give, "shot", [(0, 1), (1, 0)])
    return (total[0], total[1])


def solution(mesh):
    in_specs = (
        P("space", None, None),
        P("space", None, None),
        P("space", None, None),
        P(None, "shot", "space", None, None),
        P(None, "shot", "space", None, None),
        P("shot"),
        P("shot", None),
        P("shot", None),
        P("shot", None, None),
    )
    out_specs = (P("space", "shot", None), P("space", "shot", None))
    return jax.shard_map(shards, mesh=mesh, in_specs=in_specs, out_specs=out_specs, check_vma=False)
```

time: 342 us -> 111 us (0.32)
  other arithmetic: 135 us -> 0.11 us
  starting transfers between devices: 110 us -> 20.2 us
  Pallas kernels: 0 us -> 78.5 us
  local copies, waits for them, and re-layouts: 62.7 us -> 5.98 us
  between operations: 16.1 us -> 0.92 us
  waiting for transfers between devices: 14.3 us -> 4.36 us
    ppermute x24 -> x6, starting transfers between devices: 110 us -> 20.2 us  [the longest x3 16.9 us: shards(): swap_chips = lambda x: lax.ppermute(x, 'space', between)]
    pallas_call x0 -> x6, Pallas kernels: none -> 78.5 us  [the longest x2 30.7 us: adjoint(): pl.pallas_call(functools.partial(adjoint_kernel, shot), out_shape=out_sha...]
    scatter-add x9 -> x0, other arithmetic: 58.5 us -> none  [deposit(): flat_field = source.reshape(-1).at[places].add(amounts)]
    slice x51 -> x0, local copies, waits for them, and re-layouts: 37.2 us -> none  [the longest x36 20.7 us: ahead_diff(): lax.slice_in_dim(source, 1, length, axis=along)]
    add x17 -> x1, other arithmetic: 21.7 us -> 0.04 us  [shards(): total = keep + lax.ppermute(give, 'shot', [(0, 1), (1, 0)])]
    unnamed x16 -> x1, other arithmetic: 21.2 us -> 0.01 us
    sub x12 -> x0, other arithmetic: 16.6 us -> none  [the longest x6 9.43 us: stress_terms(): behind_x = padded[:, :, 1:-1] - padded[:, :, :-2]]
    unnamed x258 -> x29, local copies, waits for them, and re-layouts: 19.7 us -> 5.26 us
  transfers between devices with their start and end apart: 25 -> 6, of which waited for: 1 -> 1; matrix products, arithmetic and copies ran while one was open for 51% -> 0% of each run, Pallas kernels for 0% -> 52%
where the time goes in v1:
time: 111 us; the launch traced here: 110 us
  Pallas kernels  78.5 us (71%)
  starting transfers between devices  20.2 us (18%)
  local copies, waits for them, and re-layouts  5.98 us (5%)
  waiting for transfers between devices  4.36 us (4%)
    pallas_call x2, Pallas kernels, adjoint(): pl.pallas_call(functools.partial(adjoint_kernel, shot), out_shape=out_sha...  30.7 us
    pallas_call x1, Pallas kernels, forward(): pl.pallas_call(forward_kernel, out_shape=jax.ShapeDtypeStruct((2, 3, 6, 8...  28.5 us
    ppermute x3, starting transfers between devices, shards(): swap_chips = lambda x: lax.ppermute(x, 'space', between)  16.9 us
    pallas_call x2, Pallas kernels, pack(): pl.pallas_call(functools.partial(pack_kernel, with_mats), out_shape=out,...  11.9 us
    pallas_call x1, Pallas kernels, inject(): pl.pallas_call(inject_kernel, out_shape=jax.ShapeDtypeStruct((2, 3, SLOTS...  7.42 us
    unnamed x29, local copies, waits for them, and re-layouts  5.26 us
    ppermute x1, waiting for transfers between devices, shards(): total = keep + lax.ppermute(give, 'shot', [(0, 1), (1, 0)])  4.35 us
    ppermute x1, starting transfers between devices, shards(): total = keep + lax.ppermute(give, 'shot', [(0, 1), (1, 0)])  2.6 us
  transfers between devices with their start and end apart: 6, of which 1 were waited for; matrix products, arithmetic and copies ran while one was open for 0% of the time, Pallas kernels for 52%

profile of v1, /device:TPU:64, one launch (start us, length us, event | category | flops | bytes accessed | tf_op | source)
XLA Modules:
  0.0 110.0 jit_solution(542873080581086986)
XLA Ops:
  0.6 0.1 pad_add_fusion.meta
  0.7 0.0 copy-start.1
  0.7 2.3 %copy-done.1 = f32[9,2,8,64,128]{4,3,2,1,0:T(8,128)S(1)} copy-done((f32[9,2,8,64,128]{4,3,2,1,0:T(8,128)S(1)}, f32[9,2,8,64,128]{4,3,2,1,0:T(8,128)}, u32[]{:S(2)}) %copy-start.1) | copy-done | bytes 4718616
  3.0 0.0 copy-start.2
  3.0 0.9 copy-done.2
  4.0 0.0 copy-start.4
  4.0 0.9 copy-done.4
  4.9 0.0 copy-start.6
  5.0 0.9 copy-done.6
  5.9 0.0 copy-start
  5.9 0.0 slice-start
  5.9 6.2 %pack_forward.1 = (f32[46,64,128]{2,1,0:T(8,128)S(1)}, f32[46,64,128]{2,1,0:T(8,128)S(1)}) custom-call(s32[2]{0:T(128)S(1)} %pad_add_fusion.meta, f32[9,2,8,64,128]{4,3,2,1,0:T(8,128)S(1)} %copy-done.1, f32[8,64,128]{2,1,0:T(8,128)S(1)} %copy-done.2, f32[8,64,128]{2,1,0:T(8,128)S(1)} %copy-done.4, f32[8,64,128]{2,1,0:T(8,128)S(1)} %copy-done.6), custom_call_target="tpu_custom_call" | custom-call | tf_op jit(solution)/shard_map/pack_forward/pallas_call | solution.py:214
  12.1 5.6 %collective-permute-start = (f32[46,64,128]{2,1,0:T(8,128)S(1)}, f32[46,64,128]{2,1,0:T(8,128)S(1)}, u32[]{:S(2)}, u32[]{:S(2)}) collective-permute-start(f32[46,64,128]{2,1,0:T(8,128)S(1)} %get-tuple-element.9), channel_id=1, source_target_pairs={{1,2},{3,4},{5,6},{7,8},{9,10},{11,12},{13,14},{15,16},{17,18},{19... | collective-permute-start | bytes 4521992 | tf_op jit(solution)/shard_map/ppermute | solution.py:528
  17.8 0.0 copy-start.11
  17.8 0.0 copy-start.8
  17.8 0.0 slice-start.1
  17.8 0.1 collective-permute-start.1
  17.9 0.0 copy-done
  17.9 5.7 %pack_adjoint.1 = (f32[20,64,128]{2,1,0:T(8,128)S(1)}, f32[20,64,128]{2,1,0:T(8,128)S(1)}, f32[40,64,128]{2,1,0:T(8,128)S(1)}) custom-call(s32[2]{0:T(128)S(1)} %pad_add_fusion.meta, f32[9,2,8,64,128]{4,3,2,1,0:T(8,128)S(1)} %copy-done, f32[8,64,128]{2,1,0:T(8,128)S(1)} %copy-done.2, f32[8,64,128]{2,1,0:T(8,128)S(1)} %copy-done.4, f32[8,64,128]{2,1,0:T(8,128)S(1)} %copy-done.6), custom_call_target="tpu_custom_call" | custom-call | tf_op jit(solution)/shard_map/pack_adjoint/pallas_call | solution.py:214
  23.6 0.0 copy-start.3
  23.6 0.0 copy-start.5
  23.6 0.0 copy-start.7
  23.6 0.0 copy-start.9
  23.7 0.0 copy-start.10
  23.7 0.6 collective-permute-start.3
  24.2 5.6 %collective-permute-start.4 = (f32[20,64,128]{2,1,0:T(8,128)S(1)}, f32[20,64,128]{2,1,0:T(8,128)S(1)}, u32[]{:S(2)}, u32[]{:S(2)}) collective-permute-start(f32[20,64,128]{2,1,0:T(8,128)S(1)} %get-tuple-element.13), channel_id=1, source_target_pairs={{1,2},{3,4},{5,6},{7,8},{9,10},{11,12},{13,14},{15,16},{17,18},{19... | collective-permute-start | bytes 1966088 | tf_op jit(solution)/shard_map/ppermute | solution.py:528
  29.9 5.6 %collective-permute-start.2 = (f32[20,64,128]{2,1,0:T(8,128)S(1)}, f32[20,64,128]{2,1,0:T(8,128)S(1)}, u32[]{:S(2)}, u32[]{:S(2)}) collective-permute-start(f32[20,64,128]{2,1,0:T(8,128)S(1)} %get-tuple-element.11), channel_id=1, source_target_pairs={{1,2},{3,4},{5,6},{7,8},{9,10},{11,12},{13,14},{15,16},{17,18},{19... | collective-permute-start | bytes 1966088 | tf_op jit(solution)/shard_map/ppermute | solution.py:528
  35.5 0.0 copy-done.11
  35.6 0.0 copy-done.8
  35.6 7.4 %receivers.1 = f32[2,3,896,128]{3,2,1,0:T(8,128)S(1)} custom-call(s32[2]{0:T(128)S(1)} %pad_add_fusion.meta, s32[2,1024]{1,0:T(2,128)S(1)} %copy-done.8, f32[2,3,1024]{2,1,0:T(4,128)S(1)} %copy.11.amounts), custom_call_target="tpu_custom_call" | custom-call | tf_op jit(solution)/shard_map/receivers/pallas_call | solution.py:417
  43.0 0.0 collective-permute-done.cross.f_cross
  43.0 0.0 collective-permute-done.1.chip.f_chip
  43.0 0.0 slice-done
  43.0 0.0 slice-done.1
  43.0 0.0 copy-done.3
  43.0 0.0 copy-done.5
  43.0 0.0 copy-done.7
  43.1 0.0 copy-done.9
  43.1 0.0 copy-done.10
  43.1 28.5 %forward_steps.1.strains = f32[2,3,6,8,64,128]{5,4,3,2,1,0:T(8,128)S(1)} custom-call(s32[2]{0:T(128)S(1)} %pad_add_fusion.meta, s32[2]{0:T(128)S(1)} %copy-done.10, f32[2,3]{1,0:T(2,128)S(1)} %copy-done.9, f32[9,2,8,64,128]{4,3,2,1,0:T(8,128)S(1)} %bitcast.10, f32[8,64,128]{2,1,0:T(8,128)S(1)} %copy-done.3, f32[8,64,128]{2,1,0:T(8,128)S(1)} %copy-done.5, ...), custom_call_target="tpu_custom_call" | custom-call | tf_op jit(solution)/shard_map/forward_steps/pallas_call | solution.py:361
  71.6 0.0 collective-permute-done.4.cross
  71.6 0.0 collective-permute-done.3.chip
  71.7 15.3 %adjoint_steps.2.rest_0_ = f32[2,8,64,128]{3,2,1,0:T(8,128)S(1)} custom-call(s32[2]{0:T(128)S(1)} %pad_add_fusion.meta, f32[9,2,8,64,128]{4,3,2,1,0:T(8,128)S(1)} %copy-done, f32[8,64,128]{2,1,0:T(8,128)S(1)} %copy-done.3, f32[8,64,128]{2,1,0:T(8,128)S(1)} %copy-done.5, f32[8,64,128]{2,1,0:T(8,128)S(1)} %copy-done.7, ...), custom_call_target="tpu_custom_call" | custom-call | tf_op jit(solution)/shard_map/adjoint_steps/pallas_call | solution.py:510
  87.0 0.0 collective-permute-done.2.cross
  87.0 15.4 %adjoint_steps.3 = (f32[2,8,32,128]{3,2,1,0:T(8,128)S(1)}, f32[2,8,32,128]{3,2,1,0:T(8,128)S(1)}) custom-call(s32[2]{0:T(128)S(1)} %pad_add_fusion.meta, f32[9,2,8,64,128]{4,3,2,1,0:T(8,128)S(1)} %copy-done, f32[8,64,128]{2,1,0:T(8,128)S(1)} %copy-done.3, f32[8,64,128]{2,1,0:T(8,128)S(1)} %copy-done.5, f32[8,64,128]{2,1,0:T(8,128)S(1)} %copy-done.7, ...), custom_call_target="tpu_custom_call" | custom-call | tf_op jit(solution)/shard_map/adjoint_steps/pallas_call | solution.py:510
  102.3 2.6 %collective-permute-start.5 = (f32[2,8,32,128]{3,2,1,0:T(8,128)S(1)}, f32[2,8,32,128]{3,2,1,0:T(8,128)S(1)}, u32[]{:S(2)}, u32[]{:S(2)}) collective-permute-start(f32[2,8,32,128]{3,2,1,0:T(8,128)S(1)} %get-tuple-element.15), channel_id=1, source_target_pairs={{0,64},{64,0},{1,65},{65,1},{2,66},{66,2},{3,67},{67,3},{4,68},{68... | collective-permute-start | bytes 786440 | tf_op jit(solution)/shard_map/ppermute | solution.py:547
  104.9 4.4 %collective-permute-done.5 = f32[2,8,32,128]{3,2,1,0:T(8,128)S(1)} collective-permute-done((f32[2,8,32,128]{3,2,1,0:T(8,128)S(1)}, f32[2,8,32,128]{3,2,1,0:T(8,128)S(1)}, u32[]{:S(2)}, u32[]{:S(2)}) %collective-permute-start.5) | collective-permute-done | bytes 262176 | tf_op jit(solution)/shard_map/ppermute | solution.py:547
  109.3 0.7 slice_bitcast_fusion
  (3 shorter events, 0.1 us)
Async XLA Ops:
  0.7 2.3 %copy-start.1 = (f32[9,2,8,64,128]{4,3,2,1,0:T(8,128)S(1)}, f32[9,2,8,64,128]{4,3,2,1,0:T(8,128)}, u32[]{:S(2)}) copy-start(f32[9,2,8,64,128]{4,3,2,1,0:T(8,128)} %state.7) | copy-start | bytes 14155780
  3.0 0.9 copy-start.2
  4.0 0.9 copy-start.4
  4.9 0.9 copy-start.6
  5.9 12.0 %copy-start = (f32[9,2,8,64,128]{4,3,2,1,0:T(8,128)S(1)}, f32[9,2,8,64,128]{4,3,2,1,0:T(8,128)}, u32[]{:S(2)}) copy-start(f32[9,2,8,64,128]{4,3,2,1,0:T(8,128)} %state.9) | copy-start | bytes 14155780
  5.9 37.1 %slice-start = ((s8[4718592]{0:T(1024)(128)(4,1)}), s8[4194304]{0:T(1024)(128)(4,1)S(1)}, s32[]{:S(2)}) async-start(s8[4718592]{0:T(1024)(128)(4,1)} %bitcast.9), calls=%async_computation | async-start | bytes 8388608
  12.1 30.9 %collective-permute-start = (f32[46,64,128]{2,1,0:T(8,128)S(1)}, f32[46,64,128]{2,1,0:T(8,128)S(1)}, u32[]{:S(2)}, u32[]{:S(2)}) collective-permute-start(f32[46,64,128]{2,1,0:T(8,128)S(1)} %get-tuple-element.9), channel_id=1, source_target_pairs={{1,2},{3,4},{5,6},{7,8},{9,10},{11,12},{13,14},{15,16},{17,18},{19... | collective-permute-start | bytes 4521992 | tf_op jit(solution)/shard_map/ppermute | solution.py:528
  17.8 17.8 %copy-start.11 = (f32[2,3,1024]{2,0,1:T(2,128)S(1)}, f32[2,3,1024]{2,0,1:T(2,128)}, u32[]{:S(2)}) copy-start(f32[2,3,1024]{2,0,1:T(2,128)} %param.17) | copy-start | bytes 73732
  17.8 17.8 %copy-start.8 = (s32[2,1024]{1,0:T(2,128)S(1)}, s32[2,1024]{1,0:T(2,128)}, u32[]{:S(2)}) copy-start(s32[2,1024]{1,0:T(2,128)} %cells.1) | copy-start | bytes 24580
  17.8 25.2 %slice-start.1 = ((s8[4718592]{0:T(1024)(128)(4,1)}), s8[524288]{0:T(1024)(128)(4,1)S(1)}, s32[]{:S(2)}) async-start(s8[4718592]{0:T(1024)(128)(4,1)} %bitcast.9), calls=%async_computation.1 | async-start | bytes 1048576
  17.8 25.2 %collective-permute-start.1 = (f32[46,64,128]{2,1,0:T(8,128)S(1)}, f32[46,64,128]{2,1,0:T(8,128)S(1)}, u32[]{:S(2)}, u32[]{:S(2)}) collective-permute-start(f32[46,64,128]{2,1,0:T(8,128)S(1)} %get-tuple-element.10), channel_id=1, source_target_pairs={{0,1},{2,3},{4,5},{6,7},{8,9},{10,11},{12,13},{14,15},{16,17},{18,... | collective-permute-start | bytes 4521992 | tf_op jit(solution)/shard_map/ppermute | solution.py:529
  23.6 19.4 %copy-start.3 = (f32[8,64,128]{2,1,0:T(8,128)S(1)}, f32[8,64,128]{2,1,0:T(8,128)}, u32[]{:S(2)}) copy-start(f32[8,64,128]{2,1,0:T(8,128)} %lam.9) | copy-start | bytes 786436
  23.6 19.4 %copy-start.5 = (f32[8,64,128]{2,1,0:T(8,128)S(1)}, f32[8,64,128]{2,1,0:T(8,128)}, u32[]{:S(2)}) copy-start(f32[8,64,128]{2,1,0:T(8,128)} %mu.9) | copy-start | bytes 786436
  23.6 19.4 %copy-start.7 = (f32[8,64,128]{2,1,0:T(8,128)S(1)}, f32[8,64,128]{2,1,0:T(8,128)}, u32[]{:S(2)}) copy-start(f32[8,64,128]{2,1,0:T(8,128)} %buoy.9) | copy-start | bytes 786436
  23.6 19.4 %copy-start.9 = (f32[2,3]{1,0:T(2,128)S(1)}, f32[2,3]{1,0:T(2,128)}, u32[]{:S(2)}) copy-start(f32[2,3]{1,0:T(2,128)} %src_amp.1) | copy-start | bytes 76
  23.7 19.4 %copy-start.10 = (s32[2]{0:T(128)S(1)}, s32[2]{0:T(128)}, u32[]{:S(2)}) copy-start(s32[2]{0:T(128)} %src_index.1) | copy-start | bytes 28
  23.7 48.0 %collective-permute-start.3 = (f32[40,64,128]{2,1,0:T(8,128)S(1)}, f32[40,64,128]{2,1,0:T(8,128)S(1)}, u32[]{:S(2)}, u32[]{:S(2)}) collective-permute-start(f32[40,64,128]{2,1,0:T(8,128)S(1)} %get-tuple-element.12), channel_id=1, source_target_pairs={{0,1},{2,3},{4,5},{6,7},{8,9},{10,11},{12,13},{14,15},{16,17},{18,... | collective-permute-start | bytes 3932168 | tf_op jit(solution)/shard_map/ppermute | solution.py:529
  24.2 47.4 %collective-permute-start.4 = (f32[20,64,128]{2,1,0:T(8,128)S(1)}, f32[20,64,128]{2,1,0:T(8,128)S(1)}, u32[]{:S(2)}, u32[]{:S(2)}) collective-permute-start(f32[20,64,128]{2,1,0:T(8,128)S(1)} %get-tuple-element.13), channel_id=1, source_target_pairs={{1,2},{3,4},{5,6},{7,8},{9,10},{11,12},{13,14},{15,16},{17,18},{19... | collective-permute-start | bytes 1966088 | tf_op jit(solution)/shard_map/ppermute | solution.py:528
  29.9 57.1 %collective-permute-start.2 = (f32[20,64,128]{2,1,0:T(8,128)S(1)}, f32[20,64,128]{2,1,0:T(8,128)S(1)}, u32[]{:S(2)}, u32[]{:S(2)}) collective-permute-start(f32[20,64,128]{2,1,0:T(8,128)S(1)} %get-tuple-element.11), channel_id=1, source_target_pairs={{1,2},{3,4},{5,6},{7,8},{9,10},{11,12},{13,14},{15,16},{17,18},{19... | collective-permute-start | bytes 1966088 | tf_op jit(solution)/shard_map/ppermute | solution.py:528
  102.3 7.0 %collective-permute-start.5 = (f32[2,8,32,128]{3,2,1,0:T(8,128)S(1)}, f32[2,8,32,128]{3,2,1,0:T(8,128)S(1)}, u32[]{:S(2)}, u32[]{:S(2)}) collective-permute-start(f32[2,8,32,128]{3,2,1,0:T(8,128)S(1)} %get-tuple-element.15), channel_id=1, source_target_pairs={{0,64},{64,0},{1,65},{65,1},{2,66},{66,2},{3,67},{67,3},{4,68},{68... | collective-permute-start | bytes 786440 | tf_op jit(solution)/shard_map/ppermute | solution.py:547

commit v2 on v1

v2 whole, which is shorter than its diff:
```python
import functools

import jax
import jax.numpy as jnp
from jax import lax
from jax.experimental import pallas as pl
from jax.experimental.pallas import tpu as pltpu
from jax.sharding import PartitionSpec as P

courant = 0.2
VX, VY, VZ, SXX, SYY, SZZ, SYZ, SXZ, SXY = range(9)

SLOTS = 14
OWN = 3
PAD = 8

RIGHTWARD = (
    (VX, 5, 3, 0), (VY, 6, 2, 1), (VZ, 6, 2, 1), (SXX, 6, 2, 1), (SYY, 7, 1, 2), (SZZ, 7, 1, 2),
    (SYZ, 7, 1, 2), (SXZ, 6, 2, 1), (SXY, 6, 2, 1),
)
LEFTWARD = (
    (VX, 0, 2, 11), (VY, 0, 3, 11), (VZ, 0, 3, 11), (SXX, 0, 2, 11), (SYY, 0, 2, 11), (SZZ, 0, 2, 11),
    (SYZ, 0, 2, 11), (SXZ, 0, 2, 11), (SXY, 0, 2, 11),
)
MATS_RIGHTWARD = (6, 1)
MATS_LEFTWARD = (0, 11)
SENT = 20
CHUNK = 16


def of_shot(w, shot):
    return [ref.at[shot] for ref in w]


def lanes(rows):
    return lax.broadcasted_iota(jnp.int32, (rows, 128), 1)


def below_z(x):
    return jnp.where(lanes(x.shape[0]) == 0, 0.0, pltpu.roll(x, 1, 1))


def above_z(x):
    return jnp.where(lanes(x.shape[0]) == 127, 0.0, pltpu.roll(x, 127, 1))


def velocity_plane(w, kb, q, inject=None):
    for start in range(0, 64, CHUNK):
        at = pl.ds(PAD + start, CHUNK)
        down = pl.ds(PAD + start - 1, CHUNK)
        up = pl.ds(PAD + start + 1, CHUNK)
        flat = pl.ds(start, CHUNK)
        xy_b, xz_b = w[SXY][q - 1, at, :], w[SXZ][q - 1, at, :]
        new_x = w[VX][q - 1, at, :] + kb(q - 1, flat) * (
            (w[SXX][q, at, :] - w[SXX][q - 1, at, :])
            + (xy_b - w[SXY][q - 1, down, :])
            + (xz_b - below_z(xz_b))
        )
        yz, zz = w[SYZ][q, at, :], w[SZZ][q, at, :]
        scaled = kb(q, flat)
        new_y = w[VY][q, at, :] + scaled * (
            (w[SXY][q, at, :] - xy_b) + (w[SYY][q, up, :] - w[SYY][q, at, :]) + (yz - below_z(yz))
        )
        new_z = w[VZ][q, at, :] + scaled * (
            (w[SXZ][q, at, :] - xz_b) + (yz - w[SYZ][q, down, :]) + (above_z(zz) - zz)
        )
        if inject is not None:
            new_z = new_z + inject[q, flat, :]
        w[VX][q - 1, at, :] = new_x
        w[VY][q, at, :] = new_y
        w[VZ][q, at, :] = new_z


def strain_chunk(w, q, start):
    at = pl.ds(PAD + start, CHUNK)
    down = pl.ds(PAD + start - 1, CHUNK)
    up = pl.ds(PAD + start + 1, CHUNK)
    vx, vy, vz = w[VX][q, at, :], w[VY][q, at, :], w[VZ][q, at, :]
    exx = vx - w[VX][q - 1, at, :]
    eyy = vy - w[VY][q, down, :]
    ezz = vz - below_z(vz)
    eyz = (above_z(vy) - vy) + (w[VZ][q, up, :] - vz)
    exz = (above_z(vx) - vx) + (w[VZ][q + 1, at, :] - vz)
    exy = (w[VX][q, up, :] - vx) + (w[VY][q + 1, at, :] - vy)
    return exx, eyy, ezz, eyz, exz, exy


def stress_chunk(w, mats, q, start, strain, sign=1.0):
    at = pl.ds(PAD + start, CHUNK)
    flat = pl.ds(start, CHUNK)
    exx, eyy, ezz, eyz, exz, exy = strain
    twice = mats[2, q, flat, :]
    bulk = mats[1, q, flat, :] * (exx + eyy + ezz)
    once = 0.5 * twice
    for field, change in (
        (SXX, bulk + twice * exx),
        (SYY, bulk + twice * eyy),
        (SZZ, bulk + twice * ezz),
        (SYZ, once * eyz),
        (SXZ, once * exz),
        (SXY, once * exy),
    ):
        old = w[field][q, at, :]
        w[field][q, at, :] = old + change if sign > 0 else old - change


UNROLL = 4


def planes(low, high, body):
    whole = (high - low) // UNROLL

    def step(i, carry):
        for j in range(UNROLL):
            body(low + UNROLL * i + j)
        return carry

    lax.fori_loop(0, whole, step, 0)
    for q in range(low + whole * UNROLL, high):
        body(q)


def clear_edges(w, slots):
    zero = jnp.zeros((PAD, 128), jnp.float32)
    for field, top in ((VX, 1), (VY, 0), (VZ, 1), (SXY, 0), (SYY, 1), (SYZ, 0)):
        for slot in range(slots):
            w[field][slot, pl.ds(PAD + 64 if top else 0, PAD), :] = zero


def velocity_values(w, scaled, q):
    at, down, up = pl.ds(PAD, 64), pl.ds(PAD - 1, 64), pl.ds(PAD + 1, 64)
    xy_b, xz_b = w[SXY, q - 1, at, :], w[SXZ, q - 1, at, :]
    new_x = w[VX, q - 1, at, :] + scaled(q - 1) * (
        (w[SXX, q, at, :] - w[SXX, q - 1, at, :])
        + (xy_b - w[SXY, q - 1, down, :])
        + (xz_b - below_z(xz_b))
    )
    yz, zz = w[SYZ, q, at, :], w[SZZ, q, at, :]
    new_y = w[VY, q, at, :] + scaled(q) * (
        (w[SXY, q, at, :] - xy_b) + (w[SYY, q, up, :] - w[SYY, q, at, :]) + (yz - below_z(yz))
    )
    new_z = w[VZ, q, at, :] + scaled(q) * (
        (w[SXZ, q, at, :] - xz_b) + (yz - w[SYZ, q, down, :]) + (above_z(zz) - zz)
    )
    return new_x, new_y, new_z


def pack_kernel(with_mats, meta, state, lam, mu, buoy, *rest):
    if with_mats:
        cross, chip, w, b, sems, mat_sems = rest
        crosses = (cross.at[pl.ds(0, SENT)], cross.at[pl.ds(SENT, SENT)])
    else:
        cross_0, cross_1, chip, w, b, sems, mat_sems = rest
        crosses = (cross_0, cross_1)
    odd = lax.rem(meta[0], 2) == 1
    loads = {}
    for side, first in ((0, 0), (1, 5)):
        loads[2, side] = pltpu.make_async_copy(
            buoy.at[pl.ds(first, 3)], b.at[side], sems.at[2, side]
        )
    for shot in range(2):
        for side, first in ((0, 0), (1, 5)):
            loads[shot, side] = pltpu.make_async_copy(
                state.at[:, shot, pl.ds(first, 3)],
                w.at[shot, side, :, :, pl.ds(PAD, 64)],
                sems.at[shot, side],
            )
    for load in loads.values():
        load.start()
    mats = []
    if with_mats:
        for side, first in ((1, MATS_RIGHTWARD[0]), (0, MATS_LEFTWARD[0])):
            for i, array in enumerate((buoy, lam, mu)):
                mats.append((side, array.at[pl.ds(first, 2)], 2 * SENT + 2 * i))
    zero = jnp.zeros((PAD, 128), jnp.float32)
    for shot in range(2):
        for side in range(2):
            for field, row in ((SXY, 0), (SYZ, 0), (SYY, PAD + 64)):
                for slot in range(3):
                    w[shot, side, field, slot, pl.ds(row, PAD), :] = zero
    factor = courant if with_mats else -courant

    def send(to_cross):
        for i, (side, source, at) in enumerate(mats):
            target = cross if side == to_cross else chip
            pltpu.make_async_copy(source, target.at[pl.ds(at, 2)], mat_sems.at[i]).start()
        loads[2, 0].wait()
        loads[2, 1].wait()
        for shot in range(2):
            for side, table in ((1, RIGHTWARD), (0, LEFTWARD)):
                loads[shot, side].wait()
                slab = w.at[shot, side]
                out = crosses[shot] if side == to_cross else chip.at[pl.ds(SENT * shot, SENT)]
                fresh = {}
                for q in (1, 2):
                    values = velocity_values(slab, lambda i: factor * b[side, i], q)
                    fresh[VX, q - 1], fresh[VY, q], fresh[VZ, q] = values
                base = 0
                for field, first, count, _ in table:
                    for i in range(count):
                        slot = first + i - 5 * side
                        value = fresh.get((field, slot))
                        if value is None:
                            value = slab[field, slot, pl.ds(PAD, 64), :]
                        out[base + i] = value
                    base += count
        for i, (side, source, at) in enumerate(mats):
            target = cross if side == to_cross else chip
            pltpu.make_async_copy(source, target.at[pl.ds(at, 2)], mat_sems.at[i]).wait()

    @pl.when(odd)
    def _():
        send(1)

    @pl.when(jnp.logical_not(odd))
    def _():
        send(0)


def pack(meta, state, lam, mu, buoy, with_mats):
    hbm = pl.BlockSpec(memory_space=pltpu.HBM)
    big = jax.ShapeDtypeStruct((2 * SENT + (6 if with_mats else 0), 64, 128), jnp.float32)
    half = jax.ShapeDtypeStruct((SENT, 64, 128), jnp.float32)
    out = (big, big) if with_mats else (half, half, big)
    return pl.pallas_call(
        functools.partial(pack_kernel, with_mats),
        out_shape=out,
        in_specs=[pl.BlockSpec(memory_space=pltpu.SMEM)] + [hbm] * 4,
        out_specs=tuple(pl.BlockSpec(memory_space=pltpu.VMEM) for _ in out),
        scratch_shapes=[
            pltpu.VMEM((2, 2, 9, 3, 64 + 2 * PAD, 128), jnp.float32),
            pltpu.VMEM((2, 3, 64, 128), jnp.float32),
            pltpu.SemaphoreType.DMA((3, 2)),
            pltpu.SemaphoreType.DMA((6,)),
        ],
        compiler_params=pltpu.CompilerParams(vmem_limit_bytes=16 << 20),
        name="pack_forward" if with_mats else "pack_adjoint",
    )(meta, state, lam, mu, buoy)


def by_side(meta, cross, chip, action):
    odd = lax.rem(meta[0], 2) == 1

    @pl.when(odd)
    def _():
        action(chip, cross)

    @pl.when(jnp.logical_not(odd))
    def _():
        action(cross, chip)


def load_mats(meta, lam, mu, buoy, cross, chip, mats):
    scales = (courant, courant, 2.0 * courant)

    def own(p):
        for i, array in enumerate((buoy, lam, mu)):
            mats[i, p + OWN] = scales[i] * array[p]

    planes(0, 8, own)

    def halo(left, right):
        for i in range(3):
            for j in range(2):
                mats[i, 1 + j] = scales[i] * left[2 * SENT + 2 * i + j]
                mats[i, 11 + j] = scales[i] * right[2 * SENT + 2 * i + j]

    by_side(meta, cross, chip, halo)


def load_state(meta, state, shot, cross, chip, w):
    def own(p):
        for field in range(9):
            w[field][p + OWN, pl.ds(PAD, 64), :] = state[field, shot, p]

    planes(0, 8, own)

    def halo(left, right):
        for ref, table in ((left, RIGHTWARD), (right, LEFTWARD)):
            base = 0
            for field, _, count, slot in table:
                for i in range(count):
                    w[field][slot + i, pl.ds(PAD, 64), :] = ref[base + i]
                base += count

    by_side(meta, cross, chip, halo)


def forward_kernel(
    meta, src_index, src_amp, state, lam, mu, buoy, cross, chip, strains, mats, *w_both
):
    for shot in range(2):
        clear_edges(of_shot(w_both, shot), SLOTS)
    load_mats(meta, lam, mu, buoy, cross, chip, mats)
    kb = lambda q, flat: mats[0, q, flat, :]
    for shot in range(2):
        u = of_shot(w_both, shot)
        part = pl.ds(SENT * shot, SENT)
        load_state(meta, state, shot, cross.at[part], chip.at[part], u)

        def strain_only(moment, q):
            for begin in range(0, 64, CHUNK):
                for i, value in enumerate(strain_chunk(u, q, begin)):
                    strains[shot, moment, i, q - OWN, pl.ds(begin, CHUNK), :] = value

        def own(moment, q):
            for begin in range(0, 64, CHUNK):
                strain = strain_chunk(u, q, begin)
                for i, value in enumerate(strain):
                    strains[shot, moment, i, q - OWN, pl.ds(begin, CHUNK), :] = value
                stress_chunk(u, mats, q, begin, strain)

        def outer(q):
            for begin in range(0, 64, CHUNK):
                stress_chunk(u, mats, q, begin, strain_chunk(u, q, begin))

        cell = src_index[shot]
        slot = lax.shift_right_logical(cell, 13) - 8 * meta[0] + OWN
        row = jnp.bitwise_and(lax.shift_right_logical(cell, 7), 63) + PAD
        lane = jnp.bitwise_and(cell, 127)

        def source(moment, low, high):
            @pl.when(jnp.logical_and(slot >= low, slot < high))
            def _():
                amount = jnp.where(lanes(1) == lane, src_amp[shot, moment], 0.0)
                for field in (SXX, SYY, SZZ):
                    u[field][slot, pl.ds(row, 1), :] += amount

        velocity = functools.partial(velocity_plane, u, kb)
        planes(OWN, OWN + 9, velocity)
        planes(1, 3, outer)
        planes(OWN, OWN + 8, functools.partial(own, 0))
        planes(11, 13, outer)
        source(0, 1, 13)
        planes(OWN - 1, OWN + 10, velocity)
        planes(2, 3, outer)
        planes(OWN, OWN + 8, functools.partial(own, 1))
        planes(11, 12, outer)
        source(1, 2, 12)
        planes(OWN, OWN + 9, velocity)
        planes(OWN, OWN + 8, functools.partial(strain_only, 2))


def forward(meta, src_index, src_amp, state, lam, mu, buoy, cross, chip):
    vmem = pl.BlockSpec(memory_space=pltpu.VMEM)
    scalars = pl.BlockSpec(memory_space=pltpu.SMEM)
    return pl.pallas_call(
        forward_kernel,
        out_shape=(
            jax.ShapeDtypeStruct((2, 3, 6, 8, 64, 128), jnp.float32),
            jax.ShapeDtypeStruct((3, SLOTS, 64, 128), jnp.float32),
        ),
        in_specs=[scalars] * 3 + [vmem] * 6,
        out_specs=(vmem, vmem),
        scratch_shapes=[pltpu.VMEM((2, SLOTS, 64 + 2 * PAD, 128), jnp.float32)] * 9,
        compiler_params=pltpu.CompilerParams(vmem_limit_bytes=28 << 20),
        name="forward_steps",
    )(meta, src_index, src_amp, state, lam, mu, buoy, cross, chip)


def inject_kernel(meta, cells, amounts, out, rows_hot, values):
    base = (8 * meta[0] - OWN) * 64
    for shot in range(2):
        cell = cells[pl.ds(shot, 1), :]
        count = cell.shape[1]
        row = lax.shift_right_logical(cell, 7) - base
        lane = jnp.bitwise_and(cell, 127)

        def hot(k, carry):
            at = k * 128 + lax.broadcasted_iota(jnp.int32, (128, count), 0)
            rows_hot[pl.ds(k * 128, 128), :] = jnp.where(at == row, 1.0, 0.0).astype(jnp.bfloat16)
            return carry

        lax.fori_loop(0, SLOTS * 64 // 128, hot, 0)
        lane_hot = lax.broadcasted_iota(jnp.int32, (128, count), 0) == lane
        for moment in range(3):
            left = amounts[shot, pl.ds(moment, 1), :]
            for part in range(3):
                piece = left.astype(jnp.bfloat16).astype(jnp.float32)
                left = left - piece
                values[part, pl.ds(128 * moment, 128), :] = jnp.where(lane_hot, piece, 0.0).astype(
                    jnp.bfloat16
                )
        dims = (((1,), (1,)), ((), ()))
        size = SLOTS * 64 // 2
        for k in range(2):
            hot_rows = rows_hot[pl.ds(k * size, size), :]
            total = None
            for part in range(3):
                product = lax.dot_general(
                    hot_rows, values[part], dims, preferred_element_type=jnp.float32
                )
                total = product if total is None else total + product
            for moment in range(3):
                out[shot, moment, pl.ds(k * size, size), :] = total[:, 128 * moment : 128 * moment + 128]


def inject(meta, cells, amounts):
    count = cells.shape[1]
    vmem = pl.BlockSpec(memory_space=pltpu.VMEM)
    return pl.pallas_call(
        inject_kernel,
        out_shape=jax.ShapeDtypeStruct((2, 3, SLOTS * 64, 128), jnp.float32),
        in_specs=[pl.BlockSpec(memory_space=pltpu.SMEM), vmem, vmem],
        out_specs=vmem,
        scratch_shapes=[
            pltpu.VMEM((SLOTS * 64, count), jnp.bfloat16),
            pltpu.VMEM((3, 384, count), jnp.bfloat16),
        ],
        compiler_params=pltpu.CompilerParams(vmem_limit_bytes=24 << 20),
        name="receivers",
    )(meta, cells, amounts)


def adjoint_kernel(shot, meta, state, mats, cross, chip, strains, dense, *rest):
    if shot == 0:
        grads, *w = rest
    else:
        before, keep, give, grads, *w = rest
    clear_edges(w, SLOTS)
    load_state(meta, state, shot, cross, chip.at[pl.ds(SENT * shot, SENT)], w)
    kb = lambda q, flat: -mats[0, q, flat, :]

    def own(moment, stress, q):
        p = q - OWN
        for begin in range(0, 64, CHUNK):
            flat = pl.ds(begin, CHUNK)
            exx, eyy, ezz, eyz, exz, exy = strain_chunk(w, q, begin)
            fxx, fyy, fzz, fyz, fxz, fxy = [strains[shot, moment, i, p, flat, :] for i in range(6)]
            bulk = (fxx + fyy + fzz) * (exx + eyy + ezz)
            shear = 2.0 * (fxx * exx + fyy * eyy + fzz * ezz) + (
                fyz * eyz + fxz * exz + fxy * exy
            )
            if moment < 2:
                bulk, shear = bulk + grads[0, p, flat, :], shear + grads[1, p, flat, :]
            elif shot == 1:
                bulk, shear = bulk + before[0, p, flat, :], shear + before[1, p, flat, :]
            grads[0, p, flat, :] = bulk
            grads[1, p, flat, :] = shear
            if stress:
                stress_chunk(w, mats, q, begin, (exx, eyy, ezz, eyz, exz, exy), -1.0)

    def outer(q):
        for begin in range(0, 64, CHUNK):
            stress_chunk(w, mats, q, begin, strain_chunk(w, q, begin), -1.0)

    def velocity(moment, q):
        velocity_plane(w, kb, q, dense.at[shot, moment])

    for slot in (1, 2, 12, 13):
        w[VZ][slot, pl.ds(PAD, 64), :] += dense[shot, 2, slot]
    planes(OWN, OWN + 9, functools.partial(velocity, 2))
    planes(1, 3, outer)
    planes(OWN, OWN + 8, functools.partial(own, 2, True))
    planes(11, 13, outer)
    planes(OWN - 1, OWN + 10, functools.partial(velocity, 1))
    planes(2, 3, outer)
    planes(OWN, OWN + 8, functools.partial(own, 1, True))
    planes(11, 12, outer)
    planes(OWN, OWN + 9, functools.partial(velocity, 0))
    planes(OWN, OWN + 8, functools.partial(own, 0, False))
    if shot == 1:
        mine = pl.multiple_of(meta[1] * 32, 32)
        keep[...] = grads[:, :, pl.ds(mine, 32), :]
        give[...] = grads[:, :, pl.ds(pl.multiple_of(32 - mine, 32), 32), :]


def adjoint(shot, meta, state, mats, cross, chip, strains, dense, before):
    vmem = pl.BlockSpec(memory_space=pltpu.VMEM)
    whole = jax.ShapeDtypeStruct((2, 8, 64, 128), jnp.float32)
    half = jax.ShapeDtypeStruct((2, 8, 32, 128), jnp.float32)
    scratch = [pltpu.VMEM((SLOTS, 64 + 2 * PAD, 128), jnp.float32)] * 9
    operands = [meta, state, mats, cross, chip, strains, dense]
    out_shape, out_specs = whole, vmem
    if shot == 1:
        operands.append(before)
        out_shape, out_specs = (half, half), (vmem, vmem)
        scratch = [pltpu.VMEM(whole.shape, jnp.float32)] + scratch
    return pl.pallas_call(
        functools.partial(adjoint_kernel, shot),
        out_shape=out_shape,
        in_specs=[pl.BlockSpec(memory_space=pltpu.SMEM)] + [vmem] * (len(operands) - 1),
        out_specs=out_specs,
        scratch_shapes=scratch,
        compiler_params=pltpu.CompilerParams(vmem_limit_bytes=16 << 20),
        name="adjoint_steps",
    )(*operands)


def shards(
    lame_lambda, lame_shear, buoyancy, fwd_state, adj_state, src_index, src_amp, recv_index, residual
):
    count = lax.axis_size("space")
    onchip = [(i, i + 1) for i in range(0, count, 2)] + [(i + 1, i) for i in range(0, count, 2)]
    between = [(i, i + 1) for i in range(1, count - 1, 2)]
    between = between + [(j, i) for i, j in between]
    swap_chips = lambda x: lax.ppermute(x, "space", between)
    swap_cores = lambda x: lax.ppermute(x, "space", onchip)
    meta = jnp.stack([lax.axis_index("space"), lax.axis_index("shot")]).astype(jnp.int32)
    mats = (lame_lambda, lame_shear, buoyancy)
    f_cross, f_chip = pack(meta, fwd_state, *mats, True)
    f_cross = swap_chips(f_cross)
    a_cross_0, a_cross_1, a_chip = pack(meta, adj_state, *mats, False)
    a_cross_0 = swap_chips(a_cross_0)
    a_cross_1 = swap_chips(a_cross_1)
    f_chip = swap_cores(f_chip)
    a_chip = swap_cores(a_chip)
    dense = inject(meta, recv_index, residual).reshape(2, 3, SLOTS, 64, 128)
    strains, scaled = forward(meta, src_index, src_amp, fwd_state, *mats, f_cross, f_chip)
    grads = adjoint(
        0, meta, adj_state, scaled, a_cross_0, a_chip, strains, dense, None
    )
    keep, give = adjoint(
        1, meta, adj_state, scaled, a_cross_1, a_chip, strains, dense, grads
    )
    total = keep + lax.ppermute(give, "shot", [(0, 1), (1, 0)])
    return (total[0], total[1])


def solution(mesh):
    in_specs = (
        P("space", None, None),
        P("space", None, None),
        P("space", None, None),
        P(None, "shot", "space", None, None),
        P(None, "shot", "space", None, None),
        P("shot"),
        P("shot", None),
        P("shot", None),
        P("shot", None, None),
    )
    out_specs = (P("space", "shot", None), P("space", "shot", None))
    return jax.shard_map(shards, mesh=mesh, in_specs=in_specs, out_specs=out_specs, check_vma=False)
```

time: 111 us -> 61.3 us (0.55)
  Pallas kernels: 78.5 us -> 28.2 us
  waiting for transfers between devices: 4.36 us -> 6.46 us
    pallas_call x2, Pallas kernels: 30.7 us -> 9.07 us  [adjoint(): pl.pallas_call(functools.partial(adjoint_kernel, shot), out_shape=out_sha...]
    pallas_call x1, Pallas kernels: 28.5 us -> 7.51 us  [forward(): pl.pallas_call(forward_kernel, out_shape=(jax.ShapeDtypeStruct((2, 3, 6,...]
    pallas_call x2, Pallas kernels: 11.9 us -> 4.19 us  [pack(): pl.pallas_call(functools.partial(pack_kernel, with_mats), out_shape=out,...]
    ppermute x3, waiting for transfers between devices: 0.01 us -> 1.71 us  [shards(): swap_chips = lambda x: lax.ppermute(x, 'space', between)]
  transfers between devices with their start and end apart: 6 -> 6, of which waited for: 1 -> 2; matrix products, arithmetic and copies ran while one was open for 0% -> 0% of each run, Pallas kernels for 52% -> 35%
where the time goes in v2:
time: 61.3 us; the launch traced here: 61.1 us
  Pallas kernels  28.2 us (46%)
  starting transfers between devices  19.4 us (32%)
  waiting for transfers between devices  6.46 us (11%)
  local copies, waits for them, and re-layouts  5.98 us (10%)
  between operations  0.91 us (1%)
    ppermute x3, starting transfers between devices, shards(): swap_chips = lambda x: lax.ppermute(x, 'space', between)  17.1 us
    pallas_call x2, Pallas kernels, adjoint(): pl.pallas_call(functools.partial(adjoint_kernel, shot), out_shape=out_sha...  9.07 us
    pallas_call x1, Pallas kernels, forward(): pl.pallas_call(forward_kernel, out_shape=(jax.ShapeDtypeStruct((2, 3, 6,...  7.51 us
    pallas_call x1, Pallas kernels, inject(): pl.pallas_call(inject_kernel, out_shape=jax.ShapeDtypeStruct((2, 3, SLOTS...  7.42 us
    unnamed x29, local copies, waits for them, and re-layouts  5.26 us
    ppermute x1, waiting for transfers between devices, shards(): total = keep + lax.ppermute(give, 'shot', [(0, 1), (1, 0)])  4.75 us
    pallas_call x2, Pallas kernels, pack(): pl.pallas_call(functools.partial(pack_kernel, with_mats), out_shape=out,...  4.19 us
    ppermute x3, waiting for transfers between devices, shards(): swap_chips = lambda x: lax.ppermute(x, 'space', between)  1.71 us
  transfers between devices with their start and end apart: 6, of which 2 were waited for; matrix products, arithmetic and copies ran while one was open for 0% of the time, Pallas kernels for 35%

profile of v2, /device:TPU:64, one launch (start us, length us, event | category | flops | bytes accessed | tf_op | source)
XLA Modules:
  0.0 61.1 jit_solution(4550655846455175501)
XLA Ops:
  0.6 0.1 pad_add_fusion.meta
  0.7 0.0 copy-start.1
  0.7 2.3 %copy-done.1 = f32[9,2,8,64,128]{4,3,2,1,0:T(8,128)S(1)} copy-done((f32[9,2,8,64,128]{4,3,2,1,0:T(8,128)S(1)}, f32[9,2,8,64,128]{4,3,2,1,0:T(8,128)}, u32[]{:S(2)}) %copy-start.1) | copy-done | bytes 4718616
  3.0 0.0 copy-start.2
  3.0 0.9 %copy-done.2 = f32[8,64,128]{2,1,0:T(8,128)S(1)} copy-done((f32[8,64,128]{2,1,0:T(8,128)S(1)}, f32[8,64,128]{2,1,0:T(8,128)}, u32[]{:S(2)}) %copy-start.2) | copy-done | bytes 262168
  4.0 0.0 copy-start.4
  4.0 0.9 %copy-done.4 = f32[8,64,128]{2,1,0:T(8,128)S(1)} copy-done((f32[8,64,128]{2,1,0:T(8,128)S(1)}, f32[8,64,128]{2,1,0:T(8,128)}, u32[]{:S(2)}) %copy-start.4) | copy-done | bytes 262168
  4.9 0.0 copy-start.6
  5.0 0.9 %copy-done.6 = f32[8,64,128]{2,1,0:T(8,128)S(1)} copy-done((f32[8,64,128]{2,1,0:T(8,128)S(1)}, f32[8,64,128]{2,1,0:T(8,128)}, u32[]{:S(2)}) %copy-start.6) | copy-done | bytes 262168
  5.9 0.0 copy-start
  5.9 0.0 slice-start
  5.9 2.4 %pack_forward.1 = (f32[46,64,128]{2,1,0:T(8,128)S(1)}, f32[46,64,128]{2,1,0:T(8,128)S(1)}) custom-call(s32[2]{0:T(128)S(1)} %pad_add_fusion.meta, f32[9,2,8,64,128]{4,3,2,1,0:T(8,128)S(1)} %copy-done.1, f32[8,64,128]{2,1,0:T(8,128)S(1)} %copy-done.2, f32[8,64,128]{2,1,0:T(8,128)S(1)} %copy-done.4, f32[8,64,128]{2,1,0:T(8,128)S(1)} %copy-done.6), custom_call_target="tpu_custom_call" | custom-call | tf_op jit(solution)/shard_map/pack_forward/pallas_call | solution.py:225
  8.3 5.8 %collective-permute-start = (f32[46,64,128]{2,1,0:T(8,128)S(1)}, f32[46,64,128]{2,1,0:T(8,128)S(1)}, u32[]{:S(2)}, u32[]{:S(2)}) collective-permute-start(f32[46,64,128]{2,1,0:T(8,128)S(1)} %get-tuple-element.11), channel_id=1, source_target_pairs={{1,2},{3,4},{5,6},{7,8},{9,10},{11,12},{13,14},{15,16},{17,18},{19... | collective-permute-start | bytes 4521992 | tf_op jit(solution)/shard_map/ppermute | solution.py:497
  14.0 0.0 copy-start.11
  14.1 0.0 copy-start.8
  14.1 0.0 slice-start.1
  14.1 0.1 collective-permute-start.1
  14.2 0.0 copy-done
  14.2 1.8 %pack_adjoint.1 = (f32[20,64,128]{2,1,0:T(8,128)S(1)}, f32[20,64,128]{2,1,0:T(8,128)S(1)}, f32[40,64,128]{2,1,0:T(8,128)S(1)}) custom-call(s32[2]{0:T(128)S(1)} %pad_add_fusion.meta, f32[9,2,8,64,128]{4,3,2,1,0:T(8,128)S(1)} %copy-done, f32[8,64,128]{2,1,0:T(8,128)S(1)} %copy-done.2, f32[8,64,128]{2,1,0:T(8,128)S(1)} %copy-done.4, f32[8,64,128]{2,1,0:T(8,128)S(1)} %copy-done.6), custom_call_target="tpu_custom_call" | custom-call | tf_op jit(solution)/shard_map/pack_adjoint/pallas_call | solution.py:225
  16.0 0.0 copy-start.3
  16.0 0.0 copy-start.5
  16.1 0.0 copy-start.7
  16.1 0.0 copy-start.9
  16.1 0.0 copy-start.10
  16.1 0.6 collective-permute-start.3
  16.7 5.6 %collective-permute-start.4 = (f32[20,64,128]{2,1,0:T(8,128)S(1)}, f32[20,64,128]{2,1,0:T(8,128)S(1)}, u32[]{:S(2)}, u32[]{:S(2)}) collective-permute-start(f32[20,64,128]{2,1,0:T(8,128)S(1)} %get-tuple-element.17), channel_id=1, source_target_pairs={{1,2},{3,4},{5,6},{7,8},{9,10},{11,12},{13,14},{15,16},{17,18},{19... | collective-permute-start | bytes 1966088 | tf_op jit(solution)/shard_map/ppermute | solution.py:497
  22.3 5.6 %collective-permute-start.2 = (f32[20,64,128]{2,1,0:T(8,128)S(1)}, f32[20,64,128]{2,1,0:T(8,128)S(1)}, u32[]{:S(2)}, u32[]{:S(2)}) collective-permute-start(f32[20,64,128]{2,1,0:T(8,128)S(1)} %get-tuple-element.14), channel_id=1, source_target_pairs={{1,2},{3,4},{5,6},{7,8},{9,10},{11,12},{13,14},{15,16},{17,18},{19... | collective-permute-start | bytes 1966088 | tf_op jit(solution)/shard_map/ppermute | solution.py:497
  28.0 0.0 copy-done.11
  28.0 0.0 copy-done.8
  28.0 7.4 %receivers.1 = f32[2,3,896,128]{3,2,1,0:T(8,128)S(1)} custom-call(s32[2]{0:T(128)S(1)} %pad_add_fusion.meta, s32[2,1024]{1,0:T(2,128)S(1)} %copy-done.8, f32[2,3,1024]{2,1,0:T(4,128)S(1)} %copy.11.amounts), custom_call_target="tpu_custom_call" | custom-call | tf_op jit(solution)/shard_map/receivers/pallas_call | solution.py:401
  35.4 0.0 collective-permute-done.cross
  35.4 0.0 collective-permute-done.1.chip
  35.4 0.0 slice-done
  35.4 0.0 slice-done.1
  35.5 0.0 copy-done.3
  35.5 0.0 copy-done.5
  35.5 0.0 copy-done.7
  35.5 0.0 copy-done.9
  35.5 0.0 copy-done.10
  35.5 7.5 %forward_steps.1 = (f32[2,3,6,8,64,128]{5,4,3,2,1,0:T(8,128)S(1)}, f32[3,14,64,128]{3,2,1,0:T(8,128)S(1)}) custom-call(s32[2]{0:T(128)S(1)} %pad_add_fusion.meta, s32[2]{0:T(128)S(1)} %copy-done.10, f32[2,3]{1,0:T(2,128)S(1)} %copy-done.9, f32[9,2,8,64,128]{4,3,2,1,0:T(8,128)S(1)} %bitcast.10, f32[8,64,128]{2,1,0:T(8,128)S(1)} %copy-done.3, ...), custom_call_target="tpu_custom_call" | custom-call | tf_op jit(solution)/shard_map/forward_steps/pallas_call | solution.py:347
  43.0 0.0 collective-permute-done.4.cross
  43.0 0.0 collective-permute-done.3.chip
  43.1 4.5 %adjoint_steps.2.rest_0_ = f32[2,8,64,128]{3,2,1,0:T(8,128)S(1)} custom-call(s32[2]{0:T(128)S(1)} %pad_add_fusion.meta, f32[9,2,8,64,128]{4,3,2,1,0:T(8,128)S(1)} %copy-done, f32[3,14,64,128]{3,2,1,0:T(8,128)S(1)} %get-tuple-element.13.mats, f32[20,64,128]{2,1,0:T(8,128)S(1)} %collective-permute-done.4.cross, ...), custom_call_target="tpu_custom_call" | custom-call | tf_op jit(solution)/shard_map/adjoint_steps/pallas_call | solution.py:479
  47.6 1.7 %collective-permute-done.2.cross = f32[20,64,128]{2,1,0:T(8,128)S(1)} collective-permute-done((f32[20,64,128]{2,1,0:T(8,128)S(1)}, f32[20,64,128]{2,1,0:T(8,128)S(1)}, u32[]{:S(2)}, u32[]{:S(2)}) %collective-permute-start.2) | collective-permute-done | bytes 655392 | tf_op jit(solution)/shard_map/ppermute | solution.py:497
  49.3 4.5 %adjoint_steps.3 = (f32[2,8,32,128]{3,2,1,0:T(8,128)S(1)}, f32[2,8,32,128]{3,2,1,0:T(8,128)S(1)}) custom-call(s32[2]{0:T(128)S(1)} %pad_add_fusion.meta, f32[9,2,8,64,128]{4,3,2,1,0:T(8,128)S(1)} %copy-done, f32[3,14,64,128]{3,2,1,0:T(8,128)S(1)} %get-tuple-element.13.mats, f32[20,64,128]{2,1,0:T(8,128)S(1)} %collective-permute-done.2.cross, ...), custom_call_target="tpu_custom_call" | custom-call | tf_op jit(solution)/shard_map/adjoint_steps/pallas_call | solution.py:479
  53.9 1.7 %collective-permute-start.5 = (f32[2,8,32,128]{3,2,1,0:T(8,128)S(1)}, f32[2,8,32,128]{3,2,1,0:T(8,128)S(1)}, u32[]{:S(2)}, u32[]{:S(2)}) collective-permute-start(f32[2,8,32,128]{3,2,1,0:T(8,128)S(1)} %get-tuple-element.19), channel_id=1, source_target_pairs={{0,64},{64,0},{1,65},{65,1},{2,66},{66,2},{3,67},{67,3},{4,68},{68... | collective-permute-start | bytes 786440 | tf_op jit(solution)/shard_map/ppermute | solution.py:516
  55.6 4.7 %collective-permute-done.5 = f32[2,8,32,128]{3,2,1,0:T(8,128)S(1)} collective-permute-done((f32[2,8,32,128]{3,2,1,0:T(8,128)S(1)}, f32[2,8,32,128]{3,2,1,0:T(8,128)S(1)}, u32[]{:S(2)}, u32[]{:S(2)}) %collective-permute-start.5) | collective-permute-done | bytes 262176 | tf_op jit(solution)/shard_map/ppermute | solution.py:516
  60.3 0.7 %slice_bitcast_fusion = (f32[8,32,128]{2,1,0:T(8,128)}, f32[8,32,128]{2,1,0:T(8,128)}) fusion(f32[2,8,32,128]{3,2,1,0:T(8,128)S(1)} %add.3), kind=kLoop, calls=%fused_computation | loop fusion | bytes 524288 | tf_op jit(solution)/shard_map/squeeze | solution.py:517
  (3 shorter events, 0.1 us)
Async XLA Ops:
  0.7 2.3 %copy-start.1 = (f32[9,2,8,64,128]{4,3,2,1,0:T(8,128)S(1)}, f32[9,2,8,64,128]{4,3,2,1,0:T(8,128)}, u32[]{:S(2)}) copy-start(f32[9,2,8,64,128]{4,3,2,1,0:T(8,128)} %state.6) | copy-start | bytes 14155780
  3.0 0.9 %copy-start.2 = (f32[8,64,128]{2,1,0:T(8,128)S(1)}, f32[8,64,128]{2,1,0:T(8,128)}, u32[]{:S(2)}) copy-start(f32[8,64,128]{2,1,0:T(8,128)} %lam.5) | copy-start | bytes 786436
  4.0 0.9 %copy-start.4 = (f32[8,64,128]{2,1,0:T(8,128)S(1)}, f32[8,64,128]{2,1,0:T(8,128)}, u32[]{:S(2)}) copy-start(f32[8,64,128]{2,1,0:T(8,128)} %mu.5) | copy-start | bytes 786436
  4.9 0.9 %copy-start.6 = (f32[8,64,128]{2,1,0:T(8,128)S(1)}, f32[8,64,128]{2,1,0:T(8,128)}, u32[]{:S(2)}) copy-start(f32[8,64,128]{2,1,0:T(8,128)} %buoy.5) | copy-start | bytes 786436
  5.9 8.3 %copy-start = (f32[9,2,8,64,128]{4,3,2,1,0:T(8,128)S(1)}, f32[9,2,8,64,128]{4,3,2,1,0:T(8,128)}, u32[]{:S(2)}) copy-start(f32[9,2,8,64,128]{4,3,2,1,0:T(8,128)} %state.9) | copy-start | bytes 14155780
  5.9 29.5 %slice-start = ((s8[4718592]{0:T(1024)(128)(4,1)}), s8[4194304]{0:T(1024)(128)(4,1)S(1)}, s32[]{:S(2)}) async-start(s8[4718592]{0:T(1024)(128)(4,1)} %bitcast.9), calls=%async_computation | async-start | bytes 8388608
  8.3 27.2 %collective-permute-start = (f32[46,64,128]{2,1,0:T(8,128)S(1)}, f32[46,64,128]{2,1,0:T(8,128)S(1)}, u32[]{:S(2)}, u32[]{:S(2)}) collective-permute-start(f32[46,64,128]{2,1,0:T(8,128)S(1)} %get-tuple-element.11), channel_id=1, source_target_pairs={{1,2},{3,4},{5,6},{7,8},{9,10},{11,12},{13,14},{15,16},{17,18},{19... | collective-permute-start | bytes 4521992 | tf_op jit(solution)/shard_map/ppermute | solution.py:497
  14.0 13.9 %copy-start.11 = (f32[2,3,1024]{2,0,1:T(2,128)S(1)}, f32[2,3,1024]{2,0,1:T(2,128)}, u32[]{:S(2)}) copy-start(f32[2,3,1024]{2,0,1:T(2,128)} %param.17) | copy-start | bytes 73732
  14.1 13.9 %copy-start.8 = (s32[2,1024]{1,0:T(2,128)S(1)}, s32[2,1024]{1,0:T(2,128)}, u32[]{:S(2)}) copy-start(s32[2,1024]{1,0:T(2,128)} %cells.1) | copy-start | bytes 24580
  14.1 21.4 %slice-start.1 = ((s8[4718592]{0:T(1024)(128)(4,1)}), s8[524288]{0:T(1024)(128)(4,1)S(1)}, s32[]{:S(2)}) async-start(s8[4718592]{0:T(1024)(128)(4,1)} %bitcast.9), calls=%async_computation.1 | async-start | bytes 1048576
  14.1 21.3 %collective-permute-start.1 = (f32[46,64,128]{2,1,0:T(8,128)S(1)}, f32[46,64,128]{2,1,0:T(8,128)S(1)}, u32[]{:S(2)}, u32[]{:S(2)}) collective-permute-start(f32[46,64,128]{2,1,0:T(8,128)S(1)} %get-tuple-element.12), channel_id=1, source_target_pairs={{0,1},{2,3},{4,5},{6,7},{8,9},{10,11},{12,13},{14,15},{16,17},{18,... | collective-permute-start | bytes 4521992 | tf_op jit(solution)/shard_map/ppermute | solution.py:498
  16.0 19.4 %copy-start.3 = (f32[8,64,128]{2,1,0:T(8,128)S(1)}, f32[8,64,128]{2,1,0:T(8,128)}, u32[]{:S(2)}) copy-start(f32[8,64,128]{2,1,0:T(8,128)} %lam.5) | copy-start | bytes 786436
  16.0 19.4 %copy-start.5 = (f32[8,64,128]{2,1,0:T(8,128)S(1)}, f32[8,64,128]{2,1,0:T(8,128)}, u32[]{:S(2)}) copy-start(f32[8,64,128]{2,1,0:T(8,128)} %mu.5) | copy-start | bytes 786436
  16.1 19.4 %copy-start.7 = (f32[8,64,128]{2,1,0:T(8,128)S(1)}, f32[8,64,128]{2,1,0:T(8,128)}, u32[]{:S(2)}) copy-start(f32[8,64,128]{2,1,0:T(8,128)} %buoy.5) | copy-start | bytes 786436
  16.1 19.4 %copy-start.9 = (f32[2,3]{1,0:T(2,128)S(1)}, f32[2,3]{1,0:T(2,128)}, u32[]{:S(2)}) copy-start(f32[2,3]{1,0:T(2,128)} %src_amp.1) | copy-start | bytes 76
  16.1 19.4 %copy-start.10 = (s32[2]{0:T(128)S(1)}, s32[2]{0:T(128)}, u32[]{:S(2)}) copy-start(s32[2]{0:T(128)} %src_index.1) | copy-start | bytes 28
  16.1 27.0 %collective-permute-start.3 = (f32[40,64,128]{2,1,0:T(8,128)S(1)}, f32[40,64,128]{2,1,0:T(8,128)S(1)}, u32[]{:S(2)}, u32[]{:S(2)}) collective-permute-start(f32[40,64,128]{2,1,0:T(8,128)S(1)} %get-tuple-element.15), channel_id=1, source_target_pairs={{0,1},{2,3},{4,5},{6,7},{8,9},{10,11},{12,13},{14,15},{16,17},{18,... | collective-permute-start | bytes 3932168 | tf_op jit(solution)/shard_map/ppermute | solution.py:498
  16.7 26.4 %collective-permute-start.4 = (f32[20,64,128]{2,1,0:T(8,128)S(1)}, f32[20,64,128]{2,1,0:T(8,128)S(1)}, u32[]{:S(2)}, u32[]{:S(2)}) collective-permute-start(f32[20,64,128]{2,1,0:T(8,128)S(1)} %get-tuple-element.17), channel_id=1, source_target_pairs={{1,2},{3,4},{5,6},{7,8},{9,10},{11,12},{13,14},{15,16},{17,18},{19... | collective-permute-start | bytes 1966088 | tf_op jit(solution)/shard_map/ppermute | solution.py:497
  22.3 27.0 %collective-permute-start.2 = (f32[20,64,128]{2,1,0:T(8,128)S(1)}, f32[20,64,128]{2,1,0:T(8,128)S(1)}, u32[]{:S(2)}, u32[]{:S(2)}) collective-permute-start(f32[20,64,128]{2,1,0:T(8,128)S(1)} %get-tuple-element.14), channel_id=1, source_target_pairs={{1,2},{3,4},{5,6},{7,8},{9,10},{11,12},{13,14},{15,16},{17,18},{19... | collective-permute-start | bytes 1966088 | tf_op jit(solution)/shard_map/ppermute | solution.py:497
  53.9 6.5 %collective-permute-start.5 = (f32[2,8,32,128]{3,2,1,0:T(8,128)S(1)}, f32[2,8,32,128]{3,2,1,0:T(8,128)S(1)}, u32[]{:S(2)}, u32[]{:S(2)}) collective-permute-start(f32[2,8,32,128]{3,2,1,0:T(8,128)S(1)} %get-tuple-element.19), channel_id=1, source_target_pairs={{0,64},{64,0},{1,65},{65,1},{2,66},{66,2},{3,67},{67,3},{4,68},{68... | collective-permute-start | bytes 786440 | tf_op jit(solution)/shard_map/ppermute | solution.py:516

commit v3 on v2

v3 whole, which is shorter than its diff:
```python
import functools

import jax
import jax.numpy as jnp
from jax import lax
from jax.experimental import pallas as pl
from jax.experimental.pallas import tpu as pltpu
from jax.sharding import PartitionSpec as P

courant = 0.2
VX, VY, VZ, SXX, SYY, SZZ, SYZ, SXZ, SXY = range(9)

SLOTS = 14
OWN = 3
PAD = 8

NORMAL_X = (SXX, SXZ, SXY)
STRESSES = (SXX, SYY, SZZ, SYZ, SXZ, SXY)
RIGHTWARD = (
    ((VX, 1, "second"), (VX, 2, "raw"), (VY, 2, "second"), (VZ, 2, "second"))
    + tuple((field, 1, "fresh") for field in NORMAL_X)
    + tuple((field, 2, "raw") for field in STRESSES)
)
LEFTWARD = (
    ((VX, 11, "first"), (VY, 11, "raw"), (VY, 12, "first"), (VZ, 11, "raw"), (VZ, 12, "first"))
    + tuple((field, 11, "raw") for field in STRESSES)
    + tuple((field, 12, "fresh") for field in STRESSES)
)
MATS_RIGHTWARD = ((0, 6, 1), (0, 7, 2), (1, 7, 2), (2, 7, 2))
MATS_LEFTWARD = ((0, 0, 11), (0, 1, 12), (1, 0, 11), (2, 0, 11))
SENT = 17
SCALES = (courant, courant, 2.0 * courant)
VMEM_SPEC = pl.BlockSpec(memory_space=pltpu.VMEM)
SMEM_SPEC = pl.BlockSpec(memory_space=pltpu.SMEM)
SLABS = (jax.ShapeDtypeStruct((2, SLOTS, 64 + 2 * PAD, 128), jnp.float32),) * 9
STRAINS = jax.ShapeDtypeStruct((2, 3, 6, 8, 64, 128), jnp.float32)
MATS = jax.ShapeDtypeStruct((3, SLOTS, 64, 128), jnp.float32)
GRADS = jax.ShapeDtypeStruct((2, 8, 64, 128), jnp.float32)
CHUNK = 16


def of_shot(w, shot):
    return [ref.at[shot] for ref in w]


def lanes(rows):
    return lax.broadcasted_iota(jnp.int32, (rows, 128), 1)


def below_z(x):
    return jnp.where(lanes(x.shape[0]) == 0, 0.0, pltpu.roll(x, 1, 1))


def above_z(x):
    return jnp.where(lanes(x.shape[0]) == 127, 0.0, pltpu.roll(x, 127, 1))


def velocity_plane(w, kb, q, inject=None):
    for start in range(0, 64, CHUNK):
        at = pl.ds(PAD + start, CHUNK)
        down = pl.ds(PAD + start - 1, CHUNK)
        up = pl.ds(PAD + start + 1, CHUNK)
        flat = pl.ds(start, CHUNK)
        xy_b, xz_b = w[SXY][q - 1, at, :], w[SXZ][q - 1, at, :]
        new_x = w[VX][q - 1, at, :] + kb(q - 1, flat) * (
            (w[SXX][q, at, :] - w[SXX][q - 1, at, :])
            + (xy_b - w[SXY][q - 1, down, :])
            + (xz_b - below_z(xz_b))
        )
        yz, zz = w[SYZ][q, at, :], w[SZZ][q, at, :]
        scaled = kb(q, flat)
        new_y = w[VY][q, at, :] + scaled * (
            (w[SXY][q, at, :] - xy_b) + (w[SYY][q, up, :] - w[SYY][q, at, :]) + (yz - below_z(yz))
        )
        new_z = w[VZ][q, at, :] + scaled * (
            (w[SXZ][q, at, :] - xz_b) + (yz - w[SYZ][q, down, :]) + (above_z(zz) - zz)
        )
        if inject is not None:
            new_z = new_z + inject[q, flat, :]
        w[VX][q - 1, at, :] = new_x
        w[VY][q, at, :] = new_y
        w[VZ][q, at, :] = new_z


def strain_chunk(w, q, start):
    at = pl.ds(PAD + start, CHUNK)
    down = pl.ds(PAD + start - 1, CHUNK)
    up = pl.ds(PAD + start + 1, CHUNK)
    vx, vy, vz = w[VX][q, at, :], w[VY][q, at, :], w[VZ][q, at, :]
    exx = vx - w[VX][q - 1, at, :]
    eyy = vy - w[VY][q, down, :]
    ezz = vz - below_z(vz)
    eyz = (above_z(vy) - vy) + (w[VZ][q, up, :] - vz)
    exz = (above_z(vx) - vx) + (w[VZ][q + 1, at, :] - vz)
    exy = (w[VX][q, up, :] - vx) + (w[VY][q + 1, at, :] - vy)
    return exx, eyy, ezz, eyz, exz, exy


def stress_chunk(w, mats, q, start, strain, sign=1.0):
    at = pl.ds(PAD + start, CHUNK)
    flat = pl.ds(start, CHUNK)
    exx, eyy, ezz, eyz, exz, exy = strain
    twice = mats[2, q, flat, :]
    bulk = mats[1, q, flat, :] * (exx + eyy + ezz)
    once = 0.5 * twice
    for field, change in (
        (SXX, bulk + twice * exx),
        (SYY, bulk + twice * eyy),
        (SZZ, bulk + twice * ezz),
        (SYZ, once * eyz),
        (SXZ, once * exz),
        (SXY, once * exy),
    ):
        old = w[field][q, at, :]
        w[field][q, at, :] = old + change if sign > 0 else old - change


UNROLL = 2


def planes(low, count, body):
    whole = count // UNROLL

    def step(i, carry):
        for j in range(UNROLL):
            body(low + UNROLL * i + j)
        return carry

    if whole > 1:
        lax.fori_loop(0, whole, step, 0)
    else:
        for j in range(whole * UNROLL):
            body(low + j)
    for j in range(whole * UNROLL, count):
        body(low + j)


def clear_edges(w, slots):
    zero = jnp.zeros((PAD, 128), jnp.float32)
    for field, top in ((VX, 1), (VY, 0), (VZ, 1), (SXY, 0), (SYY, 1), (SYZ, 0)):
        for slot in range(slots):
            w[field][slot, pl.ds(PAD + 64 if top else 0, PAD), :] = zero


def early_velocities(w, shot, scaled, q, begin):
    at = pl.ds(PAD + begin, CHUNK)
    down = pl.ds(PAD + begin - 1, CHUNK)
    up = pl.ds(PAD + begin + 1, CHUNK)
    xy_b, xz_b = w[SXY][shot, q - 1, at, :], w[SXZ][shot, q - 1, at, :]
    new_x = w[VX][shot, q - 1, at, :] + scaled(q - 1) * (
        (w[SXX][shot, q, at, :] - w[SXX][shot, q - 1, at, :])
        + (xy_b - w[SXY][shot, q - 1, down, :])
        + (xz_b - below_z(xz_b))
    )
    yz, zz = w[SYZ][shot, q, at, :], w[SZZ][shot, q, at, :]
    new_y = w[VY][shot, q, at, :] + scaled(q) * (
        (w[SXY][shot, q, at, :] - xy_b)
        + (w[SYY][shot, q, up, :] - w[SYY][shot, q, at, :])
        + (yz - below_z(yz))
    )
    new_z = w[VZ][shot, q, at, :] + scaled(q) * (
        (w[SXZ][shot, q, at, :] - xz_b) + (yz - w[SYZ][shot, q, down, :]) + (above_z(zz) - zz)
    )
    return new_x, new_y, new_z


def pack_kernel(is_forward, meta, state, lam, mu, buoy, *rest):
    if is_forward:
        cross, chip, *w, early, edge, sems, edge_sems = rest
    else:
        cells, amounts, cross, chip, *w, early, edge, sems, edge_sems, hot, values, dense = rest
    odd = lax.rem(meta[0], 2) == 1
    edges = []
    for i, array in enumerate((buoy, lam, mu)):
        for side, first in ((0, 0), (1, 5)):
            edges.append(
                pltpu.make_async_copy(
                    array.at[pl.ds(first, 3)], edge.at[i, side], edge_sems.at[i, side]
                )
            )
    loads = [
        [
            pltpu.make_async_copy(
                state.at[field, shot],
                w[field].at[shot, pl.ds(OWN, 8), pl.ds(PAD, 64)],
                sems.at[shot, field],
            )
            for field in range(9)
        ]
        for shot in range(2)
    ]
    for load in edges + loads[0] + loads[1]:
        load.start()
    for shot in range(2):
        clear_edges(of_shot(w, shot), SLOTS)
    zero = jnp.zeros((PAD, 128), jnp.float32)
    for shot in range(2):
        for side in range(2):
            for field, row in ((VX, PAD + 64), (VY, 0), (VZ, PAD + 64)):
                for slot in range(2):
                    early[shot, side, field, slot, pl.ds(row, PAD), :] = zero
    if not is_forward:
        base = (8 * meta[0] - OWN) * 64
        for shot in range(2):
            cell = cells[pl.ds(shot, 1), :]
            for i, plane in enumerate((1, 2, 6, 7)):
                hot[pl.ds(64 * i, 64), :] = rows_of(cell, base, (plane + OWN) * 64, 64)
            split_values(amounts, shot, cell, (2,), values)
            dense[shot] = gathered(hot[...], values[...], 1)
    for load in edges:
        load.wait()
    factor = courant if is_forward else -courant

    def send(to_cross):
        for shot in range(2):
            for load in loads[shot]:
                load.wait()
            for side, table in ((1, RIGHTWARD), (0, LEFTWARD)):
                target = cross if side == to_cross else chip
                plane = 6 if side == 1 else 1
                new = early.at[shot, side]
                for j in range(2):
                    q = OWN + plane + j
                    for begin in range(0, 64, CHUNK):
                        at, flat = pl.ds(PAD + begin, CHUNK), pl.ds(begin, CHUNK)
                        scaled = lambda q: factor * edge[0, side, q - OWN - 5 * side, flat, :]
                        new_x, new_y, new_z = early_velocities(w, shot, scaled, q, begin)
                        if not is_forward:
                            row = 64 * (2 * side + j) + begin
                            new_z = new_z + dense[shot, pl.ds(row, CHUNK), :]
                        new[VX, j, at, :] = new_x
                        new[VY, j, at, :] = new_y
                        new[VZ, j, at, :] = new_z
                for begin in range(0, 64, CHUNK):
                    at, flat = pl.ds(PAD + begin, CHUNK), pl.ds(begin, CHUNK)
                    down, up = pl.ds(PAD + begin - 1, CHUNK), pl.ds(PAD + begin + 1, CHUNK)
                    vx, vy, vz = new[VX, 1, at, :], new[VY, 0, at, :], new[VZ, 0, at, :]
                    exx = vx - new[VX, 0, at, :]
                    eyy = vy - new[VY, 0, down, :]
                    ezz = vz - below_z(vz)
                    eyz = (above_z(vy) - vy) + (new[VZ, 0, up, :] - vz)
                    exz = (above_z(vx) - vx) + (new[VZ, 1, at, :] - vz)
                    exy = (new[VX, 1, up, :] - vx) + (new[VY, 1, at, :] - vy)
                    once = factor * edge[2, side, plane - 5 * side, flat, :]
                    twice = 2.0 * once
                    bulk = (factor * edge[1, side, plane - 5 * side, flat, :]) * (exx + eyy + ezz)
                    change = {
                        SXX: bulk + twice * exx,
                        SYY: bulk + twice * eyy,
                        SZZ: bulk + twice * ezz,
                        SYZ: once * eyz,
                        SXZ: once * exz,
                        SXY: once * exy,
                    }
                    for i, (field, _, kind) in enumerate(table):
                        if kind == "raw":
                            value = w[field][shot, OWN + 7 * side, at, :]
                        elif kind == "fresh":
                            value = w[field][shot, OWN + plane, at, :] + change[field]
                        else:
                            value = new[field, 0 if kind == "first" else 1, at, :]
                        target[SENT * shot + i, flat, :] = value
        if is_forward:
            for side, mats in ((1, MATS_RIGHTWARD), (0, MATS_LEFTWARD)):
                target = cross if side == to_cross else chip
                for i, (which, own, _) in enumerate(mats):
                    target[2 * SENT + i] = edge[which, side, own - 5 * side]

    @pl.when(odd)
    def _():
        send(1)

    @pl.when(jnp.logical_not(odd))
    def _():
        send(0)


def pack(meta, state, lam, mu, buoy, receivers):
    hbm = pl.BlockSpec(memory_space=pltpu.HBM)
    is_forward = receivers is None
    big = jax.ShapeDtypeStruct((2 * SENT + (4 if is_forward else 0), 64, 128), jnp.float32)
    out = (big, big) + SLABS
    whole = [pltpu.with_memory_space_constraint(x, pltpu.HBM) for x in (state, lam, mu, buoy)]
    extra, scratch = [], []
    if not is_forward:
        extra = list(receivers)
        count = extra[0].shape[1]
        scratch = [
            pltpu.VMEM((256, count), jnp.bfloat16),
            pltpu.VMEM((384, count), jnp.bfloat16),
            pltpu.VMEM((2, 256, 128), jnp.float32),
        ]
    return pl.pallas_call(
        functools.partial(pack_kernel, is_forward),
        out_shape=out,
        in_specs=[SMEM_SPEC] + [hbm] * 4 + [VMEM_SPEC] * len(extra),
        out_specs=tuple(VMEM_SPEC for _ in out),
        scratch_shapes=[
            pltpu.VMEM((2, 2, 3, 2, 64 + 2 * PAD, 128), jnp.float32),
            pltpu.VMEM((3, 2, 3, 64, 128), jnp.float32),
            pltpu.SemaphoreType.DMA((2, 9)),
            pltpu.SemaphoreType.DMA((3, 2)),
        ]
        + scratch,
        compiler_params=pltpu.CompilerParams(vmem_limit_bytes=5 << 20),
        name="pack_forward" if is_forward else "pack_adjoint",
    )(meta, *whole, *extra)


def first_plane(meta, even, odd):
    return OWN + even + lax.rem(meta[0], 2) * (odd - even)


def load_mats(lam, mu, buoy, mats):
    def own(p):
        for i, array in enumerate((buoy, lam, mu)):
            mats[i, p + OWN] = SCALES[i] * array[p]

    planes(0, 8, own)


def load_halo(ref, rightward, w_both, mats):
    for shot in range(2):
        for i, (field, slot, _) in enumerate(RIGHTWARD if rightward else LEFTWARD):
            w_both[field][shot, slot, pl.ds(PAD, 64), :] = ref[SENT * shot + i]
    if mats is not None:
        for i, (which, _, slot) in enumerate(MATS_RIGHTWARD if rightward else MATS_LEFTWARD):
            mats[which, slot] = SCALES[which] * ref[2 * SENT + i]


def load_chip_halo(meta, ref, w_both, mats):
    odd = lax.rem(meta[0], 2) == 1

    @pl.when(odd)
    def _():
        load_halo(ref, True, w_both, mats)

    @pl.when(jnp.logical_not(odd))
    def _():
        load_halo(ref, False, w_both, mats)


def load_cross_halo(meta, ref, w_both, mats):
    odd = lax.rem(meta[0], 2) == 1

    @pl.when(odd)
    def _():
        load_halo(ref, False, w_both, mats)

    @pl.when(jnp.logical_not(odd))
    def _():
        load_halo(ref, True, w_both, mats)


NEAR = ((1, 0, 8), (8, -1, 1), (1, 0, 7), (2, -1, 8), (8, -1, 1), (2, 0, 6), (3, 0, 6), (3, 0, 5))
FAR = ((0, 8, 1), (-1, 8, 1), (0, 7, 1), (-1, 7, 3), (-1, 8, 1), (0, 6, 2), (0, 6, 3), (0, 5, 3))
NEAR_SOURCES = ((1, -2, 9), (2, -1, 7))
FAR_SOURCES = ((-2, 7, 3), (-1, 6, 3))


def forward_passes(meta, src_index, src_amp, w_both, mats, strains, passes, sources):
    kb = lambda q, flat: mats[0, q, flat, :]
    slabs = [of_shot(w_both, shot) for shot in range(2)]

    def own(moment, stress, q):
        for shot, u in enumerate(slabs):
            for begin in range(0, 64, CHUNK):
                strain = strain_chunk(u, q, begin)
                for i, value in enumerate(strain):
                    strains[shot, moment, i, q - OWN, pl.ds(begin, CHUNK), :] = value
                if stress:
                    stress_chunk(u, mats, q, begin, strain)

    def outer(q):
        for u in slabs:
            for begin in range(0, 64, CHUNK):
                stress_chunk(u, mats, q, begin, strain_chunk(u, q, begin))

    def velocity(q):
        for u in slabs:
            velocity_plane(u, kb, q)

    def run(i, body):
        even, odd, count = passes[i]
        planes(first_plane(meta, even, odd), count, body)

    def source(moment):
        even, odd, count = sources[moment]
        low = first_plane(meta, even, odd)
        for shot, u in enumerate(slabs):
            cell = src_index[shot]
            slot = lax.shift_right_logical(cell, 13) - 8 * meta[0] + OWN
            row = jnp.bitwise_and(lax.shift_right_logical(cell, 7), 63) + PAD
            lane = jnp.bitwise_and(cell, 127)

            @pl.when(jnp.logical_and(slot >= low, slot < low + count))
            def _():
                amount = jnp.where(lanes(1) == lane, src_amp[shot, moment], 0.0)
                for field in (SXX, SYY, SZZ):
                    u[field][slot, pl.ds(row, 1), :] += amount

    run(0, velocity)
    run(1, outer)
    run(2, functools.partial(own, 0, True))
    source(0)
    run(3, velocity)
    run(4, outer)
    run(5, functools.partial(own, 1, True))
    source(1)
    run(6, velocity)
    run(7, functools.partial(own, 2, False))


def forward_near_kernel(meta, src_index, src_amp, lam, mu, buoy, chip, *rest):
    strains, mats, *w_both = rest[9:]
    load_mats(lam, mu, buoy, mats)
    load_chip_halo(meta, chip, w_both, mats)
    forward_passes(meta, src_index, src_amp, w_both, mats, strains, NEAR, NEAR_SOURCES)


def forward_far_kernel(meta, src_index, src_amp, cross, *rest):
    strains, mats, *w_both = rest[11:]
    load_cross_halo(meta, cross, w_both, mats)
    forward_passes(meta, src_index, src_amp, w_both, mats, strains, FAR, FAR_SOURCES)


def call(kernel, name, operands, out_shape, scalars, aliases=None):
    return pl.pallas_call(
        kernel,
        out_shape=out_shape,
        in_specs=[SMEM_SPEC] * scalars + [VMEM_SPEC] * (len(operands) - scalars),
        out_specs=tuple(VMEM_SPEC for _ in out_shape),
        input_output_aliases=aliases or {},
        compiler_params=pltpu.CompilerParams(vmem_limit_bytes=4 << 20),
        name=name,
    )(*operands)


def forward_near(meta, src_index, src_amp, lam, mu, buoy, chip, slabs):
    operands = (meta, src_index, src_amp, lam, mu, buoy, chip) + tuple(slabs)
    aliases = {7 + i: 2 + i for i in range(9)}
    return call(forward_near_kernel, "forward_near", operands, (STRAINS, MATS) + SLABS, 3, aliases)


def forward_far(meta, src_index, src_amp, cross, held):
    operands = (meta, src_index, src_amp, cross) + tuple(held)
    aliases = {4 + i: i for i in range(11)}
    return call(forward_far_kernel, "forward_far", operands, (STRAINS, MATS) + SLABS, 3, aliases)


def split_values(amounts, shot, cell, moments, values):
    count = cell.shape[1]
    lane = jnp.bitwise_and(cell, 127)
    lane_hot = lax.broadcasted_iota(jnp.int32, (128, count), 0) == lane
    for i, moment in enumerate(moments):
        left = amounts[moment, pl.ds(shot, 1), :]
        for part in range(3):
            piece = left.astype(jnp.bfloat16).astype(jnp.float32)
            left = left - piece
            values[pl.ds(128 * (len(moments) * part + i), 128), :] = jnp.where(
                lane_hot, piece, 0.0
            ).astype(jnp.bfloat16)


def rows_of(cell, base, first, count):
    row = lax.shift_right_logical(cell, 7) - base
    at = first + lax.broadcasted_iota(jnp.int32, (count, cell.shape[1]), 0)
    return jnp.where(at == row, 1.0, 0.0).astype(jnp.bfloat16)


def gathered(hot, values, moments):
    product = lax.dot_general(
        hot, values, (((1,), (1,)), ((), ())), preferred_element_type=jnp.float32
    )
    size = 128 * moments
    return product[:, :size] + product[:, size : 2 * size] + product[:, 2 * size :]


INJECT_FIRST = 2 * 64
INJECT_ROWS = 11 * 64


def inject_kernel(meta, cells, amounts, out, rows_hot, values):
    base = (8 * meta[0] - OWN) * 64
    for shot in range(2):
        cell = cells[pl.ds(shot, 1), :]

        def hot(k, carry):
            rows_hot[pl.ds(k * 64, 64), :] = rows_of(cell, base, INJECT_FIRST + k * 64, 64)
            return carry

        lax.fori_loop(0, INJECT_ROWS // 64, hot, 0)
        split_values(amounts, shot, cell, (0, 1, 2), values)
        size = INJECT_ROWS // 2
        for k in range(2):
            total = gathered(rows_hot[pl.ds(k * size, size), :], values[...], 3)
            for moment in range(3):
                out[shot, moment, pl.ds(INJECT_FIRST + k * size, size), :] = total[
                    :, 128 * moment : 128 * moment + 128
                ]


def inject(meta, cells, amounts):
    count = cells.shape[1]
    vmem = pl.BlockSpec(memory_space=pltpu.VMEM)
    return pl.pallas_call(
        inject_kernel,
        out_shape=jax.ShapeDtypeStruct((2, 3, SLOTS * 64, 128), jnp.float32),
        in_specs=[pl.BlockSpec(memory_space=pltpu.SMEM), vmem, vmem],
        out_specs=vmem,
        scratch_shapes=[
            pltpu.VMEM((INJECT_ROWS, count), jnp.bfloat16),
            pltpu.VMEM((3 * 384, count), jnp.bfloat16),
        ],
        compiler_params=pltpu.CompilerParams(vmem_limit_bytes=12 << 20),
        name="receivers",
    )(meta, cells, amounts)


def adjoint_passes(meta, w_both, mats, strains, dense, grads, passes):
    kb = lambda q, flat: -mats[0, q, flat, :]
    slabs = [of_shot(w_both, shot) for shot in range(2)]

    def own(moment, stress, q):
        p = q - OWN
        for begin in range(0, 64, CHUNK):
            flat = pl.ds(begin, CHUNK)
            if moment < 2:
                bulk, shear = grads[0, p, flat, :], grads[1, p, flat, :]
            else:
                bulk, shear = 0.0, 0.0
            for shot, w in enumerate(slabs):
                exx, eyy, ezz, eyz, exz, exy = strain_chunk(w, q, begin)
                fxx, fyy, fzz, fyz, fxz, fxy = [
                    strains[shot, moment, i, p, flat, :] for i in range(6)
                ]
                bulk = bulk + (fxx + fyy + fzz) * (exx + eyy + ezz)
                shear = shear + (
                    2.0 * (fxx * exx + fyy * eyy + fzz * ezz)
                    + (fyz * eyz + fxz * exz + fxy * exy)
                )
                if stress:
                    stress_chunk(w, mats, q, begin, (exx, eyy, ezz, eyz, exz, exy), -1.0)
            grads[0, p, flat, :] = bulk
            grads[1, p, flat, :] = shear

    def outer(q):
        for w in slabs:
            for begin in range(0, 64, CHUNK):
                stress_chunk(w, mats, q, begin, strain_chunk(w, q, begin), -1.0)

    def velocity(moment, q):
        for shot, w in enumerate(slabs):
            velocity_plane(w, kb, q, dense.at[shot, moment])

    def run(i, body):
        even, odd, count = passes[i]
        planes(first_plane(meta, even, odd), count, body)

    run(0, functools.partial(velocity, 2))
    run(1, outer)
    run(2, functools.partial(own, 2, True))
    run(3, functools.partial(velocity, 1))
    run(4, outer)
    run(5, functools.partial(own, 1, True))
    run(6, functools.partial(velocity, 0))
    run(7, functools.partial(own, 0, False))


def give_away(meta, grads, give, passes):
    even, odd, count = passes[7]
    low = first_plane(meta, even, odd) - OWN
    rows = pl.ds(pl.multiple_of(32 - 32 * meta[1], 32), 32)
    for i in range(2):
        for j in range(count):
            give[i, j] = grads[i, low + j, rows, :]


def adjoint_near_kernel(meta, mats, chip, strains, dense, *rest):
    give, grads, *w_both = rest[9:]
    load_chip_halo(meta, chip, w_both, None)
    adjoint_passes(meta, w_both, mats, strains, dense, grads, NEAR)
    give_away(meta, grads, give, NEAR)


def adjoint_far_kernel(meta, cross, mats, strains, dense, *rest):
    give, grads, *w_both = rest[10:]
    load_cross_halo(meta, cross, w_both, None)
    adjoint_passes(meta, w_both, mats, strains, dense, grads, FAR)
    give_away(meta, grads, give, FAR)


def gift(passes):
    return jax.ShapeDtypeStruct((2, passes[7][2], 32, 128), jnp.float32)


def adjoint_near(meta, mats, chip, strains, dense, slabs):
    operands = (meta, mats, chip, strains, dense) + tuple(slabs)
    aliases = {5 + i: 2 + i for i in range(9)}
    out = (gift(NEAR), GRADS) + SLABS
    return call(adjoint_near_kernel, "adjoint_near", operands, out, 1, aliases)


def adjoint_far(meta, cross, mats, strains, dense, held):
    operands = (meta, cross, mats, strains, dense) + tuple(held)
    aliases = {5 + i: 1 + i for i in range(10)}
    out = (gift(FAR), GRADS) + SLABS
    return call(adjoint_far_kernel, "adjoint_far", operands, out, 1, aliases)


def finish_kernel(meta, grads, near, far, out_lambda, out_shear):
    rows = pl.ds(pl.multiple_of(32 * meta[1], 32), 32)
    for ref, passes in ((near, NEAR), (far, FAR)):
        even, odd, count = passes[7]
        low = first_plane(meta, even, odd) - OWN
        for i, out in enumerate((out_lambda, out_shear)):
            for j in range(count):
                out[low + j] = grads[i, low + j, rows, :] + ref[i, j]


def finish(meta, grads, near, far):
    out = jax.ShapeDtypeStruct((8, 32, 128), jnp.float32)
    return call(finish_kernel, "finish", (meta, grads, near, far), (out, out), 1)


def shards(
    lame_lambda, lame_shear, buoyancy, fwd_state, adj_state, src_index, src_amp, recv_index, residual
):
    count = lax.axis_size("space")
    onchip = [(i, i + 1) for i in range(0, count, 2)] + [(i + 1, i) for i in range(0, count, 2)]
    between = [(i, i + 1) for i in range(1, count - 1, 2)]
    between = between + [(j, i) for i, j in between]
    swap_chips = lambda x: lax.ppermute(x, "space", between)
    swap_cores = lambda x: lax.ppermute(x, "space", onchip)
    meta = jnp.stack([lax.axis_index("space"), lax.axis_index("shot")]).astype(jnp.int32)
    mats = (lame_lambda, lame_shear, buoyancy)
    swap_shots = lambda x: lax.ppermute(x, "shot", [(0, 1), (1, 0)])
    amounts = residual.transpose(1, 0, 2)
    f_cross, f_chip, *f_slabs = pack(meta, fwd_state, *mats, None)
    f_cross = swap_chips(f_cross)
    a_cross, a_chip, *a_slabs = pack(meta, adj_state, *mats, (recv_index, amounts))
    a_cross = swap_chips(a_cross)
    f_chip = swap_cores(f_chip)
    dense = inject(meta, recv_index, amounts).reshape(2, 3, SLOTS, 64, 128)
    a_chip = swap_cores(a_chip)
    held = forward_near(meta, src_index, src_amp, *mats, f_chip, f_slabs)
    strains, scaled, *_ = forward_far(meta, src_index, src_amp, f_cross, held)
    near, *held = adjoint_near(meta, scaled, a_chip, strains, dense, a_slabs)
    near = swap_shots(near)
    far, grads, *_ = adjoint_far(meta, a_cross, scaled, strains, dense, held)
    far = swap_shots(far)
    return tuple(finish(meta, grads, near, far))


def solution(mesh):
    in_specs = (
        P("space", None, None),
        P("space", None, None),
        P("space", None, None),
        P(None, "shot", "space", None, None),
        P(None, "shot", "space", None, None),
        P("shot"),
        P("shot", None),
        P("shot", None),
        P("shot", None, None),
    )
    out_specs = (P("space", "shot", None), P("space", "shot", None))
    return jax.shard_map(shards, mesh=mesh, in_specs=in_specs, out_specs=out_specs, check_vma=False)
```

time: 61.3 us -> 50.9 us (0.83)
  local copies, waits for them, and re-layouts: 5.98 us -> 0.04 us
  starting transfers between devices: 19.4 us -> 13.8 us
  Pallas kernels: 28.2 us -> 31.8 us
  waiting for transfers between devices: 6.46 us -> 4.23 us
    ppermute x3 -> x2, starting transfers between devices: 17.1 us -> 11.4 us  [shards(): swap_chips = lambda x: lax.ppermute(x, 'space', between)]
    pallas_call x5 -> x7, Pallas kernels: 20.8 us -> 26.4 us  [the longest x5 18.1 us: call(): pl.pallas_call(kernel, out_shape=out_shape, in_specs=[SMEM_SPEC] * scalar...]
    unnamed x29 -> x14, local copies, waits for them, and re-layouts: 5.26 us -> 0.04 us
    pallas_call x1, Pallas kernels: 7.42 us -> 5.39 us  [inject(): pl.pallas_call(inject_kernel, out_shape=jax.ShapeDtypeStruct((2, 3, SLOTS...]
    ppermute x3 -> x2, waiting for transfers between devices: 1.71 us -> 0.01 us  [shards(): swap_chips = lambda x: lax.ppermute(x, 'space', between)]
    squeeze x1 -> x0, local copies, waits for them, and re-layouts: 0.72 us -> none  [shards(): return (total[0], total[1])]
    ppermute x1 -> x2, waiting for transfers between devices: 4.75 us -> 4.22 us  [shards(): swap_shots = lambda x: lax.ppermute(x, 'shot', [(0, 1), (1, 0)])]
    ppermute x1 -> x2, starting transfers between devices: 1.7 us -> 2.19 us  [shards(): swap_shots = lambda x: lax.ppermute(x, 'shot', [(0, 1), (1, 0)])]
  transfers between devices with their start and end apart: 6 -> 6, of which waited for: 2 -> 1; matrix products, arithmetic and copies ran while one was open for 0% -> 0% of each run, Pallas kernels for 35% -> 52%
where the time goes in v3:
time: 50.9 us; the launch traced here: 50.7 us
  Pallas kernels  31.8 us (62%)
  starting transfers between devices  13.8 us (27%)
  waiting for transfers between devices  4.23 us (8%)
  between operations  0.84 us (2%)
    pallas_call x5, Pallas kernels, call(): pl.pallas_call(kernel, out_shape=out_shape, in_specs=[SMEM_SPEC] * scalar...  18.1 us
    ppermute x2, starting transfers between devices, shards(): swap_chips = lambda x: lax.ppermute(x, 'space', between)  11.4 us
    pallas_call x2, Pallas kernels, pack(): pl.pallas_call(functools.partial(pack_kernel, is_forward), out_shape=out,...  8.27 us
    pallas_call x1, Pallas kernels, inject(): pl.pallas_call(inject_kernel, out_shape=jax.ShapeDtypeStruct((2, 3, SLOTS...  5.39 us
    ppermute x2, waiting for transfers between devices, shards(): swap_shots = lambda x: lax.ppermute(x, 'shot', [(0, 1), (1, 0)])  4.22 us
    ppermute x2, starting transfers between devices, shards(): swap_shots = lambda x: lax.ppermute(x, 'shot', [(0, 1), (1, 0)])  2.19 us
  transfers between devices with their start and end apart: 6, of which 1 were waited for; matrix products, arithmetic and copies ran while one was open for 0% of the time, Pallas kernels for 52%

profile of v3, /device:TPU:64, one launch (start us, length us, event | category | flops | bytes accessed | tf_op | source)
XLA Modules:
  0.0 50.7 jit_solution(5587302767997553565)
XLA Ops:
  0.6 0.1 pad_add_fusion.meta
  0.7 0.0 copy-start.3
  0.7 0.0 copy-start.4
  0.7 4.0 %pack_forward.1 = (f32[38,64,128]{2,1,0:T(8,128)S(1)}, f32[38,64,128]{2,1,0:T(8,128)S(1)}, f32[2,14,80,128]{3,2,1,0:T(8,128)S(1)}, f32[2,14,80,128]{3,2,1,0:T(8,...) custom-call(s32[2]{0:T(128)S(1)} %pad_add_fusion.meta, ...), custom_call_target="tpu_custom_call" | custom-call | tf_op jit(solution)/shard_map/pack_forward/pallas_call | solution.py:293
  4.8 0.1 collective-permute-start.2
  4.9 6.3 %collective-permute-start.1 = (f32[38,64,128]{2,1,0:T(8,128)S(1)}, f32[38,64,128]{2,1,0:T(8,128)S(1)}, u32[]{:S(2)}, u32[]{:S(2)}) collective-permute-start(f32[38,64,128]{2,1,0:T(8,128)S(1)} %get-tuple-element.51), channel_id=1, source_target_pairs={{1,2},{3,4},{5,6},{7,8},{9,10},{11,12},{13,14},{15,16},{17,18},{19... | collective-permute-start | bytes 3735560 | tf_op jit(solution)/shard_map/ppermute | solution.py:633
  11.2 0.0 copy-done.3
  11.2 0.0 copy-done.4
  11.2 4.2 %pack_adjoint.1 = (f32[34,64,128]{2,1,0:T(8,128)S(1)}, f32[34,64,128]{2,1,0:T(8,128)S(1)}, f32[2,14,80,128]{3,2,1,0:T(8,128)S(1)}, f32[2,14,80,128]{3,2,1,0:T(8,...) custom-call(s32[2]{0:T(128)S(1)} %pad_add_fusion.meta, ...), custom_call_target="tpu_custom_call" | custom-call | tf_op jit(solution)/shard_map/pack_adjoint/pallas_call | solution.py:293
  15.4 0.1 collective-permute-start.3
  15.5 0.0 copy-start
  15.5 0.0 copy-start.1
  15.5 0.0 copy-start.2
  15.5 0.0 copy-start.5
  15.6 0.0 copy-start.6
  15.6 5.1 %collective-permute-start = (f32[34,64,128]{2,1,0:T(8,128)S(1)}, f32[34,64,128]{2,1,0:T(8,128)S(1)}, u32[]{:S(2)}, u32[]{:S(2)}) collective-permute-start(f32[34,64,128]{2,1,0:T(8,128)S(1)} %get-tuple-element.50), channel_id=1, source_target_pairs={{1,2},{3,4},{5,6},{7,8},{9,10},{11,12},{13,14},{15,16},{17,18},{19... | collective-permute-start | bytes 3342344 | tf_op jit(solution)/shard_map/ppermute | solution.py:633
  20.7 5.4 %receivers.1 = f32[2,3,896,128]{3,2,1,0:T(8,128)S(1)} custom-call(s32[2]{0:T(128)S(1)} %pad_add_fusion.meta, s32[2,1024]{1,0:T(2,128)S(1)} %copy-done.4, f32[3,2,1024]{2,1,0:T(2,128)S(1)} %bitcast.7), custom_call_target="tpu_custom_call" | custom-call | tf_op jit(solution)/shard_map/receivers/pallas_call | solution.py:506
  26.1 0.0 collective-permute-done.2.chip
  26.1 0.0 copy-done
  26.1 0.0 copy-done.1
  26.1 0.0 copy-done.2
  26.1 0.0 copy-done.5
  26.1 0.0 copy-done.6
  26.2 5.7 %forward_near.1 = (f32[2,3,6,8,64,128]{5,4,3,2,1,0:T(8,128)S(1)}, f32[3,14,64,128]{3,2,1,0:T(8,128)S(1)}, f32[2,14,80,128]{3,2,1,0:T(8,128)S(1)}, f32[2,14,80,12...) custom-call(s32[2]{0:T(128)S(1)} %pad_add_fusion.meta, ...), custom_call_target="tpu_custom_call", output_to_operand_aliasing={{2}: (7, {}), {3}: (8, {}), {4}: (9, {}), {5}: (10, {}), {6... | custom-call | tf_op jit(solution)/shard_map/forward_near/pallas_call | solution.py:428
  31.9 0.0 collective-permute-done.1.cross
  31.9 2.4 %forward_far.1 = (f32[2,3,6,8,64,128]{5,4,3,2,1,0:T(8,128)S(1)}, f32[3,14,64,128]{3,2,1,0:T(8,128)S(1)}, f32[2,14,80,128]{3,2,1,0:T(8,128)S(1)}, f32[2,14,80,128...) custom-call(s32[2]{0:T(128)S(1)} %pad_add_fusion.meta, ...), custom_call_target="tpu_custom_call", output_to_operand_aliasing={{0}: (4, {}), {1}: (5, {}), {2}: (6, {}), {3}: (7, {}), {4}... | custom-call | tf_op jit(solution)/shard_map/forward_far/pallas_call | solution.py:428
  34.2 0.0 collective-permute-done.3.chip
  34.2 6.3 %adjoint_near.1 = (f32[2,5,32,128]{3,2,1,0:T(8,128)S(1)}, f32[2,8,64,128]{3,2,1,0:T(8,128)S(1)}, f32[2,14,80,128]{3,2,1,0:T(8,128)S(1)}, f32[2,14,80,128]{3,2,1,...) custom-call(s32[2]{0:T(128)S(1)} %pad_add_fusion.meta, ...), custom_call_target="tpu_custom_call", output_to_operand_aliasing={{2}: (5, {}), {3}: (6, {}), {4}: (7, {}), {5}: (8, {}), {6}... | custom-call | tf_op jit(solution)/shard_map/adjoint_near/pallas_call | solution.py:428
  40.6 1.7 %collective-permute-start.4 = (f32[2,5,32,128]{3,2,1,0:T(8,128)S(1)}, f32[2,5,32,128]{3,2,1,0:T(8,128)S(1)}, u32[]{:S(2)}, u32[]{:S(2)}) collective-permute-start(f32[2,5,32,128]{3,2,1,0:T(8,128)S(1)} %get-tuple-element.96), channel_id=1, source_target_pairs={{0,64},{64,0},{1,65},{65,1},{2,66},{66,2},{3,67},{67,3},{4,68},{68... | collective-permute-start | bytes 491528 | tf_op jit(solution)/shard_map/ppermute | solution.py:637
  42.3 0.0 collective-permute-done.cross
  42.3 2.5 %adjoint_far.1 = (f32[2,3,32,128]{3,2,1,0:T(8,128)S(1)}, f32[2,8,64,128]{3,2,1,0:T(8,128)S(1)}, f32[2,14,80,128]{3,2,1,0:T(8,128)S(1)}, f32[2,14,80,128]{3,2,1,0...) custom-call(s32[2]{0:T(128)S(1)} %pad_add_fusion.meta, ...), custom_call_target="tpu_custom_call", output_to_operand_aliasing={{1}: (5, {}), {2}: (6, {}), {3}: (7, {}), {4}: (8, {}), {5}... | custom-call | tf_op jit(solution)/shard_map/adjoint_far/pallas_call | solution.py:428
  44.7 0.5 collective-permute-start.5
  45.2 4.2 %collective-permute-done.5.far = f32[2,3,32,128]{3,2,1,0:T(8,128)S(1)} collective-permute-done((f32[2,3,32,128]{3,2,1,0:T(8,128)S(1)}, f32[2,3,32,128]{3,2,1,0:T(8,128)S(1)}, u32[]{:S(2)}, u32[]{:S(2)}) %collective-permute-start.5) | collective-permute-done | bytes 98336 | tf_op jit(solution)/shard_map/ppermute | solution.py:637
  49.4 0.0 collective-permute-done.4.near
  49.4 1.3 %finish.1 = (f32[8,32,128]{2,1,0:T(8,128)}, f32[8,32,128]{2,1,0:T(8,128)}) custom-call(s32[2]{0:T(128)S(1)} %pad_add_fusion.meta, f32[2,8,64,128]{3,2,1,0:T(8,128)S(1)} %get-tuple-element.95.grads, f32[2,5,32,128]{3,2,1,0:T(8,128)S(1)} %collective-permute-done.4.near, f32[2,3,32,128]{3,2,1,0:T(8,128)S(1)} %collective-permute-done.5.far), custom_call_target="tpu_custom_call" | custom-call | tf_op jit(solution)/shard_map/finish/pallas_call | solution.py:428
Async XLA Ops:
  0.7 10.5 %copy-start.3 = (f32[2,3,1024]{2,0,1:T(2,128)S(1)}, f32[2,3,1024]{2,0,1:T(2,128)}, u32[]{:S(2)}) copy-start(f32[2,3,1024]{2,0,1:T(2,128)} %param.17) | copy-start | bytes 73732
  0.7 10.5 %copy-start.4 = (s32[2,1024]{1,0:T(2,128)S(1)}, s32[2,1024]{1,0:T(2,128)}, u32[]{:S(2)}) copy-start(s32[2,1024]{1,0:T(2,128)} %cells.1) | copy-start | bytes 24580
  4.8 21.3 %collective-permute-start.2 = (f32[38,64,128]{2,1,0:T(8,128)S(1)}, f32[38,64,128]{2,1,0:T(8,128)S(1)}, u32[]{:S(2)}, u32[]{:S(2)}) collective-permute-start(f32[38,64,128]{2,1,0:T(8,128)S(1)} %get-tuple-element.52), channel_id=1, source_target_pairs={{0,1},{2,3},{4,5},{6,7},{8,9},{10,11},{12,13},{14,15},{16,17},{18,... | collective-permute-start | bytes 3735560 | tf_op jit(solution)/shard_map/ppermute | solution.py:634
  4.9 27.0 %collective-permute-start.1 = (f32[38,64,128]{2,1,0:T(8,128)S(1)}, f32[38,64,128]{2,1,0:T(8,128)S(1)}, u32[]{:S(2)}, u32[]{:S(2)}) collective-permute-start(f32[38,64,128]{2,1,0:T(8,128)S(1)} %get-tuple-element.51), channel_id=1, source_target_pairs={{1,2},{3,4},{5,6},{7,8},{9,10},{11,12},{13,14},{15,16},{17,18},{19... | collective-permute-start | bytes 3735560 | tf_op jit(solution)/shard_map/ppermute | solution.py:633
  15.4 18.8 %collective-permute-start.3 = (f32[34,64,128]{2,1,0:T(8,128)S(1)}, f32[34,64,128]{2,1,0:T(8,128)S(1)}, u32[]{:S(2)}, u32[]{:S(2)}) collective-permute-start(f32[34,64,128]{2,1,0:T(8,128)S(1)} %get-tuple-element.75), channel_id=1, source_target_pairs={{0,1},{2,3},{4,5},{6,7},{8,9},{10,11},{12,13},{14,15},{16,17},{18,... | collective-permute-start | bytes 3342344 | tf_op jit(solution)/shard_map/ppermute | solution.py:634
  15.5 10.6 %copy-start = (f32[8,64,128]{2,1,0:T(8,128)S(1)}, f32[8,64,128]{2,1,0:T(8,128)}, u32[]{:S(2)}) copy-start(f32[8,64,128]{2,1,0:T(8,128)} %lam.5) | copy-start | bytes 786436
  15.5 10.6 %copy-start.1 = (f32[8,64,128]{2,1,0:T(8,128)S(1)}, f32[8,64,128]{2,1,0:T(8,128)}, u32[]{:S(2)}) copy-start(f32[8,64,128]{2,1,0:T(8,128)} %mu.5) | copy-start | bytes 786436
  15.5 10.6 %copy-start.2 = (f32[8,64,128]{2,1,0:T(8,128)S(1)}, f32[8,64,128]{2,1,0:T(8,128)}, u32[]{:S(2)}) copy-start(f32[8,64,128]{2,1,0:T(8,128)} %buoy.5) | copy-start | bytes 786436
  15.5 10.6 %copy-start.5 = (f32[2,3]{1,0:T(2,128)S(1)}, f32[2,3]{1,0:T(2,128)}, u32[]{:S(2)}) copy-start(f32[2,3]{1,0:T(2,128)} %src_amp.3) | copy-start | bytes 76
  15.6 10.6 %copy-start.6 = (s32[2]{0:T(128)S(1)}, s32[2]{0:T(128)}, u32[]{:S(2)}) copy-start(s32[2]{0:T(128)} %src_index.3) | copy-start | bytes 28
  15.6 26.7 %collective-permute-start = (f32[34,64,128]{2,1,0:T(8,128)S(1)}, f32[34,64,128]{2,1,0:T(8,128)S(1)}, u32[]{:S(2)}, u32[]{:S(2)}) collective-permute-start(f32[34,64,128]{2,1,0:T(8,128)S(1)} %get-tuple-element.50), channel_id=1, source_target_pairs={{1,2},{3,4},{5,6},{7,8},{9,10},{11,12},{13,14},{15,16},{17,18},{19... | collective-permute-start | bytes 3342344 | tf_op jit(solution)/shard_map/ppermute | solution.py:633
  40.6 8.9 %collective-permute-start.4 = (f32[2,5,32,128]{3,2,1,0:T(8,128)S(1)}, f32[2,5,32,128]{3,2,1,0:T(8,128)S(1)}, u32[]{:S(2)}, u32[]{:S(2)}) collective-permute-start(f32[2,5,32,128]{3,2,1,0:T(8,128)S(1)} %get-tuple-element.96), channel_id=1, source_target_pairs={{0,64},{64,0},{1,65},{65,1},{2,66},{66,2},{3,67},{67,3},{4,68},{68... | collective-permute-start | bytes 491528 | tf_op jit(solution)/shard_map/ppermute | solution.py:637
  44.7 4.7 %collective-permute-start.5 = (f32[2,3,32,128]{3,2,1,0:T(8,128)S(1)}, f32[2,3,32,128]{3,2,1,0:T(8,128)S(1)}, u32[]{:S(2)}, u32[]{:S(2)}) collective-permute-start(f32[2,3,32,128]{3,2,1,0:T(8,128)S(1)} %get-tuple-element.97), channel_id=1, source_target_pairs={{0,64},{64,0},{1,65},{65,1},{2,66},{66,2},{3,67},{67,3},{4,68},{68... | collective-permute-start | bytes 294920 | tf_op jit(solution)/shard_map/ppermute | solution.py:637

commit v4 on v3

--- a/solution.py
+++ b/solution.py
@@ -115,7 +115,7 @@
         w[field][q, at, :] = old + change if sign > 0 else old - change
 
 
-UNROLL = 2
+UNROLL = 4
 
 
 def planes(low, count, body):
@@ -478,26 +478,98 @@
 
 INJECT_FIRST = 2 * 64
 INJECT_ROWS = 11 * 64
-
-
-def inject_kernel(meta, cells, amounts, out, rows_hot, values):
+GROUP = 128
+
+
+def ordinal(inside):
+    groups = inside.shape[1] // 128
+    rows = jnp.concatenate([inside[:, 128 * i : 128 * i + 128] for i in range(groups)], axis=0)
+    upper = lax.broadcasted_iota(jnp.int32, (128, 128), 0) <= lax.broadcasted_iota(
+        jnp.int32, (128, 128), 1
+    )
+    within = jnp.dot(
+        rows.astype(jnp.bfloat16),
+        jnp.where(upper, 1.0, 0.0).astype(jnp.bfloat16),
+        preferred_element_type=jnp.float32,
+    )
+    result = []
+    total = jnp.zeros((1, 1), jnp.float32)
+    for i in range(groups):
+        row = within[i : i + 1, :] + total
+        result.append(row)
+        total = row[:, 127:128]
+    return jnp.concatenate(result, axis=1)
+
+
+def inject_kernel(meta, cells, amounts, out, data, rank_ref, sizes):
     base = (8 * meta[0] - OWN) * 64
+    dims = (((1,), (1,)), ((), ()))
+    count = cells.shape[1]
     for shot in range(2):
         cell = cells[pl.ds(shot, 1), :]
-
-        def hot(k, carry):
-            rows_hot[pl.ds(k * 64, 64), :] = rows_of(cell, base, INJECT_FIRST + k * 64, 64)
+        row = lax.shift_right_logical(cell, 7) - base - INJECT_FIRST
+        inside = jnp.logical_and(row >= 0, row < INJECT_ROWS)
+        rank = ordinal(jnp.where(inside, 1.0, 0.0))
+        rank_ref[pl.ds(shot, 1), :] = jnp.where(inside, rank, 0.0)
+        sizes[shot] = rank[0, count - 1].astype(jnp.int32)
+        row = jnp.where(inside, row, 0)
+        parts = [
+            lax.shift_right_logical(row, 4).astype(jnp.float32),
+            jnp.bitwise_and(row, 15).astype(jnp.float32),
+            jnp.bitwise_and(cell, 127).astype(jnp.float32),
+        ]
+        for moment in range(3):
+            left = amounts[moment, pl.ds(shot, 1), :]
+            for part in range(3):
+                piece = left.astype(jnp.bfloat16).astype(jnp.float32)
+                left = left - piece
+                parts.append(piece)
+        parts = parts + [jnp.zeros_like(parts[0])] * 4
+        data[shot] = jnp.concatenate(parts, axis=0).astype(jnp.bfloat16)
+
+    for shot in range(2):
+
+        def group(k, carry, first=False):
+            wanted = GROUP * k + 1 + lax.broadcasted_iota(jnp.int32, (GROUP, count), 0)
+            chosen = wanted.astype(jnp.float32) == rank_ref[pl.ds(shot, 1), :]
+            few = lax.dot_general(
+                data[shot],
+                jnp.where(chosen, 1.0, 0.0).astype(jnp.bfloat16),
+                dims,
+                preferred_element_type=jnp.float32,
+            )
+            used = GROUP * k + lax.broadcasted_iota(jnp.int32, (1, GROUP), 1) < sizes[shot]
+            row = jnp.where(used, 16.0 * few[0:1, :] + few[1:2, :], -1.0).astype(jnp.int32)
+            lane = few[2:3, :].astype(jnp.int32)
+            lane_hot = lax.broadcasted_iota(jnp.int32, (128, GROUP), 0) == lane
+            values = jnp.concatenate(
+                [
+                    jnp.where(lane_hot, few[3 + 3 * moment + part : 4 + 3 * moment + part, :], 0.0)
+                    for part in range(3)
+                    for moment in range(3)
+                ],
+                axis=0,
+            ).astype(jnp.bfloat16)
+            size = INJECT_ROWS // 2
+            for i in range(2):
+                at = i * size + lax.broadcasted_iota(jnp.int32, (size, GROUP), 0)
+                total = gathered(
+                    jnp.where(at == row, 1.0, 0.0).astype(jnp.bfloat16), values, 3
+                )
+                place = pl.ds(INJECT_FIRST + i * size, size)
+                for moment in range(3):
+                    part = total[:, 128 * moment : 128 * moment + 128]
+
+                    if first:
+                        out[shot, moment, place, :] = part
+                    else:
+                        out[shot, moment, place, :] += part
+
             return carry
 
-        lax.fori_loop(0, INJECT_ROWS // 64, hot, 0)
-        split_values(amounts, shot, cell, (0, 1, 2), values)
-        size = INJECT_ROWS // 2
-        for k in range(2):
-            total = gathered(rows_hot[pl.ds(k * size, size), :], values[...], 3)
-            for moment in range(3):
-                out[shot, moment, pl.ds(INJECT_FIRST + k * size, size), :] = total[
-                    :, 128 * moment : 128 * moment + 128
-                ]
+        groups = lax.div(sizes[shot] + GROUP - 1, GROUP)
+        group(0, 0, True)
+        lax.fori_loop(1, groups, group, 0)
 
 
 def inject(meta, cells, amounts):
@@ -509,8 +581,9 @@
         in_specs=[pl.BlockSpec(memory_space=pltpu.SMEM), vmem, vmem],
         out_specs=vmem,
         scratch_shapes=[
-            pltpu.VMEM((INJECT_ROWS, count), jnp.bfloat16),
-            pltpu.VMEM((3 * 384, count), jnp.bfloat16),
+            pltpu.VMEM((2, 16, count), jnp.bfloat16),
+            pltpu.VMEM((2, count), jnp.float32),
+            pltpu.SMEM((2,), jnp.int32),
         ],
         compiler_params=pltpu.CompilerParams(vmem_limit_bytes=12 << 20),
         name="receivers",

time: 50.9 us -> 50.2 us (0.986); the launches traced: 50.7 us -> 49.3 us
  Pallas kernels: 31.8 us -> 28.1 us
  starting transfers between devices: 13.8 us -> 15 us
  waiting for transfers between devices: 4.23 us -> 5.24 us
    pallas_call x1, Pallas kernels: 5.39 us -> 3.05 us  [inject(): pl.pallas_call(inject_kernel, out_shape=jax.ShapeDtypeStruct((2, 3, SLOTS...]
    ppermute x2, waiting for transfers between devices: 0.01 us -> 2.24 us  [shards(): swap_chips = lambda x: lax.ppermute(x, 'space', between)]
    pallas_call x5, Pallas kernels: 18.1 us -> 16.8 us  [call(): pl.pallas_call(kernel, out_shape=out_shape, in_specs=[SMEM_SPEC] * scalar...]
    ppermute x2, waiting for transfers between devices: 4.22 us -> 3 us  [shards(): swap_shots = lambda x: lax.ppermute(x, 'shot', [(0, 1), (1, 0)])]
    ppermute x2, starting transfers between devices: 2.19 us -> 3.4 us  [shards(): swap_shots = lambda x: lax.ppermute(x, 'shot', [(0, 1), (1, 0)])]
  transfers between devices with their start and end apart: 6 -> 6, of which waited for: 1 -> 2; matrix products, arithmetic and copies ran while one was open for 0% -> 0% of each run, Pallas kernels for 52% -> 46%
where the time goes in v4:
time: 50.2 us; the launch traced here: 49.3 us
  Pallas kernels  28.1 us (56%)
  starting transfers between devices  15 us (30%)
  waiting for transfers between devices  5.24 us (10%)
  between operations  0.84 us (2%)
    pallas_call x5, Pallas kernels, call(): pl.pallas_call(kernel, out_shape=out_shape, in_specs=[SMEM_SPEC] * scalar...  16.8 us
    ppermute x2, starting transfers between devices, shards(): swap_chips = lambda x: lax.ppermute(x, 'space', between)  11.4 us
    pallas_call x2, Pallas kernels, pack(): pl.pallas_call(functools.partial(pack_kernel, is_forward), out_shape=out,...  8.27 us
    ppermute x2, starting transfers between devices, shards(): swap_shots = lambda x: lax.ppermute(x, 'shot', [(0, 1), (1, 0)])  3.4 us
    pallas_call x1, Pallas kernels, inject(): pl.pallas_call(inject_kernel, out_shape=jax.ShapeDtypeStruct((2, 3, SLOTS...  3.05 us
    ppermute x2, waiting for transfers between devices, shards(): swap_shots = lambda x: lax.ppermute(x, 'shot', [(0, 1), (1, 0)])  3 us
    ppermute x2, waiting for transfers between devices, shards(): swap_chips = lambda x: lax.ppermute(x, 'space', between)  2.24 us
  transfers between devices with their start and end apart: 6, of which 2 were waited for; matrix products, arithmetic and copies ran while one was open for 0% of the time, Pallas kernels for 46%

profile of v4, /device:TPU:64, one launch (start us, length us, event | category | flops | bytes accessed | tf_op | source)
XLA Modules:
  0.0 49.3 jit_solution(822050046810301918)
XLA Ops:
  0.6 0.1 pad_add_fusion.meta
  0.7 0.0 copy-start.3
  0.7 0.0 copy-start.4
  0.7 4.0 %pack_forward.1 = (f32[38,64,128]{2,1,0:T(8,128)S(1)}, f32[38,64,128]{2,1,0:T(8,128)S(1)}, f32[2,14,80,128]{3,2,1,0:T(8,128)S(1)}, f32[2,14,80,128]{3,2,1,0:T(8,...) custom-call(s32[2]{0:T(128)S(1)} %pad_add_fusion.meta, ...), custom_call_target="tpu_custom_call" | custom-call | tf_op jit(solution)/shard_map/pack_forward/pallas_call | solution.py:293
  4.8 0.1 collective-permute-start.2
  4.9 6.3 %collective-permute-start.1 = (f32[38,64,128]{2,1,0:T(8,128)S(1)}, f32[38,64,128]{2,1,0:T(8,128)S(1)}, u32[]{:S(2)}, u32[]{:S(2)}) collective-permute-start(f32[38,64,128]{2,1,0:T(8,128)S(1)} %get-tuple-element.51), channel_id=1, source_target_pairs={{1,2},{3,4},{5,6},{7,8},{9,10},{11,12},{13,14},{15,16},{17,18},{19... | collective-permute-start | bytes 3735560 | tf_op jit(solution)/shard_map/ppermute | solution.py:706
  11.2 0.0 copy-done.3
  11.2 0.0 copy-done.4
  11.2 4.2 %pack_adjoint.1 = (f32[34,64,128]{2,1,0:T(8,128)S(1)}, f32[34,64,128]{2,1,0:T(8,128)S(1)}, f32[2,14,80,128]{3,2,1,0:T(8,128)S(1)}, f32[2,14,80,128]{3,2,1,0:T(8,...) custom-call(s32[2]{0:T(128)S(1)} %pad_add_fusion.meta, ...), custom_call_target="tpu_custom_call" | custom-call | tf_op jit(solution)/shard_map/pack_adjoint/pallas_call | solution.py:293
  15.4 0.1 collective-permute-start.3
  15.5 0.0 copy-start
  15.5 0.0 copy-start.1
  15.5 0.0 copy-start.2
  15.5 0.0 copy-start.5
  15.6 0.0 copy-start.6
  15.6 5.1 %collective-permute-start = (f32[34,64,128]{2,1,0:T(8,128)S(1)}, f32[34,64,128]{2,1,0:T(8,128)S(1)}, u32[]{:S(2)}, u32[]{:S(2)}) collective-permute-start(f32[34,64,128]{2,1,0:T(8,128)S(1)} %get-tuple-element.50), channel_id=1, source_target_pairs={{1,2},{3,4},{5,6},{7,8},{9,10},{11,12},{13,14},{15,16},{17,18},{19... | collective-permute-start | bytes 3342344 | tf_op jit(solution)/shard_map/ppermute | solution.py:706
  20.7 3.0 %receivers.1 = f32[2,3,896,128]{3,2,1,0:T(8,128)S(1)} custom-call(s32[2]{0:T(128)S(1)} %pad_add_fusion.meta, s32[2,1024]{1,0:T(2,128)S(1)} %copy-done.4, f32[3,2,1024]{2,1,0:T(2,128)S(1)} %bitcast.7), custom_call_target="tpu_custom_call" | custom-call | tf_op jit(solution)/shard_map/receivers/pallas_call | solution.py:578
  23.8 0.0 collective-permute-done.2.chip
  23.8 0.0 copy-done
  23.8 0.0 copy-done.1
  23.8 0.0 copy-done.2
  23.8 0.0 copy-done.5
  23.8 0.0 copy-done.6
  23.8 5.1 %forward_near.1 = (f32[2,3,6,8,64,128]{5,4,3,2,1,0:T(8,128)S(1)}, f32[3,14,64,128]{3,2,1,0:T(8,128)S(1)}, f32[2,14,80,128]{3,2,1,0:T(8,128)S(1)}, f32[2,14,80,12...) custom-call(s32[2]{0:T(128)S(1)} %pad_add_fusion.meta, ...), custom_call_target="tpu_custom_call", output_to_operand_aliasing={{2}: (7, {}), {3}: (8, {}), {4}: (9, {}), {5}: (10, {}), {6... | custom-call | tf_op jit(solution)/shard_map/forward_near/pallas_call | solution.py:428
  28.9 0.0 collective-permute-done.1.cross
  28.9 2.5 %forward_far.1 = (f32[2,3,6,8,64,128]{5,4,3,2,1,0:T(8,128)S(1)}, f32[3,14,64,128]{3,2,1,0:T(8,128)S(1)}, f32[2,14,80,128]{3,2,1,0:T(8,128)S(1)}, f32[2,14,80,128...) custom-call(s32[2]{0:T(128)S(1)} %pad_add_fusion.meta, ...), custom_call_target="tpu_custom_call", output_to_operand_aliasing={{0}: (4, {}), {1}: (5, {}), {2}: (6, {}), {3}: (7, {}), {4}... | custom-call | tf_op jit(solution)/shard_map/forward_far/pallas_call | solution.py:428
  31.5 0.0 collective-permute-done.3.chip
  31.5 5.4 %adjoint_near.1 = (f32[2,5,32,128]{3,2,1,0:T(8,128)S(1)}, f32[2,8,64,128]{3,2,1,0:T(8,128)S(1)}, f32[2,14,80,128]{3,2,1,0:T(8,128)S(1)}, f32[2,14,80,128]{3,2,1,...) custom-call(s32[2]{0:T(128)S(1)} %pad_add_fusion.meta, ...), custom_call_target="tpu_custom_call", output_to_operand_aliasing={{2}: (5, {}), {3}: (6, {}), {4}: (7, {}), {5}: (8, {}), {6}... | custom-call | tf_op jit(solution)/shard_map/adjoint_near/pallas_call | solution.py:428
  36.9 1.7 %collective-permute-start.4 = (f32[2,5,32,128]{3,2,1,0:T(8,128)S(1)}, f32[2,5,32,128]{3,2,1,0:T(8,128)S(1)}, u32[]{:S(2)}, u32[]{:S(2)}) collective-permute-start(f32[2,5,32,128]{3,2,1,0:T(8,128)S(1)} %get-tuple-element.96), channel_id=1, source_target_pairs={{0,64},{64,0},{1,65},{65,1},{2,66},{66,2},{3,67},{67,3},{4,68},{68... | collective-permute-start | bytes 491528 | tf_op jit(solution)/shard_map/ppermute | solution.py:710
  38.6 2.2 %collective-permute-done.cross = f32[34,64,128]{2,1,0:T(8,128)S(1)} collective-permute-done((f32[34,64,128]{2,1,0:T(8,128)S(1)}, f32[34,64,128]{2,1,0:T(8,128)S(1)}, u32[]{:S(2)}, u32[]{:S(2)}) %collective-permute-start) | collective-permute-done | bytes 1114144 | tf_op jit(solution)/shard_map/ppermute | solution.py:706
  40.9 2.5 %adjoint_far.1 = (f32[2,3,32,128]{3,2,1,0:T(8,128)S(1)}, f32[2,8,64,128]{3,2,1,0:T(8,128)S(1)}, f32[2,14,80,128]{3,2,1,0:T(8,128)S(1)}, f32[2,14,80,128]{3,2,1,0...) custom-call(s32[2]{0:T(128)S(1)} %pad_add_fusion.meta, ...), custom_call_target="tpu_custom_call", output_to_operand_aliasing={{1}: (5, {}), {2}: (6, {}), {3}: (7, {}), {4}: (8, {}), {5}... | custom-call | tf_op jit(solution)/shard_map/adjoint_far/pallas_call | solution.py:428
  43.3 1.7 %collective-permute-start.5 = (f32[2,3,32,128]{3,2,1,0:T(8,128)S(1)}, f32[2,3,32,128]{3,2,1,0:T(8,128)S(1)}, u32[]{:S(2)}, u32[]{:S(2)}) collective-permute-start(f32[2,3,32,128]{3,2,1,0:T(8,128)S(1)} %get-tuple-element.97), channel_id=1, source_target_pairs={{0,64},{64,0},{1,65},{65,1},{2,66},{66,2},{3,67},{67,3},{4,68},{68... | collective-permute-start | bytes 294920 | tf_op jit(solution)/shard_map/ppermute | solution.py:710
  45.0 3.0 %collective-permute-done.5.far = f32[2,3,32,128]{3,2,1,0:T(8,128)S(1)} collective-permute-done((f32[2,3,32,128]{3,2,1,0:T(8,128)S(1)}, f32[2,3,32,128]{3,2,1,0:T(8,128)S(1)}, u32[]{:S(2)}, u32[]{:S(2)}) %collective-permute-start.5) | collective-permute-done | bytes 98336 | tf_op jit(solution)/shard_map/ppermute | solution.py:710
  48.0 0.0 collective-permute-done.4.near
  48.0 1.3 %finish.1 = (f32[8,32,128]{2,1,0:T(8,128)}, f32[8,32,128]{2,1,0:T(8,128)}) custom-call(s32[2]{0:T(128)S(1)} %pad_add_fusion.meta, f32[2,8,64,128]{3,2,1,0:T(8,128)S(1)} %get-tuple-element.95.grads, f32[2,5,32,128]{3,2,1,0:T(8,128)S(1)} %collective-permute-done.4.near, f32[2,3,32,128]{3,2,1,0:T(8,128)S(1)} %collective-permute-done.5.far), custom_call_target="tpu_custom_call" | custom-call | tf_op jit(solution)/shard_map/finish/pallas_call | solution.py:428
Async XLA Ops:
  0.7 10.5 %copy-start.3 = (f32[2,3,1024]{2,0,1:T(2,128)S(1)}, f32[2,3,1024]{2,0,1:T(2,128)}, u32[]{:S(2)}) copy-start(f32[2,3,1024]{2,0,1:T(2,128)} %param.17) | copy-start | bytes 73732
  0.7 10.5 %copy-start.4 = (s32[2,1024]{1,0:T(2,128)S(1)}, s32[2,1024]{1,0:T(2,128)}, u32[]{:S(2)}) copy-start(s32[2,1024]{1,0:T(2,128)} %cells.1) | copy-start | bytes 24580
  4.8 19.0 %collective-permute-start.2 = (f32[38,64,128]{2,1,0:T(8,128)S(1)}, f32[38,64,128]{2,1,0:T(8,128)S(1)}, u32[]{:S(2)}, u32[]{:S(2)}) collective-permute-start(f32[38,64,128]{2,1,0:T(8,128)S(1)} %get-tuple-element.52), channel_id=1, source_target_pairs={{0,1},{2,3},{4,5},{6,7},{8,9},{10,11},{12,13},{14,15},{16,17},{18,... | collective-permute-start | bytes 3735560 | tf_op jit(solution)/shard_map/ppermute | solution.py:707
  4.9 24.1 %collective-permute-start.1 = (f32[38,64,128]{2,1,0:T(8,128)S(1)}, f32[38,64,128]{2,1,0:T(8,128)S(1)}, u32[]{:S(2)}, u32[]{:S(2)}) collective-permute-start(f32[38,64,128]{2,1,0:T(8,128)S(1)} %get-tuple-element.51), channel_id=1, source_target_pairs={{1,2},{3,4},{5,6},{7,8},{9,10},{11,12},{13,14},{15,16},{17,18},{19... | collective-permute-start | bytes 3735560 | tf_op jit(solution)/shard_map/ppermute | solution.py:706
  15.4 16.1 %collective-permute-start.3 = (f32[34,64,128]{2,1,0:T(8,128)S(1)}, f32[34,64,128]{2,1,0:T(8,128)S(1)}, u32[]{:S(2)}, u32[]{:S(2)}) collective-permute-start(f32[34,64,128]{2,1,0:T(8,128)S(1)} %get-tuple-element.75), channel_id=1, source_target_pairs={{0,1},{2,3},{4,5},{6,7},{8,9},{10,11},{12,13},{14,15},{16,17},{18,... | collective-permute-start | bytes 3342344 | tf_op jit(solution)/shard_map/ppermute | solution.py:707
  15.5 8.3 %copy-start = (f32[8,64,128]{2,1,0:T(8,128)S(1)}, f32[8,64,128]{2,1,0:T(8,128)}, u32[]{:S(2)}) copy-start(f32[8,64,128]{2,1,0:T(8,128)} %lam.5) | copy-start | bytes 786436
  15.5 8.3 %copy-start.1 = (f32[8,64,128]{2,1,0:T(8,128)S(1)}, f32[8,64,128]{2,1,0:T(8,128)}, u32[]{:S(2)}) copy-start(f32[8,64,128]{2,1,0:T(8,128)} %mu.5) | copy-start | bytes 786436
  15.5 8.3 %copy-start.2 = (f32[8,64,128]{2,1,0:T(8,128)S(1)}, f32[8,64,128]{2,1,0:T(8,128)}, u32[]{:S(2)}) copy-start(f32[8,64,128]{2,1,0:T(8,128)} %buoy.5) | copy-start | bytes 786436
  15.5 8.2 %copy-start.5 = (f32[2,3]{1,0:T(2,128)S(1)}, f32[2,3]{1,0:T(2,128)}, u32[]{:S(2)}) copy-start(f32[2,3]{1,0:T(2,128)} %src_amp.3) | copy-start | bytes 76
  15.6 8.2 %copy-start.6 = (s32[2]{0:T(128)S(1)}, s32[2]{0:T(128)}, u32[]{:S(2)}) copy-start(s32[2]{0:T(128)} %src_index.3) | copy-start | bytes 28
  15.6 25.3 %collective-permute-start = (f32[34,64,128]{2,1,0:T(8,128)S(1)}, f32[34,64,128]{2,1,0:T(8,128)S(1)}, u32[]{:S(2)}, u32[]{:S(2)}) collective-permute-start(f32[34,64,128]{2,1,0:T(8,128)S(1)} %get-tuple-element.50), channel_id=1, source_target_pairs={{1,2},{3,4},{5,6},{7,8},{9,10},{11,12},{13,14},{15,16},{17,18},{19... | collective-permute-start | bytes 3342344 | tf_op jit(solution)/shard_map/ppermute | solution.py:706
  36.9 11.1 %collective-permute-start.4 = (f32[2,5,32,128]{3,2,1,0:T(8,128)S(1)}, f32[2,5,32,128]{3,2,1,0:T(8,128)S(1)}, u32[]{:S(2)}, u32[]{:S(2)}) collective-permute-start(f32[2,5,32,128]{3,2,1,0:T(8,128)S(1)} %get-tuple-element.96), channel_id=1, source_target_pairs={{0,64},{64,0},{1,65},{65,1},{2,66},{66,2},{3,67},{67,3},{4,68},{68... | collective-permute-start | bytes 491528 | tf_op jit(solution)/shard_map/ppermute | solution.py:710
  43.3 4.7 %collective-permute-start.5 = (f32[2,3,32,128]{3,2,1,0:T(8,128)S(1)}, f32[2,3,32,128]{3,2,1,0:T(8,128)S(1)}, u32[]{:S(2)}, u32[]{:S(2)}) collective-permute-start(f32[2,3,32,128]{3,2,1,0:T(8,128)S(1)} %get-tuple-element.97), channel_id=1, source_target_pairs={{0,64},{64,0},{1,65},{65,1},{2,66},{66,2},{3,67},{67,3},{4,68},{68... | collective-permute-start | bytes 294920 | tf_op jit(solution)/shard_map/ppermute | solution.py:710

commit v5 on v4

--- a/solution.py
+++ b/solution.py
@@ -36,7 +36,7 @@
 STRAINS = jax.ShapeDtypeStruct((2, 3, 6, 8, 64, 128), jnp.float32)
 MATS = jax.ShapeDtypeStruct((3, SLOTS, 64, 128), jnp.float32)
 GRADS = jax.ShapeDtypeStruct((2, 8, 64, 128), jnp.float32)
-CHUNK = 16
+CHUNK = 32
 
 
 def of_shot(w, shot):

time: 50.2 us -> 50.2 us (level)
  no operation moved by 1% of the time
where the time goes in v5:
time: 50.2 us; the launch traced here: 49.2 us
  Pallas kernels  28.1 us (56%)
  starting transfers between devices  15 us (30%)
  waiting for transfers between devices  5.23 us (10%)
  between operations  0.84 us (2%)
    pallas_call x5, Pallas kernels, call(): pl.pallas_call(kernel, out_shape=out_shape, in_specs=[SMEM_SPEC] * scalar...  16.8 us
    ppermute x2, starting transfers between devices, shards(): swap_chips = lambda x: lax.ppermute(x, 'space', between)  11.4 us
    pallas_call x2, Pallas kernels, pack(): pl.pallas_call(functools.partial(pack_kernel, is_forward), out_shape=out,...  8.24 us
    ppermute x2, starting transfers between devices, shards(): swap_shots = lambda x: lax.ppermute(x, 'shot', [(0, 1), (1, 0)])  3.41 us
    pallas_call x1, Pallas kernels, inject(): pl.pallas_call(inject_kernel, out_shape=jax.ShapeDtypeStruct((2, 3, SLOTS...  3.05 us
    ppermute x2, waiting for transfers between devices, shards(): swap_shots = lambda x: lax.ppermute(x, 'shot', [(0, 1), (1, 0)])  3 us
    ppermute x2, waiting for transfers between devices, shards(): swap_chips = lambda x: lax.ppermute(x, 'space', between)  2.22 us
  transfers between devices with their start and end apart: 6, of which 2 were waited for; matrix products, arithmetic and copies ran while one was open for 0% of the time, Pallas kernels for 46%

profile of v5, /device:TPU:64, one launch (start us, length us, event | category | flops | bytes accessed | tf_op | source)
XLA Modules:
  0.0 49.2 jit_solution(7766424750981240491)
XLA Ops:
  0.6 0.1 pad_add_fusion.meta
  0.7 0.0 copy-start.3
  0.7 0.0 copy-start.4
  0.7 4.0 %pack_forward.1 = (f32[38,64,128]{2,1,0:T(8,128)S(1)}, f32[38,64,128]{2,1,0:T(8,128)S(1)}, f32[2,14,80,128]{3,2,1,0:T(8,128)S(1)}, f32[2,14,80,128]{3,2,1,0:T(8,...) custom-call(s32[2]{0:T(128)S(1)} %pad_add_fusion.meta, ...), custom_call_target="tpu_custom_call" | custom-call | tf_op jit(solution)/shard_map/pack_forward/pallas_call | solution.py:293
  4.8 0.1 collective-permute-start.2
  4.9 6.3 %collective-permute-start.1 = (f32[38,64,128]{2,1,0:T(8,128)S(1)}, f32[38,64,128]{2,1,0:T(8,128)S(1)}, u32[]{:S(2)}, u32[]{:S(2)}) collective-permute-start(f32[38,64,128]{2,1,0:T(8,128)S(1)} %get-tuple-element.51), channel_id=1, source_target_pairs={{1,2},{3,4},{5,6},{7,8},{9,10},{11,12},{13,14},{15,16},{17,18},{19... | collective-permute-start | bytes 3735560 | tf_op jit(solution)/shard_map/ppermute | solution.py:706
  11.2 0.0 copy-done.3
  11.2 0.0 copy-done.4
  11.2 4.2 %pack_adjoint.1 = (f32[34,64,128]{2,1,0:T(8,128)S(1)}, f32[34,64,128]{2,1,0:T(8,128)S(1)}, f32[2,14,80,128]{3,2,1,0:T(8,128)S(1)}, f32[2,14,80,128]{3,2,1,0:T(8,...) custom-call(s32[2]{0:T(128)S(1)} %pad_add_fusion.meta, ...), custom_call_target="tpu_custom_call" | custom-call | tf_op jit(solution)/shard_map/pack_adjoint/pallas_call | solution.py:293
  15.4 0.1 collective-permute-start.3
  15.5 0.0 copy-start
  15.5 0.0 copy-start.1
  15.5 0.0 copy-start.2
  15.5 0.0 copy-start.5
  15.5 0.0 copy-start.6
  15.5 5.1 %collective-permute-start = (f32[34,64,128]{2,1,0:T(8,128)S(1)}, f32[34,64,128]{2,1,0:T(8,128)S(1)}, u32[]{:S(2)}, u32[]{:S(2)}) collective-permute-start(f32[34,64,128]{2,1,0:T(8,128)S(1)} %get-tuple-element.50), channel_id=1, source_target_pairs={{1,2},{3,4},{5,6},{7,8},{9,10},{11,12},{13,14},{15,16},{17,18},{19... | collective-permute-start | bytes 3342344 | tf_op jit(solution)/shard_map/ppermute | solution.py:706
  20.7 3.0 %receivers.1 = f32[2,3,896,128]{3,2,1,0:T(8,128)S(1)} custom-call(s32[2]{0:T(128)S(1)} %pad_add_fusion.meta, s32[2,1024]{1,0:T(2,128)S(1)} %copy-done.4, f32[3,2,1024]{2,1,0:T(2,128)S(1)} %bitcast.7), custom_call_target="tpu_custom_call" | custom-call | tf_op jit(solution)/shard_map/receivers/pallas_call | solution.py:578
  23.7 0.0 collective-permute-done.2.chip
  23.7 0.0 copy-done
  23.7 0.0 copy-done.1
  23.8 0.0 copy-done.2
  23.8 0.0 copy-done.5
  23.8 0.0 copy-done.6
  23.8 5.1 %forward_near.1 = (f32[2,3,6,8,64,128]{5,4,3,2,1,0:T(8,128)S(1)}, f32[3,14,64,128]{3,2,1,0:T(8,128)S(1)}, f32[2,14,80,128]{3,2,1,0:T(8,128)S(1)}, f32[2,14,80,12...) custom-call(s32[2]{0:T(128)S(1)} %pad_add_fusion.meta, ...), custom_call_target="tpu_custom_call", output_to_operand_aliasing={{2}: (7, {}), {3}: (8, {}), {4}: (9, {}), {5}: (10, {}), {6... | custom-call | tf_op jit(solution)/shard_map/forward_near/pallas_call | solution.py:428
  28.9 0.0 collective-permute-done.1.cross
  28.9 2.5 %forward_far.1 = (f32[2,3,6,8,64,128]{5,4,3,2,1,0:T(8,128)S(1)}, f32[3,14,64,128]{3,2,1,0:T(8,128)S(1)}, f32[2,14,80,128]{3,2,1,0:T(8,128)S(1)}, f32[2,14,80,128...) custom-call(s32[2]{0:T(128)S(1)} %pad_add_fusion.meta, ...), custom_call_target="tpu_custom_call", output_to_operand_aliasing={{0}: (4, {}), {1}: (5, {}), {2}: (6, {}), {3}: (7, {}), {4}... | custom-call | tf_op jit(solution)/shard_map/forward_far/pallas_call | solution.py:428
  31.4 0.0 collective-permute-done.3.chip
  31.4 5.5 %adjoint_near.1 = (f32[2,5,32,128]{3,2,1,0:T(8,128)S(1)}, f32[2,8,64,128]{3,2,1,0:T(8,128)S(1)}, f32[2,14,80,128]{3,2,1,0:T(8,128)S(1)}, f32[2,14,80,128]{3,2,1,...) custom-call(s32[2]{0:T(128)S(1)} %pad_add_fusion.meta, ...), custom_call_target="tpu_custom_call", output_to_operand_aliasing={{2}: (5, {}), {3}: (6, {}), {4}: (7, {}), {5}: (8, {}), {6}... | custom-call | tf_op jit(solution)/shard_map/adjoint_near/pallas_call | solution.py:428
  36.9 1.7 %collective-permute-start.4 = (f32[2,5,32,128]{3,2,1,0:T(8,128)S(1)}, f32[2,5,32,128]{3,2,1,0:T(8,128)S(1)}, u32[]{:S(2)}, u32[]{:S(2)}) collective-permute-start(f32[2,5,32,128]{3,2,1,0:T(8,128)S(1)} %get-tuple-element.96), channel_id=1, source_target_pairs={{0,64},{64,0},{1,65},{65,1},{2,66},{66,2},{3,67},{67,3},{4,68},{68... | collective-permute-start | bytes 491528 | tf_op jit(solution)/shard_map/ppermute | solution.py:710
  38.6 2.2 %collective-permute-done.cross = f32[34,64,128]{2,1,0:T(8,128)S(1)} collective-permute-done((f32[34,64,128]{2,1,0:T(8,128)S(1)}, f32[34,64,128]{2,1,0:T(8,128)S(1)}, u32[]{:S(2)}, u32[]{:S(2)}) %collective-permute-start) | collective-permute-done | bytes 1114144 | tf_op jit(solution)/shard_map/ppermute | solution.py:706
  40.8 2.4 %adjoint_far.1 = (f32[2,3,32,128]{3,2,1,0:T(8,128)S(1)}, f32[2,8,64,128]{3,2,1,0:T(8,128)S(1)}, f32[2,14,80,128]{3,2,1,0:T(8,128)S(1)}, f32[2,14,80,128]{3,2,1,0...) custom-call(s32[2]{0:T(128)S(1)} %pad_add_fusion.meta, ...), custom_call_target="tpu_custom_call", output_to_operand_aliasing={{1}: (5, {}), {2}: (6, {}), {3}: (7, {}), {4}: (8, {}), {5}... | custom-call | tf_op jit(solution)/shard_map/adjoint_far/pallas_call | solution.py:428
  43.3 1.7 %collective-permute-start.5 = (f32[2,3,32,128]{3,2,1,0:T(8,128)S(1)}, f32[2,3,32,128]{3,2,1,0:T(8,128)S(1)}, u32[]{:S(2)}, u32[]{:S(2)}) collective-permute-start(f32[2,3,32,128]{3,2,1,0:T(8,128)S(1)} %get-tuple-element.97), channel_id=1, source_target_pairs={{0,64},{64,0},{1,65},{65,1},{2,66},{66,2},{3,67},{67,3},{4,68},{68... | collective-permute-start | bytes 294920 | tf_op jit(solution)/shard_map/ppermute | solution.py:710
  45.0 3.0 %collective-permute-done.5.far = f32[2,3,32,128]{3,2,1,0:T(8,128)S(1)} collective-permute-done((f32[2,3,32,128]{3,2,1,0:T(8,128)S(1)}, f32[2,3,32,128]{3,2,1,0:T(8,128)S(1)}, u32[]{:S(2)}, u32[]{:S(2)}) %collective-permute-start.5) | collective-permute-done | bytes 98336 | tf_op jit(solution)/shard_map/ppermute | solution.py:710
  48.0 0.0 collective-permute-done.4.near
  48.0 1.3 %finish.1 = (f32[8,32,128]{2,1,0:T(8,128)}, f32[8,32,128]{2,1,0:T(8,128)}) custom-call(s32[2]{0:T(128)S(1)} %pad_add_fusion.meta, f32[2,8,64,128]{3,2,1,0:T(8,128)S(1)} %get-tuple-element.95.grads, f32[2,5,32,128]{3,2,1,0:T(8,128)S(1)} %collective-permute-done.4.near, f32[2,3,32,128]{3,2,1,0:T(8,128)S(1)} %collective-permute-done.5.far), custom_call_target="tpu_custom_call" | custom-call | tf_op jit(solution)/shard_map/finish/pallas_call | solution.py:428
Async XLA Ops:
  0.7 10.4 %copy-start.3 = (f32[2,3,1024]{2,0,1:T(2,128)S(1)}, f32[2,3,1024]{2,0,1:T(2,128)}, u32[]{:S(2)}) copy-start(f32[2,3,1024]{2,0,1:T(2,128)} %param.17) | copy-start | bytes 73732
  0.7 10.5 %copy-start.4 = (s32[2,1024]{1,0:T(2,128)S(1)}, s32[2,1024]{1,0:T(2,128)}, u32[]{:S(2)}) copy-start(s32[2,1024]{1,0:T(2,128)} %cells.1) | copy-start | bytes 24580
  4.8 19.0 %collective-permute-start.2 = (f32[38,64,128]{2,1,0:T(8,128)S(1)}, f32[38,64,128]{2,1,0:T(8,128)S(1)}, u32[]{:S(2)}, u32[]{:S(2)}) collective-permute-start(f32[38,64,128]{2,1,0:T(8,128)S(1)} %get-tuple-element.52), channel_id=1, source_target_pairs={{0,1},{2,3},{4,5},{6,7},{8,9},{10,11},{12,13},{14,15},{16,17},{18,... | collective-permute-start | bytes 3735560 | tf_op jit(solution)/shard_map/ppermute | solution.py:707
  4.9 24.1 %collective-permute-start.1 = (f32[38,64,128]{2,1,0:T(8,128)S(1)}, f32[38,64,128]{2,1,0:T(8,128)S(1)}, u32[]{:S(2)}, u32[]{:S(2)}) collective-permute-start(f32[38,64,128]{2,1,0:T(8,128)S(1)} %get-tuple-element.51), channel_id=1, source_target_pairs={{1,2},{3,4},{5,6},{7,8},{9,10},{11,12},{13,14},{15,16},{17,18},{19... | collective-permute-start | bytes 3735560 | tf_op jit(solution)/shard_map/ppermute | solution.py:706
  15.4 16.1 %collective-permute-start.3 = (f32[34,64,128]{2,1,0:T(8,128)S(1)}, f32[34,64,128]{2,1,0:T(8,128)S(1)}, u32[]{:S(2)}, u32[]{:S(2)}) collective-permute-start(f32[34,64,128]{2,1,0:T(8,128)S(1)} %get-tuple-element.75), channel_id=1, source_target_pairs={{0,1},{2,3},{4,5},{6,7},{8,9},{10,11},{12,13},{14,15},{16,17},{18,... | collective-permute-start | bytes 3342344 | tf_op jit(solution)/shard_map/ppermute | solution.py:707
  15.5 8.3 %copy-start = (f32[8,64,128]{2,1,0:T(8,128)S(1)}, f32[8,64,128]{2,1,0:T(8,128)}, u32[]{:S(2)}) copy-start(f32[8,64,128]{2,1,0:T(8,128)} %lam.5) | copy-start | bytes 786436
  15.5 8.3 %copy-start.1 = (f32[8,64,128]{2,1,0:T(8,128)S(1)}, f32[8,64,128]{2,1,0:T(8,128)}, u32[]{:S(2)}) copy-start(f32[8,64,128]{2,1,0:T(8,128)} %mu.5) | copy-start | bytes 786436
  15.5 8.3 %copy-start.2 = (f32[8,64,128]{2,1,0:T(8,128)S(1)}, f32[8,64,128]{2,1,0:T(8,128)}, u32[]{:S(2)}) copy-start(f32[8,64,128]{2,1,0:T(8,128)} %buoy.5) | copy-start | bytes 786436
  15.5 8.3 %copy-start.5 = (f32[2,3]{1,0:T(2,128)S(1)}, f32[2,3]{1,0:T(2,128)}, u32[]{:S(2)}) copy-start(f32[2,3]{1,0:T(2,128)} %src_amp.3) | copy-start | bytes 76
  15.5 8.2 %copy-start.6 = (s32[2]{0:T(128)S(1)}, s32[2]{0:T(128)}, u32[]{:S(2)}) copy-start(s32[2]{0:T(128)} %src_index.3) | copy-start | bytes 28
  15.5 25.3 %collective-permute-start = (f32[34,64,128]{2,1,0:T(8,128)S(1)}, f32[34,64,128]{2,1,0:T(8,128)S(1)}, u32[]{:S(2)}, u32[]{:S(2)}) collective-permute-start(f32[34,64,128]{2,1,0:T(8,128)S(1)} %get-tuple-element.50), channel_id=1, source_target_pairs={{1,2},{3,4},{5,6},{7,8},{9,10},{11,12},{13,14},{15,16},{17,18},{19... | collective-permute-start | bytes 3342344 | tf_op jit(solution)/shard_map/ppermute | solution.py:706
  36.9 11.1 %collective-permute-start.4 = (f32[2,5,32,128]{3,2,1,0:T(8,128)S(1)}, f32[2,5,32,128]{3,2,1,0:T(8,128)S(1)}, u32[]{:S(2)}, u32[]{:S(2)}) collective-permute-start(f32[2,5,32,128]{3,2,1,0:T(8,128)S(1)} %get-tuple-element.96), channel_id=1, source_target_pairs={{0,64},{64,0},{1,65},{65,1},{2,66},{66,2},{3,67},{67,3},{4,68},{68... | collective-permute-start | bytes 491528 | tf_op jit(solution)/shard_map/ppermute | solution.py:710
  43.3 4.7 %collective-permute-start.5 = (f32[2,3,32,128]{3,2,1,0:T(8,128)S(1)}, f32[2,3,32,128]{3,2,1,0:T(8,128)S(1)}, u32[]{:S(2)}, u32[]{:S(2)}) collective-permute-start(f32[2,3,32,128]{3,2,1,0:T(8,128)S(1)} %get-tuple-element.97), channel_id=1, source_target_pairs={{0,64},{64,0},{1,65},{65,1},{2,66},{66,2},{3,67},{67,3},{4,68},{68... | collective-permute-start | bytes 294920 | tf_op jit(solution)/shard_map/ppermute | solution.py:710
